TPU v7x, 32 devices: a whole 2x2x4 slice. The times are simulated.
32 devices in a mesh: dp: 4 (over z), latent: 8 (over y, x, core).
Axes of the slice: x: 2, y: 2, z: 4, core: 2. Of those that a mesh axis runs over, the one named last changes fastest.
Arguments:
- inputs: bfloat16 [64, 2048], P(('dp', 'latent')), may hold values from -6 to 6
- blocks: int32 [64, 4], P(('dp', 'latent')), may hold values from 0 to 127, all different within a row; in each aligned block of 16 rows (0 to 15, 16 to 31, ...) at most 2 rows name the same one
- weights: bfloat16 [8192, 2048], P('latent'), as said below
- enc_bias: float32 [8192], P('latent'), may hold values from -3 to 3
- dec_bias: float32 [2048], replicated, may hold values from -3 to 3
Outputs:
- recon: bfloat16 [64, 2048], P(('dp', 'latent'))
- grad_weights: float32 [8192, 2048], P('latent', 'dp')
- block_scores: float32 [128, 64], P('latent', 'dp')
Inputs may be any that keep to these rules, and one draw needn't show every extreme that they name: Each row names 4 different blocks. Within the rows of one data group (aligned runs of 16 rows) no block is named by more than 2 rows, and some block is named by exactly 2 rows. `weights`: rows have different lengths.
All inputs are finite; a program needn't handle non-finite values.
Results may differ from a plain program's by a relative error of at most 0.0068.
Values may be sent and summed in bfloat16 or wider, within the bound.
No kernel may reach another device: no remote copies, remote signals or barrier semaphores. Data moves between devices by JAX's collectives and lax.ppermute only.
A program may use at most 64 MiB of HBM per device.

v0:
```python
import jax
import jax.numpy as jnp
from jax import lax
from jax.sharding import PartitionSpec as P

BLK = 64
CAP = 2


def local(inputs, blocks, weights, enc_bias, dec_bias):
    lat_rows, width = weights.shape
    block_count = lat_rows // BLK
    centered = (inputs.astype(jnp.float32) - dec_bias).astype(jnp.bfloat16)
    panels, row_lists = (
        lax.all_gather(centered, "latent", axis=0, tiled=True),
        lax.all_gather(blocks, "latent", axis=0, tiled=True),
    )
    rows_group = panels.shape[0]
    squares = jnp.sum(jnp.square(weights.astype(jnp.float32)), axis=1)
    row_norms = jnp.sqrt(squares + 1e-06)
    unit_rows = (weights.astype(jnp.float32) / row_norms[:, None]).astype(jnp.bfloat16)
    unit_blocks = unit_rows.reshape(block_count, BLK, width)
    first_block = lax.axis_index("latent") * block_count
    block_ids = first_block + jnp.arange(block_count, dtype=jnp.int32)
    hit_rows = jnp.any(row_lists[None, :, :] == block_ids[:, None, None], axis=2).astype(jnp.int32)
    before = jnp.cumsum(hit_rows, axis=1) - hit_rows
    slot_ids = jnp.arange(CAP, dtype=jnp.int32)
    picked = (hit_rows[:, None, :] == 1) & (before[:, None, :] == slot_ids[None, :, None])
    row_ids = jnp.sum(
        jnp.where(picked, jnp.arange(rows_group, dtype=jnp.int32)[None, None, :], 0), axis=2
    )
    live_slots = jnp.any(picked, axis=2).astype(jnp.float32)[:, :, None]
    full_dot = jnp.dot(unit_rows, panels.T, preferred_element_type=jnp.float32)
    block_scores = jnp.mean(
        jax.nn.softplus(full_dot + enc_bias[:, None]).reshape(block_count, BLK, rows_group), axis=1
    )
    dot_blocks = full_dot.reshape(block_count, BLK, rows_group)
    base_pre = jnp.transpose(
        jnp.take_along_axis(
            dot_blocks, jnp.broadcast_to(row_ids[:, None, :], (block_count, BLK, CAP)), axis=2
        ),
        (0, 2, 1),
    )
    preact = base_pre + enc_bias.reshape(block_count, BLK)[:, None, :]
    latent_codes = (jax.nn.softplus(preact) * live_slots).astype(jnp.bfloat16)
    slot_rows = panels[row_ids]
    contrib = jnp.einsum(
        "jcm,jmd->jcd", latent_codes, unit_blocks, preferred_element_type=jnp.float32
    )
    partial_value = (
        jnp.zeros((rows_group, width), jnp.float32)
        .at[row_ids.reshape(-1)]
        .add(contrib.reshape(-1, width))
    )
    own_sums = lax.psum_scatter(partial_value, "latent", scatter_dimension=0, tiled=True)
    recon_full = dec_bias + own_sums
    recon_rows = recon_full.astype(jnp.bfloat16)
    errors = (recon_full - inputs.astype(jnp.float32)).astype(jnp.bfloat16)
    all_errors = lax.all_gather(errors, "latent", axis=0, tiled=True)
    slot_errors = all_errors[row_ids]
    code_grad = jnp.einsum(
        "jcd,jmd->jcm", slot_errors, unit_blocks, preferred_element_type=jnp.float32
    )
    pre_grad = (code_grad * jax.nn.sigmoid(preact) * live_slots).astype(jnp.bfloat16)
    along_unit = jnp.sum(
        latent_codes.astype(jnp.float32) * code_grad + pre_grad.astype(jnp.float32) * base_pre,
        axis=1,
    )
    norm_blocks = row_norms.reshape(block_count, BLK)
    groups = lax.axis_size("dp")
    col_count = width // groups
    moved_rows, moved_errors = (
        lax.all_to_all(slot_rows[None], "dp", split_axis=3, concat_axis=0, tiled=True),
        lax.all_to_all(slot_errors[None], "dp", split_axis=3, concat_axis=0, tiled=True),
    )
    got_codes, got_grad = (
        lax.all_gather(latent_codes[None], "dp", axis=0, tiled=True),
        lax.all_gather(pre_grad[None], "dp", axis=0, tiled=True),
    )
    got_along = lax.all_gather(along_unit[None], "dp", axis=0, tiled=True)
    col_start = lax.axis_index("dp") * col_count
    unit_cols = (
        lax.dynamic_slice_in_dim(unit_rows, col_start, col_count, 1)
        .astype(jnp.float32)
        .reshape(block_count, BLK, col_count)
    )
    got_left = jnp.concatenate([got_codes, got_grad], axis=2)
    got_right = jnp.concatenate([moved_errors, moved_rows], axis=2)
    outer_terms = jnp.einsum(
        "gjcm,gjcd->gjmd", got_left, got_right, preferred_element_type=jnp.float32
    )
    group_parts = (outer_terms - unit_cols[None] * got_along[..., None]) / norm_blocks[
        None, :, :, None
    ]
    group_parts = lax.optimization_barrier(group_parts.astype(jnp.bfloat16)).astype(jnp.float32)
    grad_weights = jnp.sum(group_parts, axis=0).reshape(lat_rows, col_count)
    return (recon_rows, grad_weights, block_scores)


def solution(mesh):
    in_specs = (
        P(("dp", "latent"), None),
        P(("dp", "latent"), None),
        P("latent", None),
        P("latent"),
        P(),
    )
    out_specs = (P(("dp", "latent"), None), P("latent", "dp"), P("latent", "dp"))
    return jax.shard_map(local, mesh=mesh, in_specs=in_specs, out_specs=out_specs, check_vma=False)
```

profile of v0, /device:TPU:0, one launch (start us, length us, event | category | flops | bytes accessed | tf_op | source)
XLA Modules:
  0.0 189.1 jit_solution(11037067307001685502)
XLA Ops:
  7.2 10.5 %all-gather.3 = s32[8,2,4]{2,1,0:T(2,128)S(1)} all-gather(s32[1,2,4]{2,1,0:T(2,128)} %bitcast.63), channel_id=1, replica_groups=mesh['dp'=4,'latent'=8] {'latent'}, dimensions={0}, use_global_device_ids=true | all-gather | bytes 288 | tf_op jit(solution)/shard_map/all_gather | solution.py:16
  18.3 0.7 fusion.17
  19.1 9.1 %all-gather.4 = bf16[8,2,2048]{2,1,0:T(2,128)(2,1)S(1)} all-gather(bf16[1,2,2048]{2,1,0:T(2,128)(2,1)S(1)} %fusion.17), channel_id=1, replica_groups=mesh['dp'=4,'latent'=8] {'latent'}, dimensions={0}, use_global_device_ids=true | all-gather | bytes 73728 | tf_op jit(solution)/shard_map/all_gather | solution.py:15
  29.0 0.8 copy.75
  29.7 1.7 reshape.170
  31.5 4.9 %all-to-all-start.1 = ((bf16[4,2,8192]{2,1,0:T(2,128)(2,1)}), bf16[4,2,8192]{2,1,0:T(2,128)(2,1)}, u32[]{:S(2)}, u32[]{:S(2)}) async-start(bf16[4,2,8192]{2,1,0:T(2,128)(2,1)} %reshape.170), calls=%async_computation.1 | async-start | bytes 262144 | tf_op jit(solution)/shard_map/all_to_all | solution.py:73
  36.6 0.7 copy.65
  38.0 3.1 %fusion = f32[1024]{0:T(1024)S(1)} fusion(bf16[1024,2048]{1,0:T(8,128)(2,1)} %param.7), kind=kLoop, calls=%fused_computation.6 | loop fusion | flops 6290432 | bytes 4198400 | tf_op jit(solution)/shard_map/reduce_sum | solution.py:19
  41.8 0.7 copy.70
  43.6 3.9 %fusion.1 = bf16[1024,2048]{1,0:T(8,128)(2,1)S(1)} fusion(bf16[1024,2048]{1,0:T(8,128)(2,1)} %param.7, f32[1024]{0:T(1024)S(1)} %add_sqrt_fusion), kind=kLoop, calls=%fused_computation.7 | loop fusion | flops 6291456 | bytes 8392704 | tf_op jit(solution)/shard_map/convert_element_type | solution.py:21
  47.5 2.0 %compare_select_fusion = (f32[1024,16]{0,1:T(8,128)}, f32[1024,16]{0,1:T(8,128)S(1)}) fusion(f32[1024]{0:T(1024)S(1)} %copy-done.2, bf16[1024,2048]{1,0:T(8,128)(2,1)S(1)} %fusion.1, bf16[16,2048]{1,0:T(8,128)(2,1)S(1)} %reshape.164), kind=kOutput, calls=%fused_computation.13 | convolution fusion | flops 67223552 | bytes 4395008 | tf_op jit(solution)/shard_map/dot_general | solution.py:33
  49.6 16.8 %gather_fusion.2 = f32[2048]{0:T(1024)S(1)} fusion(f32[16,64,16]{1,0,2:T(8,128)S(1)} %reshape.118, s32[2048]{0:T(1024)S(1)} %reshape.140), kind=kCustom, calls=%fused_computation.2 | custom fusion | bytes 40960 | tf_op jit(solution)/shard_map/jit(take_along_axis)/gather | solution.py:39
  67.4 2.8 %fusion.21 = f32[16,2,2048]{2,1,0:T(2,128)S(1)} fusion(bf16[16,2,64]{2,1,0:T(2,128)(2,1)S(1)} %get-tuple-element.14, bf16[16,64,2048]{2,1,0:T(8,128)(2,1)} %bitcast.49), kind=kOutput, calls=%fused_computation.53 | convolution fusion | flops 8388608 | bytes 4460544 | tf_op jit(solution)/shard_map/jcm,jmd->jcd/dot_general | solution.py:47
  70.4 1.7 scatter_custom_fusion
  72.4 1.3 constant_dynamic-slice_fusion
  73.8 0.7 copy.78
  76.0 13.7 %all-gather = bf16[64,2,64]{2,1,0:T(2,128)(2,1)S(1)} all-gather(bf16[16,2,64]{2,1,0:T(2,128)(2,1)S(1)} %get-tuple-element.14), channel_id=2, replica_groups=mesh['dp'=4,'latent'=8] {'dp'}, dimensions={0}, use_global_device_ids=true | all-gather | bytes 20480 | tf_op jit(solution)/shard_map/all_gather | solution.py:77
  89.7 36.1 %all-reduce.3.cloned.1.call-done = f32[16,2048]{1,0:T(8,128)} async-done(((f32[16,2048]{1,0:T(8,128)}), f32[16,2048]{1,0:T(8,128)}) %all-reduce.3.cloned.1.call-update) | async-done | bytes 131088
  125.7 1.5 fusion.18
  127.2 8.7 %all-gather.5 = bf16[8,2,2048]{2,1,0:T(2,128)(2,1)S(1)} all-gather(bf16[1,2,2048]{2,1,0:T(2,128)(2,1)S(1)} %get-tuple-element.16), channel_id=1, replica_groups=mesh['dp'=4,'latent'=8] {'latent'}, dimensions={0}, use_global_device_ids=true | all-gather | bytes 73728 | tf_op jit(solution)/shard_map/all_gather | solution.py:59
  136.8 0.8 copy.72
  137.6 1.7 reshape.172
  139.3 4.6 %all-to-all-start = ((bf16[4,2,8192]{2,1,0:T(2,128)(2,1)}), bf16[4,2,8192]{2,1,0:T(2,128)(2,1)S(1)}, u32[]{:S(2)}, u32[]{:S(2)}) async-start(bf16[4,2,8192]{2,1,0:T(2,128)(2,1)} %reshape.172), calls=%async_computation | async-start | bytes 262144 | tf_op jit(solution)/shard_map/all_to_all | solution.py:74
  143.9 3.4 %add_reduce_fusion = (f32[16,64]{1,0:T(8,128)S(1)}, bf16[16,2,64]{2,1,0:T(2,128)(2,1)S(1)}) fusion(f32[16,2,64]{2,1,0:T(2,128)S(1)} %get-tuple-element.15, bf16[16,2,64]{2,1,0:T(2,128)(2,1)S(1)} %get-tuple-element.14, f32[16,2]{1,0:T(8,128)S(1)} %copy-done.12, f32[16,64]{1,0:T(8,128)S(1)} %copy-done.11, bf16[16,2,2048]{2,1,0:T(2,128)(2,1)S(1)} %reshape.125, ...), kind=kOutput, calls=%fused_computation.31 | convolution fusion | flops 8414208 | bytes 4350080 | tf_op jit(solution)/shard_map/jcd,jmd->jcm/dot_general | solution.py:61
  147.3 13.7 %all-gather.2 = f32[64,64]{1,0:T(8,128)S(1)} all-gather(f32[16,64]{1,0:T(8,128)S(1)} %get-tuple-element.12), channel_id=4, replica_groups=mesh['dp'=4,'latent'=8] {'dp'}, dimensions={0}, use_global_device_ids=true | all-gather | bytes 20480 | tf_op jit(solution)/shard_map/all_gather | solution.py:80
  161.0 13.1 %all-gather.1 = bf16[64,2,64]{2,1,0:T(2,128)(2,1)S(1)} all-gather(bf16[16,2,64]{2,1,0:T(2,128)(2,1)S(1)} %get-tuple-element.13), channel_id=3, replica_groups=mesh['dp'=4,'latent'=8] {'dp'}, dimensions={0}, use_global_device_ids=true | all-gather | bytes 20480 | tf_op jit(solution)/shard_map/all_gather | solution.py:78
  174.1 1.6 reshape.171
  175.8 0.7 copy.77
  176.5 0.7 reshape.173
  177.2 0.7 copy.74
  178.0 2.1 %divide_convert_fusion = bf16[4,16,64,512]{3,2,1,0:T(8,128)(2,1)S(1)} fusion(f32[16,64]{1,0:T(8,128)S(1)} %sqrt.15, f32[4,16,64]{2,1,0:T(8,128)S(1)} %bitcast.60, f32[16,64,512]{2,1,0:T(8,128)S(1)} %convert.1, bf16[4,16,2,512]{3,2,1,0:T(2,128)(2,1)S(1)} %bitcast.57, bf16[4,16,2,512]{3,2,1,0:T(2,128)(2,1)S(1)} %bitcast.58, ...), kind=kOutput, calls=%fused_computation.9 | convolution fusion | flops 25755648 | bytes 6606848 | tf_op jit(solution)/shard_map/gjcm,gjcd->gjmd/dot_general | solution.py:89
  180.1 2.1 %convert_reduce_fusion = f32[16,64,512]{2,1,0:T(8,128)} fusion(bf16[4,16,64,512]{3,2,1,0:T(8,128)(2,1)S(1)} %divide_convert_fusion), kind=kLoop, calls=%fused_computation.8 | loop fusion | flops 3670016 | bytes 6291456 | tf_op jit(solution)/shard_map/reduce_sum | solution.py:96
  (78 shorter events, 7.4 us)
Async XLA Ops:
  18.3 10.5 %copy-start.3 = (s32[1024]{0:T(1024)}, s32[1024]{0:T(1024)S(1)}, u32[]{:S(2)}) copy-start(s32[1024]{0:T(1024)S(1)} %pad_clamp_fusion) | copy-start | bytes 12292
  28.2 12.9 %copy-start.2 = (f32[1024]{0:T(1024)S(1)}, f32[1024]{0:T(1024)}, u32[]{:S(2)}) copy-start(f32[1024]{0:T(1024)} %param.8) | copy-start | bytes 12292
  31.5 107.9 %all-to-all-start.1 = ((bf16[4,2,8192]{2,1,0:T(2,128)(2,1)}), bf16[4,2,8192]{2,1,0:T(2,128)(2,1)}, u32[]{:S(2)}, u32[]{:S(2)}) async-start(bf16[4,2,8192]{2,1,0:T(2,128)(2,1)} %reshape.170), calls=%async_computation.1 | async-start | bytes 262144 | tf_op jit(solution)/shard_map/all_to_all | solution.py:73
  36.3 89.4 %all-reduce.3.cloned.1.call-start = ((), (), s32[]{:S(2)}) async-start(), calls=%async_computation.2 | async-start | bytes 262144
  36.6 6.5 %copy-start.5 = (s32[16,2]{1,0:T(8,128)}, s32[16,2]{1,0:T(8,128)S(1)}, u32[]{:S(2)}) copy-start(s32[16,2]{1,0:T(8,128)S(1)} %copy.64) | copy-start | bytes 388
  41.1 6.4 %copy-start.7 = (f32[1024]{0:T(1024)}, f32[1024]{0:T(1024)S(1)}, u32[]{:S(2)}) copy-start(f32[1024]{0:T(1024)S(1)} %add_sqrt_fusion) | copy-start | bytes 12292
  47.5 2.0 %copy-start = (bf16[1024,2048]{1,0:T(8,128)(2,1)}, bf16[1024,2048]{1,0:T(8,128)(2,1)S(1)}, u32[]{:S(2)}) copy-start(bf16[1024,2048]{1,0:T(8,128)(2,1)S(1)} %fusion.1) | copy-start | bytes 12582916
  49.6 17.6 %copy-start.6 = (s32[16,2]{1,0:T(8,128)S(1)}, s32[16,2]{1,0:T(8,128)}, u32[]{:S(2)}) copy-start(s32[16,2]{1,0:T(8,128)} %copy-done.5) | copy-start | bytes 388
  49.6 17.6 %copy-start.11 = (f32[16,64]{1,0:T(8,128)S(1)}, f32[16,64]{1,0:T(8,128)}, u32[]{:S(2)}) copy-start(f32[16,64]{1,0:T(8,128)} %add.114) | copy-start | bytes 12292
  49.6 17.6 %copy-start.12 = (f32[16,2]{1,0:T(8,128)S(1)}, f32[16,2]{1,0:T(8,128)}, u32[]{:S(2)}) copy-start(f32[16,2]{1,0:T(8,128)} %copy.70) | copy-start | bytes 388
  49.6 17.6 %copy-start.13 = (s32[16,2]{1,0:T(8,128)S(1)}, s32[16,2]{1,0:T(8,128)}, u32[]{:S(2)}) copy-start(s32[16,2]{1,0:T(8,128)} %copy.66) | copy-start | bytes 388
  49.6 17.6 %copy-start.14 = (pred[16,2]{1,0:T(8,128)(4,1)S(1)}, pred[16,2]{1,0:T(8,128)(4,1)}, u32[]{:S(2)}) copy-start(pred[16,2]{1,0:T(8,128)(4,1)} %copy.65) | copy-start | bytes 100
  66.5 5.7 %copy-start.1 = (f32[1024,16]{0,1:T(8,128)S(1)}, f32[1024,16]{0,1:T(8,128)}, u32[]{:S(2)}) copy-start(f32[1024,16]{0,1:T(8,128)} %get-tuple-element.20) | copy-start | bytes 196612
  66.9 6.8 %copy-start.8 = (f32[1024]{0:T(1024)S(1)}, f32[1024]{0:T(1024)}, u32[]{:S(2)}) copy-start(f32[1024]{0:T(1024)} %copy-done.7) | copy-start | bytes 12292
  70.2 4.5 %copy-start.15 = (u32[32]{0:T(128)S(1)}, u32[32]{0:T(128)}, u32[]{:S(2)}) copy-start(u32[32]{0:T(128)} %constant.78) | copy-start | bytes 388
  70.2 55.5 %copy-start.9 = (bf16[2,2048]{1,0:T(2,128)(2,1)S(1)}, bf16[2,2048]{1,0:T(2,128)(2,1)}, u32[]{:S(2)}) copy-start(bf16[2,2048]{1,0:T(2,128)(2,1)} %param.5) | copy-start | bytes 24580
  70.2 55.5 %copy-start.10 = (f32[2048]{0:T(1024)S(1)}, f32[2048]{0:T(1024)}, u32[]{:S(2)}) copy-start(f32[2048]{0:T(1024)} %param.9) | copy-start | bytes 24580
  70.2 65.7 %copy-start.4 = (s32[1024]{0:T(1024)S(1)}, s32[1024]{0:T(1024)}, u32[]{:S(2)}) copy-start(s32[1024]{0:T(1024)} %copy-done.3) | copy-start | bytes 12292
  139.3 37.2 %all-to-all-start = ((bf16[4,2,8192]{2,1,0:T(2,128)(2,1)}), bf16[4,2,8192]{2,1,0:T(2,128)(2,1)S(1)}, u32[]{:S(2)}, u32[]{:S(2)}) async-start(bf16[4,2,8192]{2,1,0:T(2,128)(2,1)} %reshape.172), calls=%async_computation | async-start | bytes 262144 | tf_op jit(solution)/shard_map/all_to_all | solution.py:74
Sparse Core Ops, SparseCore 0:
  72.3 53.3 all-reduce.2
where the time goes:
time: 190 us; the launch traced here: 189 us
  blocking collectives  68.8 us (36%)
  waiting for transfers between devices  36.1 us (19%)
  local copies, waits for them, and re-layouts  34.6 us (18%)
  between operations  15.1 us (8%)
  other arithmetic  14.7 us (8%)
  matrix products  10.3 us (5%)
  starting transfers between devices  9.47 us (5%)
    unnamed x2, waiting for transfers between devices  36.1 us
    gather x5, local copies, waits for them, and re-layouts, local(): jnp.take_along_axis(dot_blocks, jnp.broadcast_to(row_ids[:, None, :], (bl...  18 us
    all_gather x1, blocking collectives, local(): lax.all_gather(latent_codes[None], 'dp', axis=0, tiled=True)  13.7 us
    all_gather x1, blocking collectives, local(): got_along = lax.all_gather(along_unit[None], 'dp', axis=0, tiled=True)  13.7 us
    all_gather x1, blocking collectives, local(): lax.all_gather(pre_grad[None], 'dp', axis=0, tiled=True)  13.1 us
    all_gather x1, blocking collectives, local(): lax.all_gather(blocks, 'latent', axis=0, tiled=True)  10.5 us
    all_gather x1, blocking collectives, local(): lax.all_gather(centered, 'latent', axis=0, tiled=True)  9.08 us
    all_gather x1, blocking collectives, local(): all_errors = lax.all_gather(errors, 'latent', axis=0, tiled=True)  8.72 us
  transfers between devices with their start and end apart: 3, of which 1 were waited for; matrix products, arithmetic and copies ran while one was open for 26% of the time, Pallas kernels for 0%

commit v1 on v0

v1 whole, which is shorter than its diff:
```python
import jax
import jax.numpy as jnp
from jax import lax
from jax.sharding import PartitionSpec as P

BLK = 64
CAP = 2
RADIX = 32
LANES = 128
DIRECT = 4


def swap(x, axis, mask):
    size = lax.axis_size(axis)
    return lax.ppermute(x, axis, [(i, i ^ mask) for i in range(size)])


def local(inputs, blocks, weights, enc_bias, dec_bias):
    rows_dev, width = inputs.shape
    lat_rows = weights.shape[0]
    block_count = lat_rows // BLK
    chips = lax.axis_size("latent") // 2
    groups = lax.axis_size("dp")
    half = chips * rows_dev
    rows_group = 2 * half
    col_count = width // groups
    me = lax.axis_index("latent")
    my_group = lax.axis_index("dp")

    lists = jnp.concatenate([blocks // RADIX, blocks % RADIX], axis=1).astype(jnp.bfloat16)
    lists = jnp.pad(lists, ((0, 0), (0, LANES - lists.shape[1])))
    payload = jnp.concatenate([inputs, lists], axis=1)
    both = jnp.concatenate([payload, swap(payload, "latent", 1)], axis=0)
    got = [both] + [swap(both, "latent", 2 * k) for k in range(1, chips)]
    rows = jnp.concatenate([g[:rows_dev] for g in got] + [g[rows_dev:] for g in got], axis=0)

    wide = weights.astype(jnp.float32)
    row_norms = jnp.sqrt(jnp.sum(jnp.square(wide), axis=1) + 1e-06)
    unit_rows = (wide / row_norms[:, None]).astype(jnp.bfloat16)

    group_inputs = rows[:, :width].astype(jnp.float32)
    centered = (group_inputs - dec_bias).astype(jnp.bfloat16)
    top = blocks.shape[1]
    coded = rows[:, width : width + 2 * top].astype(jnp.float32)
    named = (coded[:, :top] * RADIX + coded[:, top:]).astype(jnp.int32)
    block_of = me * block_count + jnp.arange(lat_rows, dtype=jnp.int32) // BLK
    hit = named[:, 0:1] == block_of[None, :]
    for k in range(1, top):
        hit = hit | (named[:, k : k + 1] == block_of[None, :])
    hit = hit.astype(jnp.float32)

    base_pre = lax.dot_general(
        centered, unit_rows, (((1,), (1,)), ((), ())), preferred_element_type=jnp.float32
    )
    preact = base_pre + enc_bias[None, :]
    act = jax.nn.softplus(preact)
    codes = (act * hit).astype(jnp.bfloat16)
    contrib = jnp.dot(codes, unit_rows, preferred_element_type=jnp.float32)
    sums = contrib[:half] + swap(contrib[half:], "latent", 1)
    if chips <= DIRECT:
        parts = [sums] + [swap(sums, "latent", 2 * j) for j in range(1, chips)]
        total = []
        for k in range(chips):
            value = dec_bias
            for j in range(chips):
                at = (k ^ j) * rows_dev
                value = value + parts[j][at : at + rows_dev]
            total.append(value)
        recon_full = jnp.concatenate(total, axis=0)
        errors = (recon_full - group_inputs[:half]).astype(jnp.bfloat16)
    else:
        recon_full = dec_bias + sums[:rows_dev]
        for j in range(1, chips):
            recon_full = recon_full + swap(sums[j * rows_dev : (j + 1) * rows_dev], "latent", 2 * j)
        errors = (recon_full - group_inputs[:rows_dev]).astype(jnp.bfloat16)
        errors = [errors] + [swap(errors, "latent", 2 * j) for j in range(1, chips)]
        errors = jnp.concatenate(errors, axis=0)
    recon_rows = recon_full[:rows_dev].astype(jnp.bfloat16)
    errors = jnp.concatenate([errors, swap(errors, "latent", 1)], axis=0)

    means = jnp.mean(act.reshape(rows_group, block_count, BLK), axis=2)
    place = jnp.arange(rows_group, dtype=jnp.int32)
    owner = (place // rows_dev) ^ me
    relative = (owner % 2) * half + (owner // 2) * rows_dev + place % rows_dev
    order = (relative[None, :] == place[:, None]).astype(jnp.float32)
    block_scores = lax.dot_general(
        means, order, (((0,), (0,)), ((), ())), precision=lax.Precision.HIGHEST
    )

    code_grad = lax.dot_general(
        errors, unit_rows, (((1,), (1,)), ((), ())), preferred_element_type=jnp.float32
    )
    pre_grad = (code_grad * jax.nn.sigmoid(preact) * hit).astype(jnp.bfloat16)
    along = jnp.sum(
        codes.astype(jnp.float32) * code_grad + pre_grad.astype(jnp.float32) * base_pre, axis=0
    )
    along_high = lax.reduce_precision(along, 8, 7)
    along_low = along - along_high

    earlier = (place[:, None] > place[None, :]).astype(jnp.float32)
    before = jnp.dot(earlier, hit)
    compact = []
    for s in range(CAP):
        mine = hit * (before == s)
        compact.append(jnp.sum(mine * codes.astype(jnp.float32), axis=0))
        compact.append(jnp.sum(mine * pre_grad.astype(jnp.float32), axis=0))
        compact.append(jnp.sum(mine * (place[:, None] + 1).astype(jnp.float32), axis=0))
    compact = jnp.stack(compact + [along_high, along_low]).astype(jnp.bfloat16)
    right = jnp.concatenate([errors, centered], axis=0)
    flat = compact.reshape(-1, col_count)
    sent = []
    for k in range(groups):
        cols = lax.dynamic_slice_in_dim(right, (my_group ^ k) * col_count, col_count, 1)
        packet = jnp.concatenate([cols, flat], axis=0)
        sent.append(swap(packet, "dp", k) if k else packet)

    lefts, rights, alongs = [], [], []
    for packet in sent:
        rights.append(packet[: 2 * rows_group])
        terms = packet[2 * rows_group :].reshape(-1, lat_rows).astype(jnp.float32)
        code_part, grad_part = 0.0, 0.0
        for s in range(CAP):
            at = (terms[3 * s + 2][None, :] == (place[:, None] + 1).astype(jnp.float32)).astype(
                jnp.float32
            )
            code_part = code_part + at * terms[3 * s][None, :]
            grad_part = grad_part + at * terms[3 * s + 1][None, :]
        lefts += [code_part, grad_part]
        alongs.append(terms[3 * CAP] + terms[3 * CAP + 1])
    outer = 0.0
    for g in range(0, groups, DIRECT):
        left = jnp.concatenate(lefts[2 * g : 2 * (g + DIRECT)], axis=0).astype(jnp.bfloat16)
        right = jnp.concatenate(rights[g : g + DIRECT], axis=0)
        outer = outer + lax.dot_general(
            left, right, (((0,), (0,)), ((), ())), preferred_element_type=jnp.float32
        )
    along_all = sum(alongs)
    unit_cols = lax.dynamic_slice_in_dim(unit_rows, my_group * col_count, col_count, 1)
    grad_weights = (outer - unit_cols.astype(jnp.float32) * along_all[:, None]) / row_norms[:, None]
    return (recon_rows, grad_weights, block_scores)


def solution(mesh):
    in_specs = (
        P(("dp", "latent"), None),
        P(("dp", "latent"), None),
        P("latent", None),
        P("latent"),
        P(),
    )
    out_specs = (P(("dp", "latent"), None), P("latent", "dp"), P("latent", "dp"))
    return jax.shard_map(local, mesh=mesh, in_specs=in_specs, out_specs=out_specs, check_vma=False)
```

time: 190 us -> 48.9 us (0.26)
  blocking collectives: 68.8 us -> 0 us
  local copies, waits for them, and re-layouts: 34.6 us -> 0.9 us
  waiting for transfers between devices: 36.1 us -> 11.8 us
  between operations: 15.1 us -> 1.1 us
  other arithmetic: 14.7 us -> 10.4 us
  starting transfers between devices: 9.47 us -> 12.8 us
    all_gather x6 -> x0, blocking collectives: 68.8 us -> none  [the longest x1 13.7 us: local(): lax.all_gather(latent_codes[None], 'dp', axis=0, tiled=True)]
    unnamed x2 -> x0, waiting for transfers between devices: 36.1 us -> none
    gather x8 -> x0, local copies, waits for them, and re-layouts: 19.4 us -> none  [the longest x5 18 us: local(): jnp.take_along_axis(dot_blocks, jnp.broadcast_to(row_ids[:, None, :], (bl...]
    ppermute x0 -> x12, starting transfers between devices: none -> 12.8 us  [swap(): return lax.ppermute(x, axis, [(i, i ^ mask) for i in range(size)])]
    ppermute x0 -> x12, waiting for transfers between devices: none -> 11.8 us  [swap(): return lax.ppermute(x, axis, [(i, i ^ mask) for i in range(size)])]
    all_to_all x2 -> x0, starting transfers between devices: 9.47 us -> none  [the longest x1 4.87 us: local(): lax.all_to_all(slot_rows[None], 'dp', split_axis=3, concat_axis=0, tiled=...]
    unnamed x41 -> x31, local copies, waits for them, and re-layouts: 7.23 us -> 0.28 us
    reduce_sum x4 -> x3, other arithmetic: 5.41 us -> 3.5 us  [the longest x1 3.22 us: local(): row_norms = jnp.sqrt(jnp.sum(jnp.square(wide), axis=1) + 1e-06)]
  transfers between devices with their start and end apart: 3 -> 12, of which waited for: 1 -> 10; matrix products, arithmetic and copies ran while one was open for 26% -> 17% of each run, Pallas kernels for 0% -> 0%
where the time goes in v1:
time: 48.9 us; the launch traced here: 48.7 us
  starting transfers between devices  12.8 us (26%)
  waiting for transfers between devices  11.8 us (24%)
  matrix products  11.7 us (24%)
  other arithmetic  10.4 us (21%)
  between operations  1.1 us (2%)
  local copies, waits for them, and re-layouts  0.9 us (2%)
    ppermute x12, starting transfers between devices, swap(): return lax.ppermute(x, axis, [(i, i ^ mask) for i in range(size)])  12.8 us
    ppermute x12, waiting for transfers between devices, swap(): return lax.ppermute(x, axis, [(i, i ^ mask) for i in range(size)])  11.8 us
    convert_element_type x1, other arithmetic, local(): unit_rows = (wide / row_norms[:, None]).astype(jnp.bfloat16)  3.69 us
    dot_general x1, matrix products, local(): lax.dot_general(centered, unit_rows, (((1,), (1,)), ((), ())), preferred_...  3.59 us
    dot_general x1, matrix products, local(): lax.dot_general(errors, unit_rows, (((1,), (1,)), ((), ())), preferred_el...  3.38 us
    reduce_sum x1, other arithmetic, local(): row_norms = jnp.sqrt(jnp.sum(jnp.square(wide), axis=1) + 1e-06)  3.22 us
    dot_general x1, matrix products, local(): lax.dot_general(left, right, (((0,), (0,)), ((), ())), preferred_element_...  3.05 us
  transfers between devices with their start and end apart: 12, of which 10 were waited for; matrix products, arithmetic and copies ran while one was open for 17% of the time, Pallas kernels for 0%

profile of v1, /device:TPU:0, one launch (start us, length us, event | category | flops | bytes accessed | tf_op | source)
XLA Modules:
  0.0 48.7 jit_solution(15922316655490405729)
XLA Ops:
  0.6 0.7 %fusion.65 = (bf16[2,4]{1,0:T(2,128)(2,1)S(1)}, bf16[2,4]{1,0:T(2,128)(2,1)S(1)}) fusion(s32[2,4]{1,0:T(2,128)} %param.6), kind=kLoop, calls=%fused_computation.184 | loop fusion | flops 168 | bytes 64 | tf_op jit(solution)/shard_map/convert.8
  1.4 0.7 %pad_maximum_fusion.5 = bf16[2,2176]{1,0:T(2,128)(2,1)S(1)} fusion(bf16[2,128]{1,0:T(2,128)(2,1)S(1)} %fusion.68, bf16[2,2048]{1,0:T(2,128)(2,1)} %param.5), kind=kLoop, calls=%fused_computation.109 | loop fusion | flops 17408 | bytes 17408 | tf_op jit(solution)/shard_map/concatenate | solution.py:32
  2.1 0.5 %collective-permute-start = (bf16[2,2176]{1,0:T(2,128)(2,1)S(1)}, bf16[2,2176]{1,0:T(2,128)(2,1)S(1)}, u32[]{:S(2)}, u32[]{:S(2)}) collective-permute-start(bf16[2,2176]{1,0:T(2,128)(2,1)S(1)} %pad_maximum_fusion.5), channel_id=1, source_target_pairs={{0,1},{1,0},{2,3},{3,2},{4,5},{5,4},{6,7},{7,6},{8,9},{9,8},{10,11... | collective-permute-start | bytes 26120 | tf_op jit(solution)/shard_map/ppermute | solution.py:15
  2.6 3.2 %fusion = f32[1024]{0:T(1024)S(1)} fusion(bf16[1024,2048]{1,0:T(8,128)(2,1)} %param.7), kind=kLoop, calls=%fused_computation.2 | loop fusion | flops 6290432 | bytes 4198400 | tf_op jit(solution)/shard_map/reduce_sum | solution.py:38
  5.9 0.2 copy-done.1
  6.1 3.7 %fusion.1 = bf16[1024,2048]{1,0:T(8,128)(2,1)} fusion(bf16[1024,2048]{1,0:T(8,128)(2,1)S(1)} %copy-done.1, f32[1024]{0:T(1024)S(1)} %add_sqrt_fusion), kind=kLoop, calls=%fused_computation.3 | loop fusion | flops 6291456 | bytes 8392704 | tf_op jit(solution)/shard_map/convert_element_type | solution.py:39
  9.8 3.5 %collective-permute-start.3 = (bf16[4,2176]{1,0:T(4,128)(2,1)S(1)}, bf16[4,2176]{1,0:T(4,128)(2,1)S(1)}, u32[]{:S(2)}, u32[]{:S(2)}) collective-permute-start(bf16[4,2176]{1,0:T(4,128)(2,1)S(1)} %pad_maximum_fusion.4), channel_id=1, source_target_pairs={{0,6},{1,7},{2,4},{3,5},{4,2},{5,3},{6,0},{7,1},{8,14},{9,15},{10,... | collective-permute-start | bytes 52232 | tf_op jit(solution)/shard_map/ppermute | solution.py:15
  13.4 0.5 %collective-permute-start.2 = (bf16[4,2176]{1,0:T(4,128)(2,1)S(1)}, bf16[4,2176]{1,0:T(4,128)(2,1)S(1)}, u32[]{:S(2)}, u32[]{:S(2)}) collective-permute-start(bf16[4,2176]{1,0:T(4,128)(2,1)S(1)} %pad_maximum_fusion.4), channel_id=1, source_target_pairs={{0,4},{1,5},{2,6},{3,7},{4,0},{5,1},{6,2},{7,3},{8,12},{9,13},{10,... | collective-permute-start | bytes 52232 | tf_op jit(solution)/shard_map/ppermute | solution.py:15
  13.9 0.2 collective-permute-start.1
  14.0 1.1 %collective-permute-done.3 = bf16[4,2176]{1,0:T(4,128)(2,1)S(1)} collective-permute-done((bf16[4,2176]{1,0:T(4,128)(2,1)S(1)}, bf16[4,2176]{1,0:T(4,128)(2,1)S(1)}, u32[]{:S(2)}, u32[]{:S(2)}) %collective-permute-start.3) | collective-permute-done | bytes 17440 | tf_op jit(solution)/shard_map/ppermute | solution.py:15
  15.1 2.0 %collective-permute-done.2 = bf16[4,2176]{1,0:T(4,128)(2,1)S(1)} collective-permute-done((bf16[4,2176]{1,0:T(4,128)(2,1)S(1)}, bf16[4,2176]{1,0:T(4,128)(2,1)S(1)}, u32[]{:S(2)}, u32[]{:S(2)}) %collective-permute-start.2) | collective-permute-done | bytes 17440 | tf_op jit(solution)/shard_map/ppermute | solution.py:15
  17.1 0.5 %collective-permute-done.1 = bf16[4,2176]{1,0:T(4,128)(2,1)S(1)} collective-permute-done((bf16[4,2176]{1,0:T(4,128)(2,1)S(1)}, bf16[4,2176]{1,0:T(4,128)(2,1)S(1)}, u32[]{:S(2)}, u32[]{:S(2)}) %collective-permute-start.1) | collective-permute-done | bytes 17440 | tf_op jit(solution)/shard_map/ppermute | solution.py:15
  17.6 0.1 concatenate.42
  17.9 0.2 slice_reduce_fusion.3
  18.1 3.6 %select_convert_fusion.1 = (bf16[16,1024]{1,0:T(8,128)(2,1)S(1)}, f32[16,1024]{1,0:T(8,128)S(1)}, f32[16,1024]{1,0:T(8,128)S(1)}) fusion(s32[16]{0:T(128)S(1)} %get-tuple-element.13, s32[16]{0:T(128)S(1)} %get-tuple-element.14, s32[16]{0:T(128)S(1)} %get-tuple-element.15, s32[1024]{0:T(1024)S(1)} %fusion.52, s32[16]{0:T(128)S(1)} %get-tuple-element.12, ...), kind=kOutput, calls=%fused_computation.77 | convolution fusion | flops 67354624 | bytes 4432128 | tf_op jit(solution)/shard_map/dot_general | solution.py:52
  21.7 0.7 %fusion.79 = f32[16,2048]{1,0:T(8,128)S(1)} fusion(bf16[16,1024]{1,0:T(8,128)(2,1)S(1)} %get-tuple-element.18, bf16[1024,2048]{1,0:T(8,128)(2,1)S(1)} %copy-done), kind=kOutput, calls=%fused_computation.202 | convolution fusion | flops 67108864 | bytes 4358144 | tf_op jit(solution)/shard_map/dot_general | solution.py:58
  22.5 1.2 %collective-permute-done.4 = f32[8,2048]{1,0:T(8,128)S(1)} collective-permute-done((f32[8,2048]{1,0:T(8,128)S(1)}, f32[8,2048]{1,0:T(8,128)S(1)}, u32[]{:S(2)}, u32[]{:S(2)}) %collective-permute-start.4) | collective-permute-done | bytes 65568 | tf_op jit(solution)/shard_map/ppermute | solution.py:15
  23.7 1.6 %collective-permute-start.7 = (f32[8,2048]{1,0:T(8,128)S(1)}, f32[8,2048]{1,0:T(8,128)S(1)}, u32[]{:S(2)}, u32[]{:S(2)}) collective-permute-start(f32[8,2048]{1,0:T(8,128)S(1)} %slice_add_fusion), channel_id=1, source_target_pairs={{0,6},{1,7},{2,4},{3,5},{4,2},{5,3},{6,0},{7,1},{8,14},{9,15},{10,... | collective-permute-start | bytes 196616 | tf_op jit(solution)/shard_map/ppermute | solution.py:15
  25.4 1.9 %collective-permute-start.5 = (f32[8,2048]{1,0:T(8,128)S(1)}, f32[8,2048]{1,0:T(8,128)S(1)}, u32[]{:S(2)}, u32[]{:S(2)}) collective-permute-start(f32[8,2048]{1,0:T(8,128)S(1)} %slice_add_fusion), channel_id=1, source_target_pairs={{0,2},{1,3},{2,0},{3,1},{4,6},{5,7},{6,4},{7,5},{8,10},{9,11},{10,... | collective-permute-start | bytes 196616 | tf_op jit(solution)/shard_map/ppermute | solution.py:15
  27.3 0.2 broadcast_compare_fusion.1
  27.7 1.3 %collective-permute-done.7 = f32[8,2048]{1,0:T(8,128)S(1)} collective-permute-done((f32[8,2048]{1,0:T(8,128)S(1)}, f32[8,2048]{1,0:T(8,128)S(1)}, u32[]{:S(2)}, u32[]{:S(2)}) %collective-permute-start.7) | collective-permute-done | bytes 65568 | tf_op jit(solution)/shard_map/ppermute | solution.py:15
  29.0 1.2 %collective-permute-done.6 = f32[8,2048]{1,0:T(8,128)S(1)} collective-permute-done((f32[8,2048]{1,0:T(8,128)S(1)}, f32[8,2048]{1,0:T(8,128)S(1)}, u32[]{:S(2)}, u32[]{:S(2)}) %collective-permute-start.6) | collective-permute-done | bytes 65568 | tf_op jit(solution)/shard_map/ppermute | solution.py:15
  30.3 0.7 %slice_add_fusion.9 = (f32[2,2048]{1,0:T(2,128)S(1)}, f32[2,2048]{1,0:T(2,128)S(1)}, f32[2,2048]{1,0:T(2,128)S(1)}, bf16[2,2048]{1,0:T(2,128)(2,1)}, f32[2,2048]{1,0:T(2,128)S(1)}) fusion(f32[8,2048]{1,0:T(8,128)S(1)} %collective-permute-done.7, f32[8,2048]{1,0:T(8,128)S(1)} %collective-permute-done.6, f32[8,2048]{1,0:T(8,128)S(1)} %collective-permute-done.5, ...), kind=kLoop, calls=%fused_computation.101 | loop fusion | flops 69632 | bytes 344064 | tf_op jit(solution)/shard_map/add | solution.py:67
  31.1 0.8 %fusion.49 = f32[16,16]{1,0:T(8,128)} fusion(f32[16,16]{1,0:T(8,128)S(1)} %reduce_sum.92, s32[16]{0:T(128)S(1)} %fusion.66), kind=kOutput, calls=%fused_computation.118 | convolution fusion | flops 49664 | bytes 2112 | tf_op jit(solution)/shard_map/dot_general | solution.py:86
  31.9 0.4 collective-permute-done.8
  32.3 3.4 %select_convert_fusion = (bf16[16,1024]{1,0:T(8,128)(2,1)S(1)}, f32[16,1024]{1,0:T(8,128)S(1)}) fusion(f32[16,1024]{1,0:T(8,128)S(1)} %get-tuple-element.71, f32[1024]{0:T(1024)S(1)} %copy-done.4, s32[16]{0:T(128)S(1)} %get-tuple-element.13, s32[16]{0:T(128)S(1)} %get-tuple-element.14, s32[16]{0:T(128)S(1)} %get-tuple-element.15, s32[1024]{0:T(1024)S(1)} %fusion.52, ...), kind=kOutput, calls=%fused_computation.76 | convolution fusion | flops 67469312 | bytes 4432128 | tf_op jit(solution)/shard_map/dot_general | solution.py:90
  35.7 0.2 fusion.30
  36.1 3.7 %collective-permute-start.11 = (bf16[48,512]{1,0:T(8,128)(2,1)S(1)}, bf16[48,512]{1,0:T(8,128)(2,1)S(1)}, u32[]{:S(2)}, u32[]{:S(2)}) collective-permute-start(bf16[48,512]{1,0:T(8,128)(2,1)S(1)} %get-tuple-element.58), channel_id=1, source_target_pairs={{0,24},{8,16},{16,8},{24,0},{1,25},{9,17},{17,9},{25,1},{2,26},{10... | collective-permute-start | bytes 147464 | tf_op jit(solution)/shard_map/ppermute | solution.py:15
  39.8 0.8 %collective-permute-start.9 = (bf16[48,512]{1,0:T(8,128)(2,1)S(1)}, bf16[48,512]{1,0:T(8,128)(2,1)S(1)}, u32[]{:S(2)}, u32[]{:S(2)}) collective-permute-start(bf16[48,512]{1,0:T(8,128)(2,1)S(1)} %get-tuple-element.60), channel_id=1, source_target_pairs={{0,8},{8,0},{16,24},{24,16},{1,9},{9,1},{17,25},{25,17},{2,10},{10... | collective-permute-start | bytes 147464 | tf_op jit(solution)/shard_map/ppermute | solution.py:15
  40.7 1.4 %collective-permute-done.11 = bf16[48,512]{1,0:T(8,128)(2,1)S(1)} collective-permute-done((bf16[48,512]{1,0:T(8,128)(2,1)S(1)}, bf16[48,512]{1,0:T(8,128)(2,1)S(1)}, u32[]{:S(2)}, u32[]{:S(2)}) %collective-permute-start.11) | collective-permute-done | bytes 49184 | tf_op jit(solution)/shard_map/ppermute | solution.py:15
  42.1 2.6 %collective-permute-done.10 = bf16[48,512]{1,0:T(8,128)(2,1)S(1)} collective-permute-done((bf16[48,512]{1,0:T(8,128)(2,1)S(1)}, bf16[48,512]{1,0:T(8,128)(2,1)S(1)}, u32[]{:S(2)}, u32[]{:S(2)}) %collective-permute-start.10) | collective-permute-done | bytes 49184 | tf_op jit(solution)/shard_map/ppermute | solution.py:15
  45.6 3.1 %subtract_divide_fusion = f32[1024,512]{1,0:T(8,128)} fusion(bf16[128,1024]{1,0:T(8,128)(2,1)S(1)} %fusion.40, f32[1024]{0:T(1024)S(1)} %add_sqrt_fusion, f32[1024]{0:T(1024)S(1)} %add_add_fusion, bf16[1024,2048]{1,0:T(8,128)(2,1)} %fusion.1, s32[]{:T(128)S(6)} %select_n.79, bf16[32,512]{1,0:T(8,128)(2,1)S(1)} %slice.370, bf16[32,512]{1,0:T(8,128)(2,1)S(1)} %slice.369, ...), kind=kOutput, calls=%fused_computation.4 | convolution fusion | flops 136839168 | bytes 3547140 | tf_op jit(solution)/shard_map/dot_general | solution.py:134
  (82 shorter events, 1.9 us)
Async XLA Ops:
  2.1 7.7 %collective-permute-start = (bf16[2,2176]{1,0:T(2,128)(2,1)S(1)}, bf16[2,2176]{1,0:T(2,128)(2,1)S(1)}, u32[]{:S(2)}, u32[]{:S(2)}) collective-permute-start(bf16[2,2176]{1,0:T(2,128)(2,1)S(1)} %pad_maximum_fusion.5), channel_id=1, source_target_pairs={{0,1},{1,0},{2,3},{3,2},{4,5},{5,4},{6,7},{7,6},{8,9},{9,8},{10,11... | collective-permute-start | bytes 26120 | tf_op jit(solution)/shard_map/ppermute | solution.py:15
  2.6 3.4 %copy-start.1 = (bf16[1024,2048]{1,0:T(8,128)(2,1)S(1)}, bf16[1024,2048]{1,0:T(8,128)(2,1)}, u32[]{:S(2)}) copy-start(bf16[1024,2048]{1,0:T(8,128)(2,1)} %param.7) | copy-start | bytes 12582916
  6.1 3.7 %copy-start.3 = (bf16[2,2048]{1,0:T(2,128)(2,1)S(1)}, bf16[2,2048]{1,0:T(2,128)(2,1)}, u32[]{:S(2)}) copy-start(bf16[2,2048]{1,0:T(2,128)(2,1)} %param.5) | copy-start | bytes 24580
  6.1 12.0 %copy-start.2 = (f32[2048]{0:T(1024)S(1)}, f32[2048]{0:T(1024)}, u32[]{:S(2)}) copy-start(f32[2048]{0:T(1024)} %param.9) | copy-start | bytes 24580
  6.1 12.0 %copy-start.4 = (f32[1024]{0:T(1024)S(1)}, f32[1024]{0:T(1024)}, u32[]{:S(2)}) copy-start(f32[1024]{0:T(1024)} %param.8) | copy-start | bytes 12292
  9.8 5.3 %collective-permute-start.3 = (bf16[4,2176]{1,0:T(4,128)(2,1)S(1)}, bf16[4,2176]{1,0:T(4,128)(2,1)S(1)}, u32[]{:S(2)}, u32[]{:S(2)}) collective-permute-start(bf16[4,2176]{1,0:T(4,128)(2,1)S(1)} %pad_maximum_fusion.4), channel_id=1, source_target_pairs={{0,6},{1,7},{2,4},{3,5},{4,2},{5,3},{6,0},{7,1},{8,14},{9,15},{10,... | collective-permute-start | bytes 52232 | tf_op jit(solution)/shard_map/ppermute | solution.py:15
  13.4 3.8 %collective-permute-start.2 = (bf16[4,2176]{1,0:T(4,128)(2,1)S(1)}, bf16[4,2176]{1,0:T(4,128)(2,1)S(1)}, u32[]{:S(2)}, u32[]{:S(2)}) collective-permute-start(bf16[4,2176]{1,0:T(4,128)(2,1)S(1)} %pad_maximum_fusion.4), channel_id=1, source_target_pairs={{0,4},{1,5},{2,6},{3,7},{4,0},{5,1},{6,2},{7,3},{8,12},{9,13},{10,... | collective-permute-start | bytes 52232 | tf_op jit(solution)/shard_map/ppermute | solution.py:15
  13.9 3.8 %collective-permute-start.1 = (bf16[4,2176]{1,0:T(4,128)(2,1)S(1)}, bf16[4,2176]{1,0:T(4,128)(2,1)S(1)}, u32[]{:S(2)}, u32[]{:S(2)}) collective-permute-start(bf16[4,2176]{1,0:T(4,128)(2,1)S(1)} %pad_maximum_fusion.4), channel_id=1, source_target_pairs={{0,2},{1,3},{2,0},{3,1},{4,6},{5,7},{6,4},{7,5},{8,10},{9,11},{10,... | collective-permute-start | bytes 52232 | tf_op jit(solution)/shard_map/ppermute | solution.py:15
  17.8 4.0 %copy-start = (bf16[1024,2048]{1,0:T(8,128)(2,1)S(1)}, bf16[1024,2048]{1,0:T(8,128)(2,1)}, u32[]{:S(2)}) copy-start(bf16[1024,2048]{1,0:T(8,128)(2,1)} %fusion.1) | copy-start | bytes 12582916
  22.4 1.3 %collective-permute-start.4 = (f32[8,2048]{1,0:T(8,128)S(1)}, f32[8,2048]{1,0:T(8,128)S(1)}, u32[]{:S(2)}, u32[]{:S(2)}) collective-permute-start(f32[8,2048]{1,0:T(8,128)S(1)} %slice.323), channel_id=1, source_target_pairs={{0,1},{1,0},{2,3},{3,2},{4,5},{5,4},{6,7},{7,6},{8,9},{9,8},{10,11... | collective-permute-start | bytes 196616 | tf_op jit(solution)/shard_map/ppermute | solution.py:15
  23.7 5.3 %collective-permute-start.7 = (f32[8,2048]{1,0:T(8,128)S(1)}, f32[8,2048]{1,0:T(8,128)S(1)}, u32[]{:S(2)}, u32[]{:S(2)}) collective-permute-start(f32[8,2048]{1,0:T(8,128)S(1)} %slice_add_fusion), channel_id=1, source_target_pairs={{0,6},{1,7},{2,4},{3,5},{4,2},{5,3},{6,0},{7,1},{8,14},{9,15},{10,... | collective-permute-start | bytes 196616 | tf_op jit(solution)/shard_map/ppermute | solution.py:15
  25.3 5.0 %collective-permute-start.6 = (f32[8,2048]{1,0:T(8,128)S(1)}, f32[8,2048]{1,0:T(8,128)S(1)}, u32[]{:S(2)}, u32[]{:S(2)}) collective-permute-start(f32[8,2048]{1,0:T(8,128)S(1)} %slice_add_fusion), channel_id=1, source_target_pairs={{0,4},{1,5},{2,6},{3,7},{4,0},{5,1},{6,2},{7,3},{8,12},{9,13},{10,... | collective-permute-start | bytes 196616 | tf_op jit(solution)/shard_map/ppermute | solution.py:15
  25.4 4.9 %collective-permute-start.5 = (f32[8,2048]{1,0:T(8,128)S(1)}, f32[8,2048]{1,0:T(8,128)S(1)}, u32[]{:S(2)}, u32[]{:S(2)}) collective-permute-start(f32[8,2048]{1,0:T(8,128)S(1)} %slice_add_fusion), channel_id=1, source_target_pairs={{0,2},{1,3},{2,0},{3,1},{4,6},{5,7},{6,4},{7,5},{8,10},{9,11},{10,... | collective-permute-start | bytes 196616 | tf_op jit(solution)/shard_map/ppermute | solution.py:15
  31.0 1.3 %collective-permute-start.8 = (bf16[8,2048]{1,0:T(8,128)(2,1)S(1)}, bf16[8,2048]{1,0:T(8,128)(2,1)S(1)}, u32[]{:S(2)}, u32[]{:S(2)}) collective-permute-start(bf16[8,2048]{1,0:T(8,128)(2,1)S(1)} %fusion.35), channel_id=1, source_target_pairs={{0,1},{1,0},{2,3},{3,2},{4,5},{5,4},{6,7},{7,6},{8,9},{9,8},{10,11... | collective-permute-start | bytes 98312 | tf_op jit(solution)/shard_map/ppermute | solution.py:15
  36.1 6.0 %collective-permute-start.11 = (bf16[48,512]{1,0:T(8,128)(2,1)S(1)}, bf16[48,512]{1,0:T(8,128)(2,1)S(1)}, u32[]{:S(2)}, u32[]{:S(2)}) collective-permute-start(bf16[48,512]{1,0:T(8,128)(2,1)S(1)} %get-tuple-element.58), channel_id=1, source_target_pairs={{0,24},{8,16},{16,8},{24,0},{1,25},{9,17},{17,9},{25,1},{2,26},{10... | collective-permute-start | bytes 147464 | tf_op jit(solution)/shard_map/ppermute | solution.py:15
  39.8 5.0 %collective-permute-start.10 = (bf16[48,512]{1,0:T(8,128)(2,1)S(1)}, bf16[48,512]{1,0:T(8,128)(2,1)S(1)}, u32[]{:S(2)}, u32[]{:S(2)}) collective-permute-start(bf16[48,512]{1,0:T(8,128)(2,1)S(1)} %get-tuple-element.59), channel_id=1, source_target_pairs={{0,16},{8,24},{16,0},{24,8},{1,17},{9,25},{17,1},{25,9},{2,18},{10... | collective-permute-start | bytes 147464 | tf_op jit(solution)/shard_map/ppermute | solution.py:15
  39.8 5.2 %collective-permute-start.9 = (bf16[48,512]{1,0:T(8,128)(2,1)S(1)}, bf16[48,512]{1,0:T(8,128)(2,1)S(1)}, u32[]{:S(2)}, u32[]{:S(2)}) collective-permute-start(bf16[48,512]{1,0:T(8,128)(2,1)S(1)} %get-tuple-element.60), channel_id=1, source_target_pairs={{0,8},{8,0},{16,24},{24,16},{1,9},{9,1},{17,25},{25,17},{2,10},{10... | collective-permute-start | bytes 147464 | tf_op jit(solution)/shard_map/ppermute | solution.py:15

commit v2 on v0

v2 whole, which is shorter than its diff:
```python
import functools

import jax
import jax.numpy as jnp
from jax import lax
from jax.experimental import pallas as pl
from jax.experimental.pallas import tpu as pltpu
from jax.sharding import PartitionSpec as P

BLK = 64
CAP = 2
RADIX = 32
LANES = 128
DIRECT = 4
TERMS = 8
VMEM = pl.BlockSpec(memory_space=pltpu.VMEM)
HBM = pl.BlockSpec(memory_space=pltpu.MemorySpace.HBM)
ANY = pl.BlockSpec(memory_space=pl.ANY)
F32, BF16 = jnp.float32, jnp.bfloat16


def swap(x, axis, mask):
    size = lax.axis_size(axis)
    return lax.ppermute(x, axis, [(i, i ^ mask) for i in range(size)])


def params(mib):
    return pltpu.CompilerParams(vmem_limit_bytes=mib * 2**20)


def shape(dims, dtype):
    return jax.ShapeDtypeStruct(dims, dtype)


def normalize_kernel(after_ref, weights_ref, unit_ref, turned_ref, norms_ref, held_ref, sems):
    del after_ref
    lat_rows, width = weights_ref.shape
    copies = []
    for at in range(lat_rows // LANES):
        rows = pl.ds(at * LANES, LANES)
        copies.append(
            pltpu.make_async_copy(weights_ref.at[rows], held_ref.at[rows], sems.at[at])
        )
        copies[-1].start()
    for at, copy in enumerate(copies):
        copy.wait()
        rows = pl.ds(at * LANES, LANES)
        squares = jnp.zeros((LANES, LANES), F32)
        for left in range(0, width, LANES):
            tile = held_ref[rows, left : left + LANES].astype(F32)
            squares = squares + tile * tile
        norms = jnp.sqrt(jnp.sum(squares, axis=1, keepdims=True) + 1e-06)
        norms_ref[rows, :] = norms
        scale = jnp.broadcast_to(1.0 / norms, (LANES, LANES))
        for left in range(0, width, LANES):
            tile = held_ref[rows, left : left + LANES].astype(F32)
            unit = (tile * scale).astype(BF16)
            unit_ref[rows, left : left + LANES] = unit
            turned_ref[left : left + LANES, rows] = unit.T


def normalize(after, weights):
    lat_rows, width = weights.shape
    return pl.pallas_call(
        normalize_kernel,
        name="normalize",
        out_shape=(
            shape((lat_rows, width), BF16),
            shape((width, lat_rows), BF16),
            shape((lat_rows, 1), F32),
        ),
        in_specs=[ANY, HBM],
        out_specs=(VMEM, VMEM, VMEM),
        scratch_shapes=[
            pltpu.VMEM((lat_rows, width), BF16),
            pltpu.SemaphoreType.DMA((lat_rows // LANES,)),
        ],
        compiler_params=params(20),
        cost_estimate=pl.CostEstimate(
            flops=4 * lat_rows * width, bytes_accessed=6 * lat_rows * width, transcendentals=0
        ),
    )(after, weights)


def forward_kernel(rows_dev, top, dec_ref, enc_ref, unit_ref, turned_ref, *refs):
    chips = len(refs) - 9
    pieces = refs[:chips]
    keep_ref, send_ref, cent_ref, own_ref, codes_ref, base_ref, act_ref, hit_ref, rows_ref = refs[
        chips:
    ]
    half = chips * rows_dev
    lat_rows, width = unit_ref.shape
    for k, piece in enumerate(pieces):
        value = piece[...].astype(F32)
        rows_ref[k * rows_dev : (k + 1) * rows_dev, :] = value[:rows_dev]
        rows_ref[half + k * rows_dev : half + (k + 1) * rows_dev, :] = value[rows_dev:]
    own_ref[...] = rows_ref[:half, :width]
    centered = (rows_ref[:, :width] - dec_ref[...]).astype(BF16)
    cent_ref[...] = centered
    base = jnp.dot(centered, turned_ref[...], preferred_element_type=F32)
    base_ref[...] = base
    preact = base + enc_ref[...]
    act = jnp.maximum(preact, 0.0) + jnp.log1p(jnp.exp(-jnp.abs(preact)))
    act_ref[...] = act
    first = lax.axis_index("latent") * (lat_rows // BLK)
    lat = lax.broadcasted_iota(jnp.int32, (2 * half, lat_rows), 1)
    block_of = (first + lat // BLK).astype(F32)
    names = rows_ref[:, width:]
    hit = jnp.zeros((2 * half, lat_rows), F32)
    for k in range(top):
        name = names[:, k : k + 1] * RADIX + names[:, top + k : top + k + 1]
        hit = jnp.where(name == block_of, 1.0, hit)
    hit_ref[...] = hit
    codes = (act * hit).astype(BF16)
    codes_ref[...] = codes
    contrib = jnp.dot(codes, unit_ref[...], preferred_element_type=F32)
    keep_ref[...] = contrib[:half]
    send_ref[...] = contrib[half:]


def forward(rows_dev, top, dec, enc, unit, turned, pieces):
    lat_rows, width = unit.shape
    half = len(pieces) * rows_dev
    count = 2 * half
    return pl.pallas_call(
        functools.partial(forward_kernel, rows_dev, top),
        name="forward",
        out_shape=(
            shape((half, width), F32),
            shape((half, width), F32),
            shape((count, width), BF16),
            shape((half, width), F32),
            shape((count, lat_rows), BF16),
            shape((count, lat_rows), F32),
            shape((count, lat_rows), F32),
            shape((count, lat_rows), F32),
        ),
        in_specs=[VMEM] * (4 + len(pieces)),
        out_specs=(VMEM,) * 8,
        scratch_shapes=[pltpu.VMEM((count, width + LANES), F32)],
        compiler_params=params(20),
        cost_estimate=pl.CostEstimate(
            flops=4 * count * lat_rows * width,
            bytes_accessed=4 * lat_rows * width,
            transcendentals=2 * count * lat_rows,
        ),
    )(dec, enc, unit, turned, *pieces)


def side_kernel(rows_dev, act_ref, hit_ref, codes_ref, base_ref, enc_ref, *outs):
    scores_ref, gate_ref, second_ref, compact_ref = outs
    count, lat_rows = act_ref.shape
    block_count = lat_rows // BLK
    half = count // 2
    me = lax.axis_index("latent")
    latent = lax.broadcasted_iota(jnp.int32, (block_count, lat_rows), 1)
    block = lax.broadcasted_iota(jnp.int32, (block_count, lat_rows), 0)
    inside = jnp.where(latent // BLK == block, 1.0 / BLK, 0.0).astype(F32)
    means = lax.dot_general(
        inside,
        act_ref[...],
        (((1,), (1,)), ((), ())),
        preferred_element_type=F32,
        precision=lax.Precision.HIGHEST,
    )
    at = lax.broadcasted_iota(jnp.int32, (count, count), 0)
    place = lax.broadcasted_iota(jnp.int32, (count, count), 1)
    owner = (place // rows_dev) ^ me
    relative = (owner % 2) * half + (owner // 2) * rows_dev + place % rows_dev
    order = jnp.where(relative == at, 1.0, 0.0).astype(F32)
    scores_ref[...] = jnp.dot(
        means, order, preferred_element_type=F32, precision=lax.Precision.HIGHEST
    )
    hit = hit_ref[...]
    preact = base_ref[...] + enc_ref[...]
    gate_ref[...] = hit * jax.nn.sigmoid(preact)
    earlier = jnp.where(place < at, 1.0, 0.0).astype(BF16)
    before = jnp.dot(earlier, hit.astype(BF16), preferred_element_type=F32)
    second = jnp.where(before == 1.0, hit, 0.0)
    first = jnp.where(before == 0.0, hit, 0.0)
    second_ref[...] = second
    codes = codes_ref[...].astype(F32)
    number = (lax.broadcasted_iota(jnp.int32, (count, lat_rows), 0) + 1).astype(F32)
    rows = []
    for slot in (first, second):
        rows.append(jnp.sum(slot * codes, axis=0, keepdims=True))
    for slot in (first, second):
        rows.append(jnp.sum(slot * number, axis=0, keepdims=True))
    for at, row in enumerate(rows):
        compact_ref[at : at + 1, :] = row


def side(rows_dev, act, hit, codes, base, enc):
    count, lat_rows = act.shape
    return pl.pallas_call(
        functools.partial(side_kernel, rows_dev),
        name="side",
        out_shape=(
            shape((lat_rows // BLK, count), F32),
            shape((count, lat_rows), F32),
            shape((count, lat_rows), F32),
            shape((2 * CAP, lat_rows), F32),
        ),
        in_specs=[VMEM] * 5,
        out_specs=(VMEM,) * 4,
        compiler_params=params(20),
        cost_estimate=pl.CostEstimate(
            flops=8 * count * lat_rows * 64, bytes_accessed=32 * count * lat_rows, transcendentals=0
        ),
    )(act, hit, codes, base, enc)


def errors_kernel(rows_dev, dec_ref, own_ref, *refs):
    parts, (recon_ref, errors_ref) = refs[:-2], refs[-2:]
    chips = len(parts)
    total = parts[0][...]
    for j in range(1, chips):
        value = parts[j][...]
        turned = [
            value[(k ^ j) * rows_dev : ((k ^ j) + 1) * rows_dev] for k in range(chips)
        ]
        total = total + jnp.concatenate(turned, axis=0)
    full = total + dec_ref[...]
    recon_ref[...] = full[:rows_dev].astype(BF16)
    errors_ref[...] = (full - own_ref[...]).astype(BF16)


def errors_of(rows_dev, dec, own, parts):
    half, width = own.shape
    return pl.pallas_call(
        functools.partial(errors_kernel, rows_dev),
        name="errors",
        out_shape=(shape((rows_dev, width), BF16), shape((half, width), BF16)),
        in_specs=[VMEM] * (2 + len(parts)),
        out_specs=(VMEM, VMEM),
        compiler_params=params(16),
    )(dec, own, *parts)


def backward_kernel(groups, turned_ref, mine_ref, other_ref, cent_ref, *refs):
    codes_ref, base_ref, gate_ref, second_ref, compact_ref = refs[:5]
    packets, errors_ref = refs[5:-1], refs[-1]
    width, lat_rows = turned_ref.shape
    half = mine_ref.shape[0]
    count = 2 * half
    cols = width // groups
    errors_ref[:half, :] = mine_ref[...]
    errors_ref[half:, :] = other_ref[...]
    grad = jnp.dot(errors_ref[...], turned_ref[...], preferred_element_type=F32)
    pre_grad = (grad * gate_ref[...]).astype(BF16).astype(F32)
    codes = codes_ref[...].astype(F32)
    along = jnp.sum(codes * grad + pre_grad * base_ref[...], axis=0, keepdims=True)
    high = along.astype(BF16).astype(F32)
    both = jnp.sum(pre_grad, axis=0, keepdims=True)
    later = jnp.sum(pre_grad * second_ref[...], axis=0, keepdims=True)
    table = compact_ref[...]
    terms = jnp.concatenate([table, both - later, later, high, along - high], axis=0).astype(BF16)
    group = lax.axis_index("dp")
    for k, packet in enumerate(packets):
        at = pl.ds(pl.multiple_of((group ^ k) * cols, LANES), cols)
        packet[:count, :] = errors_ref[:, at]
        packet[count : 2 * count, :] = cent_ref[:, at]
        for part in range(lat_rows // cols):
            rows = pl.ds(2 * count + part * TERMS, TERMS)
            packet[rows, :] = terms[:, part * cols : (part + 1) * cols]


def backward(groups, turned, mine, other, cent, codes, base, gate, second, compact):
    width, lat_rows = turned.shape
    count = cent.shape[0]
    cols = width // groups
    packet = shape((2 * count + TERMS * lat_rows // cols, cols), BF16)
    return pl.pallas_call(
        functools.partial(backward_kernel, groups),
        name="backward",
        out_shape=(packet,) * groups,
        in_specs=[VMEM] * 9,
        out_specs=(VMEM,) * groups,
        scratch_shapes=[pltpu.VMEM((count, width), BF16)],
        compiler_params=params(20),
        cost_estimate=pl.CostEstimate(
            flops=2 * count * lat_rows * width, bytes_accessed=2 * lat_rows * width, transcendentals=0
        ),
    )(turned, mine, other, cent, codes, base, gate, second, compact)


def gradient_kernel(count, unit_ref, norms_ref, *refs):
    out_ref, left_ref, right_ref, held_ref, sems = refs[-5:]
    packets = refs[:-5]
    lat_rows, cols = out_ref.shape
    along = jnp.zeros((1, lat_rows), F32)
    number = (lax.broadcasted_iota(jnp.int32, (count, lat_rows), 0) + 1).astype(F32)
    for g, packet in enumerate(packets):
        base = g * 2 * count
        right_ref[base : base + 2 * count, :] = packet[: 2 * count, :]
        parts = [
            packet[2 * count + p * TERMS : 2 * count + (p + 1) * TERMS, :].astype(F32)
            for p in range(lat_rows // cols)
        ]
        terms = jnp.concatenate(parts, axis=1)
        code0, code1, row0, row1, grad0, grad1, high, low = [
            terms[t : t + 1] for t in range(TERMS)
        ]
        at0, at1 = number == row0, number == row1
        code = jnp.where(at0, code0, jnp.where(at1, code1, 0.0))
        grad = jnp.where(at0, grad0, jnp.where(at1, grad1, 0.0))
        left_ref[base : base + count, :] = code.astype(BF16)
        left_ref[base + count : base + 2 * count, :] = grad.astype(BF16)
        along = along + (high + low)
    start = pl.multiple_of(lax.axis_index("dp") * cols, LANES)
    copies = []
    for at in range(lat_rows // LANES):
        rows = pl.ds(at * LANES, LANES)
        outer = lax.dot_general(
            left_ref[:, rows],
            right_ref[...],
            (((0,), (0,)), ((), ())),
            preferred_element_type=F32,
        )
        column = jnp.broadcast_to(along[:, at * LANES : (at + 1) * LANES], (LANES, LANES)).T
        unit = unit_ref[rows, pl.ds(start, cols)].astype(F32)
        inverse = 1.0 / norms_ref[rows, :]
        held_ref[rows, :] = (outer - unit * column[:, :1]) * inverse
        copies.append(pltpu.make_async_copy(held_ref.at[rows], out_ref.at[rows], sems.at[at]))
        copies[-1].start()
    for copy in copies:
        copy.wait()


def gradient(count, unit, norms, packets):
    lat_rows = unit.shape[0]
    cols = packets[0].shape[1]
    depth = 2 * count * len(packets)
    return pl.pallas_call(
        functools.partial(gradient_kernel, count),
        name="gradient",
        out_shape=shape((lat_rows, cols), F32),
        in_specs=[VMEM] * (2 + len(packets)),
        out_specs=HBM,
        scratch_shapes=[
            pltpu.VMEM((depth, lat_rows), BF16),
            pltpu.VMEM((depth, cols), BF16),
            pltpu.VMEM((lat_rows, cols), F32),
            pltpu.SemaphoreType.DMA((lat_rows // LANES,)),
        ],
        compiler_params=params(24),
        cost_estimate=pl.CostEstimate(
            flops=2 * depth * lat_rows * cols, bytes_accessed=8 * lat_rows * cols, transcendentals=0
        ),
    )(unit, norms, *packets)


def local(inputs, blocks, weights, enc_bias, dec_bias):
    rows_dev = inputs.shape[0]
    top = blocks.shape[1]
    chips = lax.axis_size("latent") // 2
    groups = lax.axis_size("dp")
    count = 2 * chips * rows_dev
    dec, enc = dec_bias[None, :], enc_bias[None, :]

    both_rows = jnp.concatenate([inputs, swap(inputs, "latent", 1)], axis=0)
    both_names = jnp.concatenate([blocks, swap(blocks, "latent", 1)], axis=0)
    lists = jnp.concatenate([both_names // RADIX, both_names % RADIX], axis=1).astype(BF16)
    lists = jnp.pad(lists, ((0, 0), (0, LANES - lists.shape[1])))
    both = jnp.concatenate([both_rows, lists], axis=1)
    pieces = [both] + [swap(both, "latent", 2 * k) for k in range(1, chips)]

    unit, turned, norms = normalize(both, weights)
    keep, send, cent, own, codes, base, act, hit = forward(
        rows_dev, top, dec, enc, unit, turned, pieces
    )
    sums = keep + swap(send, "latent", 1)
    if chips <= DIRECT:
        parts = [sums] + [swap(sums, "latent", 2 * j) for j in range(1, chips)]
        recon, errors = errors_of(rows_dev, dec, own, parts)
    else:
        full = dec_bias + sums[:rows_dev]
        for j in range(1, chips):
            full = full + swap(sums[j * rows_dev : (j + 1) * rows_dev], "latent", 2 * j)
        recon = full.astype(BF16)
        errors = (full - own[:rows_dev]).astype(BF16)
        errors = [errors] + [swap(errors, "latent", 2 * j) for j in range(1, chips)]
        errors = jnp.concatenate(errors, axis=0)
    block_scores, gate, second, compact = side(rows_dev, act, hit, codes, base, enc)
    other = swap(errors, "latent", 1)
    packets = backward(
        groups, turned, errors, other, cent, codes, base, gate, second, compact
    )
    packets = [swap(p, "dp", k) if k else p for k, p in enumerate(packets)]
    grad_weights = gradient(count, unit, norms, packets)
    return (recon, grad_weights, block_scores)


def solution(mesh):
    in_specs = (
        P(("dp", "latent"), None),
        P(("dp", "latent"), None),
        P("latent", None),
        P("latent"),
        P(),
    )
    out_specs = (P(("dp", "latent"), None), P("latent", "dp"), P("latent", "dp"))
    return jax.shard_map(local, mesh=mesh, in_specs=in_specs, out_specs=out_specs, check_vma=False)
```

time: 190 us -> 39.1 us (0.21)
  blocking collectives: 68.8 us -> 0 us
  local copies, waits for them, and re-layouts: 34.6 us -> 2.2 us
  waiting for transfers between devices: 36.1 us -> 12.3 us
  between operations: 15.1 us -> 0.72 us
  other arithmetic: 14.7 us -> 1.5 us
  matrix products: 10.3 us -> 0 us
  Pallas kernels: 0 us -> 9.07 us
  starting transfers between devices: 9.47 us -> 13.1 us
    all_gather x6 -> x0, blocking collectives: 68.8 us -> none  [the longest x1 13.7 us: local(): lax.all_gather(latent_codes[None], 'dp', axis=0, tiled=True)]
    unnamed x2 -> x0, waiting for transfers between devices: 36.1 us -> none
    gather x8 -> x0, local copies, waits for them, and re-layouts: 19.4 us -> none  [the longest x5 18 us: local(): jnp.take_along_axis(dot_blocks, jnp.broadcast_to(row_ids[:, None, :], (bl...]
    ppermute x0 -> x13, starting transfers between devices: none -> 13.1 us  [swap(): return lax.ppermute(x, axis, [(i, i ^ mask) for i in range(size)])]
    ppermute x0 -> x13, waiting for transfers between devices: none -> 12.3 us  [swap(): return lax.ppermute(x, axis, [(i, i ^ mask) for i in range(size)])]
    dot_general x4 -> x0, matrix products: 10.3 us -> none  [the longest x1 3.39 us: local(): jnp.einsum('jcd,jmd->jcm', slot_errors, unit_blocks, preferred_element_ty...]
    all_to_all x2 -> x0, starting transfers between devices: 9.47 us -> none  [the longest x1 4.87 us: local(): lax.all_to_all(slot_rows[None], 'dp', split_axis=3, concat_axis=0, tiled=...]
    pallas_call x0 -> x6, Pallas kernels: none -> 9.07 us  [the longest x1 3.65 us: normalize(): pl.pallas_call(normalize_kernel, name='normalize', out_shape=(shape((lat_...]
  transfers between devices with their start and end apart: 3 -> 13, of which waited for: 1 -> 8; matrix products, arithmetic and copies ran while one was open for 26% -> 2% of each run, Pallas kernels for 0% -> 12%
where the time goes in v2:
time: 39.1 us; the launch traced here: 38.8 us
  starting transfers between devices  13.1 us (34%)
  waiting for transfers between devices  12.3 us (31%)
  Pallas kernels  9.07 us (23%)
  local copies, waits for them, and re-layouts  2.2 us (6%)
  other arithmetic  1.5 us (4%)
  between operations  0.72 us (2%)
    ppermute x13, starting transfers between devices, swap(): return lax.ppermute(x, axis, [(i, i ^ mask) for i in range(size)])  13.1 us
    ppermute x13, waiting for transfers between devices, swap(): return lax.ppermute(x, axis, [(i, i ^ mask) for i in range(size)])  12.3 us
    pallas_call x1, Pallas kernels, normalize(): pl.pallas_call(normalize_kernel, name='normalize', out_shape=(shape((lat_...  3.65 us
    unnamed x6, local copies, waits for them, and re-layouts  2.2 us
    pallas_call x1, Pallas kernels, gradient(): pl.pallas_call(functools.partial(gradient_kernel, count), name='gradient'...  1.85 us
    pallas_call x1, Pallas kernels, forward(): pl.pallas_call(functools.partial(forward_kernel, rows_dev, top), name='fo...  1.26 us
    pallas_call x1, Pallas kernels, side(): pl.pallas_call(functools.partial(side_kernel, rows_dev), name='side', out...  0.97 us
  transfers between devices with their start and end apart: 13, of which 8 were waited for; matrix products, arithmetic and copies ran while one was open for 2% of the time, Pallas kernels for 12%

profile of v2, /device:TPU:0, one launch (start us, length us, event | category | flops | bytes accessed | tf_op | source)
XLA Modules:
  0.0 38.8 jit_solution(7331151408819659276)
XLA Ops:
  0.7 0.5 %collective-permute-start.1 = (s32[2,4]{1,0:T(2,128)}, s32[2,4]{1,0:T(2,128)S(1)}, u32[]{:S(2)}, u32[]{:S(2)}) collective-permute-start(s32[2,4]{1,0:T(2,128)} %param.6), channel_id=1, source_target_pairs={{0,1},{1,0},{2,3},{3,2},{4,5},{5,4},{6,7},{7,6},{8,9},{9,8},{10,11... | collective-permute-start | bytes 104 | tf_op jit(solution)/shard_map/ppermute | solution.py:24
  1.2 0.1 collective-permute-start
  1.2 1.0 %collective-permute-done.1 = s32[2,4]{1,0:T(2,128)S(1)} collective-permute-done((s32[2,4]{1,0:T(2,128)}, s32[2,4]{1,0:T(2,128)S(1)}, u32[]{:S(2)}, u32[]{:S(2)}) %collective-permute-start.1) | collective-permute-done | bytes 64 | tf_op jit(solution)/shard_map/ppermute | solution.py:24
  2.2 0.7 %fusion = (bf16[4,4]{1,0:T(4,128)(2,1)S(1)}, bf16[4,4]{1,0:T(4,128)(2,1)S(1)}) fusion(s32[2,4]{1,0:T(2,128)S(1)} %collective-permute-done.1, s32[2,4]{1,0:T(2,128)} %param.6), kind=kLoop, calls=%fused_computation.6 | loop fusion | flops 352 | bytes 128 | tf_op jit(solution)/shard_map/convert
  2.9 0.1 fusion.5
  3.0 0.7 %pad_maximum_fusion.after_ref.refs_0_ = bf16[4,2176]{1,0:T(4,128)(2,1)S(1)} fusion(bf16[4,128]{1,0:T(4,128)(2,1)S(1)} %fusion.5, bf16[2,2048]{1,0:T(2,128)(2,1)S(1)} %collective-permute-done, bf16[2,2048]{1,0:T(2,128)(2,1)} %param.5), kind=kLoop, calls=%fused_computation | loop fusion | flops 52224 | bytes 34816 | tf_op jit(solution)/shard_map/concatenate | solution.py:365
  3.7 3.8 %collective-permute-start.4 = (bf16[4,2176]{1,0:T(4,128)(2,1)S(1)}, bf16[4,2176]{1,0:T(4,128)(2,1)S(1)}, u32[]{:S(2)}, u32[]{:S(2)}) collective-permute-start(bf16[4,2176]{1,0:T(4,128)(2,1)S(1)} %pad_maximum_fusion.after_ref.refs_0_), channel_id=1, source_target_pairs={{0,6},{1,7},{2,4},{3,5},{4,2},{5,3},{6,0},{7,1},{8,14},{9,15},{10,... | collective-permute-start | bytes 52232 | tf_op jit(solution)/shard_map/ppermute | solution.py:24
  7.5 0.5 %collective-permute-start.3 = (bf16[4,2176]{1,0:T(4,128)(2,1)S(1)}, bf16[4,2176]{1,0:T(4,128)(2,1)S(1)}, u32[]{:S(2)}, u32[]{:S(2)}) collective-permute-start(bf16[4,2176]{1,0:T(4,128)(2,1)S(1)} %pad_maximum_fusion.after_ref.refs_0_), channel_id=1, source_target_pairs={{0,4},{1,5},{2,6},{3,7},{4,0},{5,1},{6,2},{7,3},{8,12},{9,13},{10,... | collective-permute-start | bytes 52232 | tf_op jit(solution)/shard_map/ppermute | solution.py:24
  8.0 0.1 collective-permute-start.2
  8.2 2.2 %copy-done = bf16[1024,2048]{1,0:T(8,128)(2,1)S(1)} copy-done((bf16[1024,2048]{1,0:T(8,128)(2,1)S(1)}, bf16[1024,2048]{1,0:T(8,128)(2,1)}, u32[]{:S(2)}) %copy-start) | copy-done | bytes 4194328
  10.4 3.7 %normalize.1 = (bf16[1024,2048]{1,0:T(8,128)(2,1)S(1)}, bf16[2048,1024]{1,0:T(8,128)(2,1)S(1)}, f32[1024,1]{1,0:T(8,128)S(1)}) custom-call(bf16[4,2176]{1,0:T(4,128)(2,1)S(1)} %pad_maximum_fusion.after_ref.refs_0_, bf16[1024,2048]{1,0:T(8,128)(2,1)S(1)} %copy-done), custom_call_target="tpu_custom_call" | custom-call | flops 8388608 | bytes 12582912 | tf_op jit(solution)/shard_map/normalize/pallas_call | solution.py:64
  14.0 0.0 collective-permute-done.4.refs_3_
  14.0 0.0 collective-permute-done.3.refs_2_
  14.1 1.3 %forward.1 = (f32[8,2048]{1,0:T(8,128)S(1)}, f32[8,2048]{1,0:T(8,128)S(1)}, bf16[16,2048]{1,0:T(8,128)(2,1)S(1)}, f32[8,2048]{1,0:T(8,128)S(1)}, bf16[16,1024]{1...) custom-call(f32[1,2048]{1,0:T(1,128)S(1)} %bitcast.2, ...), custom_call_target="tpu_custom_call" | custom-call | flops 134217728 | bytes 8388608 | tf_op jit(solution)/shard_map/forward/pallas_call | solution.py:125
  15.3 1.3 %collective-permute-done.5 = f32[8,2048]{1,0:T(8,128)S(1)} collective-permute-done((f32[8,2048]{1,0:T(8,128)S(1)}, f32[8,2048]{1,0:T(8,128)S(1)}, u32[]{:S(2)}, u32[]{:S(2)}) %collective-permute-start.5) | collective-permute-done | bytes 65568 | tf_op jit(solution)/shard_map/ppermute | solution.py:24
  16.6 2.9 %collective-permute-start.8 = (f32[8,2048]{1,0:T(8,128)S(1)}, f32[8,2048]{1,0:T(8,128)S(1)}, u32[]{:S(2)}, u32[]{:S(2)}) collective-permute-start(f32[8,2048]{1,0:T(8,128)S(1)} %add.13.refs_0_), channel_id=1, source_target_pairs={{0,6},{1,7},{2,4},{3,5},{4,2},{5,3},{6,0},{7,1},{8,14},{9,15},{10,... | collective-permute-start | bytes 196616 | tf_op jit(solution)/shard_map/ppermute | solution.py:24
  19.5 0.5 %collective-permute-start.7 = (f32[8,2048]{1,0:T(8,128)S(1)}, f32[8,2048]{1,0:T(8,128)S(1)}, u32[]{:S(2)}, u32[]{:S(2)}) collective-permute-start(f32[8,2048]{1,0:T(8,128)S(1)} %add.13.refs_0_), channel_id=1, source_target_pairs={{0,4},{1,5},{2,6},{3,7},{4,0},{5,1},{6,2},{7,3},{8,12},{9,13},{10,... | collective-permute-start | bytes 196616 | tf_op jit(solution)/shard_map/ppermute | solution.py:24
  20.0 0.1 collective-permute-start.6
  20.2 1.8 %collective-permute-done.8.refs_3_ = f32[8,2048]{1,0:T(8,128)S(1)} collective-permute-done((f32[8,2048]{1,0:T(8,128)S(1)}, f32[8,2048]{1,0:T(8,128)S(1)}, u32[]{:S(2)}, u32[]{:S(2)}) %collective-permute-start.8) | collective-permute-done | bytes 65568 | tf_op jit(solution)/shard_map/ppermute | solution.py:24
  21.9 1.9 %collective-permute-done.7.refs_2_ = f32[8,2048]{1,0:T(8,128)S(1)} collective-permute-done((f32[8,2048]{1,0:T(8,128)S(1)}, f32[8,2048]{1,0:T(8,128)S(1)}, u32[]{:S(2)}, u32[]{:S(2)}) %collective-permute-start.7) | collective-permute-done | bytes 65568 | tf_op jit(solution)/shard_map/ppermute | solution.py:24
  23.8 0.5 %collective-permute-done.6.refs_1_ = f32[8,2048]{1,0:T(8,128)S(1)} collective-permute-done((f32[8,2048]{1,0:T(8,128)S(1)}, f32[8,2048]{1,0:T(8,128)S(1)}, u32[]{:S(2)}, u32[]{:S(2)}) %collective-permute-start.6) | collective-permute-done | bytes 65568 | tf_op jit(solution)/shard_map/ppermute | solution.py:24
  24.3 0.6 %errors.1 = (bf16[2,2048]{1,0:T(2,128)(2,1)}, bf16[8,2048]{1,0:T(8,128)(2,1)S(1)}) custom-call(f32[1,2048]{1,0:T(1,128)S(1)} %bitcast.3, f32[8,2048]{1,0:T(8,128)S(1)} %get-tuple-element.26.own_ref, f32[8,2048]{1,0:T(8,128)S(1)} %add.13.refs_0_, f32[8,2048]{1,0:T(8,128)S(1)} %collective-permute-done.6.refs_1_, f32[8,2048]{1,0:T(8,128)S(1)} %collective-permute-done.7.refs_2_, ...), custom_call_target="tpu_custom_call" | custom-call | tf_op jit(solution)/shard_map/errors/pallas_call | solution.py:230
  24.9 1.0 %side.1 = (f32[16,16]{1,0:T(8,128)}, f32[16,1024]{1,0:T(8,128)S(1)}, f32[16,1024]{1,0:T(8,128)S(1)}, f32[4,1024]{1,0:T(4,128)S(1)}) custom-call(f32[16,1024]{1,0:T(8,128)S(1)} %get-tuple-element.35.act_ref, f32[16,1024]{1,0:T(8,128)S(1)} %get-tuple-element.36.hit_ref, bf16[16,1024]{1,0:T(8,128)(2,1)S(1)} %get-tuple-element.33.codes_ref.refs_0_, ...), custom_call_target="tpu_custom_call" | custom-call | flops 8388608 | bytes 524288 | tf_op jit(solution)/shard_map/side/pallas_call | solution.py:195
  25.9 0.2 collective-permute-done.9.other_ref
  26.1 0.7 %backward.1 = (bf16[48,512]{1,0:T(8,128)(2,1)S(1)}, bf16[48,512]{1,0:T(8,128)(2,1)S(1)}, bf16[48,512]{1,0:T(8,128)(2,1)S(1)}, bf16[48,512]{1,0:T(8,128)(2,1)S(1)}) custom-call(bf16[2048,1024]{1,0:T(8,128)(2,1)S(1)} %get-tuple-element.25.turned_ref, bf16[8,2048]{1,0:T(8,128)(2,1)S(1)} %get-tuple-element.31.mine_ref, ...), custom_call_target="tpu_custom_call" | custom-call | flops 67108864 | bytes 4194304 | tf_op jit(solution)/shard_map/backward/pallas_call | solution.py:273
  26.8 1.6 %collective-permute-start.10 = (bf16[48,512]{1,0:T(8,128)(2,1)S(1)}, bf16[48,512]{1,0:T(8,128)(2,1)S(1)}, u32[]{:S(2)}, u32[]{:S(2)}) collective-permute-start(bf16[48,512]{1,0:T(8,128)(2,1)S(1)} %get-tuple-element.41), channel_id=1, source_target_pairs={{0,8},{8,0},{16,24},{24,16},{1,9},{9,1},{17,25},{25,17},{2,10},{10... | collective-permute-start | bytes 147464 | tf_op jit(solution)/shard_map/ppermute | solution.py:24
  28.5 2.6 %collective-permute-start.11 = (bf16[48,512]{1,0:T(8,128)(2,1)S(1)}, bf16[48,512]{1,0:T(8,128)(2,1)S(1)}, u32[]{:S(2)}, u32[]{:S(2)}) collective-permute-start(bf16[48,512]{1,0:T(8,128)(2,1)S(1)} %get-tuple-element.42), channel_id=1, source_target_pairs={{0,16},{8,24},{16,0},{24,8},{1,17},{9,25},{17,1},{25,9},{2,18},{10... | collective-permute-start | bytes 147464 | tf_op jit(solution)/shard_map/ppermute | solution.py:24
  31.1 0.2 collective-permute-start.12
  31.3 0.0 collective-permute-done.10.refs_1_
  31.3 3.2 %collective-permute-done.11.refs_2_ = bf16[48,512]{1,0:T(8,128)(2,1)S(1)} collective-permute-done((bf16[48,512]{1,0:T(8,128)(2,1)S(1)}, bf16[48,512]{1,0:T(8,128)(2,1)S(1)}, u32[]{:S(2)}, u32[]{:S(2)}) %collective-permute-start.11) | collective-permute-done | bytes 49184 | tf_op jit(solution)/shard_map/ppermute | solution.py:24
  34.5 2.5 %collective-permute-done.12.refs_3_ = bf16[48,512]{1,0:T(8,128)(2,1)S(1)} collective-permute-done((bf16[48,512]{1,0:T(8,128)(2,1)S(1)}, bf16[48,512]{1,0:T(8,128)(2,1)S(1)}, u32[]{:S(2)}, u32[]{:S(2)}) %collective-permute-start.12) | collective-permute-done | bytes 49184 | tf_op jit(solution)/shard_map/ppermute | solution.py:24
  37.0 1.9 %gradient.1 = f32[1024,512]{1,0:T(8,128)} custom-call(bf16[1024,2048]{1,0:T(8,128)(2,1)S(1)} %get-tuple-element.24.unit_ref, f32[1024,1]{1,0:T(8,128)S(1)} %get-tuple-element.30.norms_ref, bf16[48,512]{1,0:T(8,128)(2,1)S(1)} %get-tuple-element.40.refs_0_, bf16[48,512]{1,0:T(8,128)(2,1)S(1)} %collective-permute-done.10.refs_1_, ...), custom_call_target="tpu_custom_call" | custom-call | flops 134217728 | bytes 4194304 | tf_op jit(solution)/shard_map/gradient/pallas_call | solution.py:334
  (10 shorter events, 0.0 us)
Async XLA Ops:
  0.6 13.4 %copy-start.1 = (f32[2048]{0:T(1024)S(1)}, f32[2048]{0:T(1024)}, u32[]{:S(2)}) copy-start(f32[2048]{0:T(1024)} %param.9) | copy-start | bytes 24580
  0.6 13.4 %copy-start.2 = (f32[1024]{0:T(1024)S(1)}, f32[1024]{0:T(1024)}, u32[]{:S(2)}) copy-start(f32[1024]{0:T(1024)} %param.8) | copy-start | bytes 12292
  0.7 1.5 %collective-permute-start.1 = (s32[2,4]{1,0:T(2,128)}, s32[2,4]{1,0:T(2,128)S(1)}, u32[]{:S(2)}, u32[]{:S(2)}) collective-permute-start(s32[2,4]{1,0:T(2,128)} %param.6), channel_id=1, source_target_pairs={{0,1},{1,0},{2,3},{3,2},{4,5},{5,4},{6,7},{7,6},{8,9},{9,8},{10,11... | collective-permute-start | bytes 104 | tf_op jit(solution)/shard_map/ppermute | solution.py:24
  1.2 1.8 %collective-permute-start = (bf16[2,2048]{1,0:T(2,128)(2,1)}, bf16[2,2048]{1,0:T(2,128)(2,1)S(1)}, u32[]{:S(2)}, u32[]{:S(2)}) collective-permute-start(bf16[2,2048]{1,0:T(2,128)(2,1)} %param.5), channel_id=1, source_target_pairs={{0,1},{1,0},{2,3},{3,2},{4,5},{5,4},{6,7},{7,6},{8,9},{9,8},{10,11... | collective-permute-start | bytes 24584 | tf_op jit(solution)/shard_map/ppermute | solution.py:24
  3.7 10.3 %collective-permute-start.4 = (bf16[4,2176]{1,0:T(4,128)(2,1)S(1)}, bf16[4,2176]{1,0:T(4,128)(2,1)S(1)}, u32[]{:S(2)}, u32[]{:S(2)}) collective-permute-start(bf16[4,2176]{1,0:T(4,128)(2,1)S(1)} %pad_maximum_fusion.after_ref.refs_0_), channel_id=1, source_target_pairs={{0,6},{1,7},{2,4},{3,5},{4,2},{5,3},{6,0},{7,1},{8,14},{9,15},{10,... | collective-permute-start | bytes 52232 | tf_op jit(solution)/shard_map/ppermute | solution.py:24
  7.5 6.5 %collective-permute-start.3 = (bf16[4,2176]{1,0:T(4,128)(2,1)S(1)}, bf16[4,2176]{1,0:T(4,128)(2,1)S(1)}, u32[]{:S(2)}, u32[]{:S(2)}) collective-permute-start(bf16[4,2176]{1,0:T(4,128)(2,1)S(1)} %pad_maximum_fusion.after_ref.refs_0_), channel_id=1, source_target_pairs={{0,4},{1,5},{2,6},{3,7},{4,0},{5,1},{6,2},{7,3},{8,12},{9,13},{10,... | collective-permute-start | bytes 52232 | tf_op jit(solution)/shard_map/ppermute | solution.py:24
  8.0 6.0 %collective-permute-start.2 = (bf16[4,2176]{1,0:T(4,128)(2,1)S(1)}, bf16[4,2176]{1,0:T(4,128)(2,1)S(1)}, u32[]{:S(2)}, u32[]{:S(2)}) collective-permute-start(bf16[4,2176]{1,0:T(4,128)(2,1)S(1)} %pad_maximum_fusion.after_ref.refs_0_), channel_id=1, source_target_pairs={{0,2},{1,3},{2,0},{3,1},{4,6},{5,7},{6,4},{7,5},{8,10},{9,11},{10,... | collective-permute-start | bytes 52232 | tf_op jit(solution)/shard_map/ppermute | solution.py:24
  8.2 2.2 %copy-start = (bf16[1024,2048]{1,0:T(8,128)(2,1)S(1)}, bf16[1024,2048]{1,0:T(8,128)(2,1)}, u32[]{:S(2)}) copy-start(bf16[1024,2048]{1,0:T(8,128)(2,1)} %weights_ref.1) | copy-start | bytes 12582916
  15.3 1.3 %collective-permute-start.5 = (f32[8,2048]{1,0:T(8,128)S(1)}, f32[8,2048]{1,0:T(8,128)S(1)}, u32[]{:S(2)}, u32[]{:S(2)}) collective-permute-start(f32[8,2048]{1,0:T(8,128)S(1)} %get-tuple-element.28), channel_id=1, source_target_pairs={{0,1},{1,0},{2,3},{3,2},{4,5},{5,4},{6,7},{7,6},{8,9},{9,8},{10,11... | collective-permute-start | bytes 196616 | tf_op jit(solution)/shard_map/ppermute | solution.py:24
  16.6 5.3 %collective-permute-start.8 = (f32[8,2048]{1,0:T(8,128)S(1)}, f32[8,2048]{1,0:T(8,128)S(1)}, u32[]{:S(2)}, u32[]{:S(2)}) collective-permute-start(f32[8,2048]{1,0:T(8,128)S(1)} %add.13.refs_0_), channel_id=1, source_target_pairs={{0,6},{1,7},{2,4},{3,5},{4,2},{5,3},{6,0},{7,1},{8,14},{9,15},{10,... | collective-permute-start | bytes 196616 | tf_op jit(solution)/shard_map/ppermute | solution.py:24
  19.5 4.3 %collective-permute-start.7 = (f32[8,2048]{1,0:T(8,128)S(1)}, f32[8,2048]{1,0:T(8,128)S(1)}, u32[]{:S(2)}, u32[]{:S(2)}) collective-permute-start(f32[8,2048]{1,0:T(8,128)S(1)} %add.13.refs_0_), channel_id=1, source_target_pairs={{0,4},{1,5},{2,6},{3,7},{4,0},{5,1},{6,2},{7,3},{8,12},{9,13},{10,... | collective-permute-start | bytes 196616 | tf_op jit(solution)/shard_map/ppermute | solution.py:24
  20.0 4.3 %collective-permute-start.6 = (f32[8,2048]{1,0:T(8,128)S(1)}, f32[8,2048]{1,0:T(8,128)S(1)}, u32[]{:S(2)}, u32[]{:S(2)}) collective-permute-start(f32[8,2048]{1,0:T(8,128)S(1)} %add.13.refs_0_), channel_id=1, source_target_pairs={{0,2},{1,3},{2,0},{3,1},{4,6},{5,7},{6,4},{7,5},{8,10},{9,11},{10,... | collective-permute-start | bytes 196616 | tf_op jit(solution)/shard_map/ppermute | solution.py:24
  24.9 1.2 %collective-permute-start.9 = (bf16[8,2048]{1,0:T(8,128)(2,1)S(1)}, bf16[8,2048]{1,0:T(8,128)(2,1)S(1)}, u32[]{:S(2)}, u32[]{:S(2)}) collective-permute-start(bf16[8,2048]{1,0:T(8,128)(2,1)S(1)} %get-tuple-element.31.mine_ref), channel_id=1, source_target_pairs={{0,1},{1,0},{2,3},{3,2},{4,5},{5,4},{6,7},{7,6},{8,9},{9,8},{10,11... | collective-permute-start | bytes 98312 | tf_op jit(solution)/shard_map/ppermute | solution.py:24
  26.8 4.5 %collective-permute-start.10 = (bf16[48,512]{1,0:T(8,128)(2,1)S(1)}, bf16[48,512]{1,0:T(8,128)(2,1)S(1)}, u32[]{:S(2)}, u32[]{:S(2)}) collective-permute-start(bf16[48,512]{1,0:T(8,128)(2,1)S(1)} %get-tuple-element.41), channel_id=1, source_target_pairs={{0,8},{8,0},{16,24},{24,16},{1,9},{9,1},{17,25},{25,17},{2,10},{10... | collective-permute-start | bytes 147464 | tf_op jit(solution)/shard_map/ppermute | solution.py:24
  28.5 6.0 %collective-permute-start.11 = (bf16[48,512]{1,0:T(8,128)(2,1)S(1)}, bf16[48,512]{1,0:T(8,128)(2,1)S(1)}, u32[]{:S(2)}, u32[]{:S(2)}) collective-permute-start(bf16[48,512]{1,0:T(8,128)(2,1)S(1)} %get-tuple-element.42), channel_id=1, source_target_pairs={{0,16},{8,24},{16,0},{24,8},{1,17},{9,25},{17,1},{25,9},{2,18},{10... | collective-permute-start | bytes 147464 | tf_op jit(solution)/shard_map/ppermute | solution.py:24
  31.1 5.9 %collective-permute-start.12 = (bf16[48,512]{1,0:T(8,128)(2,1)S(1)}, bf16[48,512]{1,0:T(8,128)(2,1)S(1)}, u32[]{:S(2)}, u32[]{:S(2)}) collective-permute-start(bf16[48,512]{1,0:T(8,128)(2,1)S(1)} %get-tuple-element.43), channel_id=1, source_target_pairs={{0,24},{8,16},{16,8},{24,0},{1,25},{9,17},{17,9},{25,1},{2,26},{10... | collective-permute-start | bytes 147464 | tf_op jit(solution)/shard_map/ppermute | solution.py:24

commit v3 on v2

--- a/solution.py
+++ b/solution.py
@@ -13,6 +13,7 @@
 LANES = 128
 DIRECT = 4
 TERMS = 8
+HEAD = 256
 VMEM = pl.BlockSpec(memory_space=pltpu.VMEM)
 HBM = pl.BlockSpec(memory_space=pltpu.MemorySpace.HBM)
 ANY = pl.BlockSpec(memory_space=pl.ANY)
@@ -32,18 +33,50 @@
     return jax.ShapeDtypeStruct(dims, dtype)
 
 
-def normalize_kernel(after_ref, weights_ref, unit_ref, turned_ref, norms_ref, held_ref, sems):
-    del after_ref
-    lat_rows, width = weights_ref.shape
+def pack_kernel(own_ref, mate_ref, names_ref, mate_names_ref, out_ref):
+    rows_dev, width = own_ref.shape
+    out_ref[:rows_dev, :width] = own_ref[...]
+    out_ref[rows_dev:, :width] = mate_ref[...]
+    lane = lax.broadcasted_iota(jnp.int32, (rows_dev, LANES), 1)
+    for at, ref in enumerate((names_ref, mate_names_ref)):
+        names = ref[...]
+        top = names.shape[1]
+        coded = jnp.zeros((rows_dev, LANES), jnp.int32)
+        for k in range(top):
+            name = names[:, k : k + 1]
+            coded = jnp.where(lane == k, name // RADIX, coded)
+            coded = jnp.where(lane == top + k, name % RADIX, coded)
+        out_ref[at * rows_dev : (at + 1) * rows_dev, width:] = coded.astype(F32).astype(BF16)
+
+
+def pack(own, mate, names, mate_names):
+    rows_dev, width = own.shape
+    return pl.pallas_call(
+        pack_kernel,
+        name="pack",
+        out_shape=shape((2 * rows_dev, width + LANES), BF16),
+        in_specs=[VMEM] * 4,
+        out_specs=VMEM,
+        compiler_params=params(4),
+    )(own, mate, names, mate_names)
+
+
+def normalize_kernel(first_row, *refs):
+    weights_ref, extra = refs[0], refs[1:3]
+    unit_ref, turned_ref, norms_ref = refs[3:6]
+    held_ref, sems = refs[-2:]
+    lat_rows, width = unit_ref.shape
     copies = []
     for at in range(lat_rows // LANES):
         rows = pl.ds(at * LANES, LANES)
-        copies.append(
-            pltpu.make_async_copy(weights_ref.at[rows], held_ref.at[rows], sems.at[at])
-        )
+        source = weights_ref.at[pl.ds(first_row + at * LANES, LANES)]
+        copies.append(pltpu.make_async_copy(source, held_ref.at[rows], sems.at[at]))
         copies[-1].start()
-    for at, copy in enumerate(copies):
-        copy.wait()
+    for ref, out in zip(extra, refs[6:-2]):
+        copies.append(pltpu.make_async_copy(ref, out, sems.at[len(copies)]))
+        copies[-1].start()
+    for at in range(lat_rows // LANES):
+        copies[at].wait()
         rows = pl.ds(at * LANES, LANES)
         squares = jnp.zeros((LANES, LANES), F32)
         for left in range(0, width, LANES):
@@ -57,47 +90,51 @@
             unit = (tile * scale).astype(BF16)
             unit_ref[rows, left : left + LANES] = unit
             turned_ref[left : left + LANES, rows] = unit.T
-
-
-def normalize(after, weights):
-    lat_rows, width = weights.shape
-    return pl.pallas_call(
-        normalize_kernel,
-        name="normalize",
-        out_shape=(
-            shape((lat_rows, width), BF16),
-            shape((width, lat_rows), BF16),
-            shape((lat_rows, 1), F32),
-        ),
-        in_specs=[ANY, HBM],
-        out_specs=(VMEM, VMEM, VMEM),
+    for copy in copies[lat_rows // LANES :]:
+        copy.wait()
+
+
+def normalize(name, weights, first_row, lat_rows, extra, brought, mib):
+    width = weights.shape[1]
+    outs = (
+        shape((lat_rows, width), BF16),
+        shape((width, lat_rows), BF16),
+        shape((lat_rows, 1), F32),
+    )
+    if brought:
+        outs += tuple(shape(x.shape, x.dtype) for x in extra)
+    return pl.pallas_call(
+        functools.partial(normalize_kernel, first_row),
+        name=name,
+        out_shape=outs,
+        in_specs=[HBM, ANY, ANY],
+        out_specs=(VMEM,) * len(outs),
         scratch_shapes=[
             pltpu.VMEM((lat_rows, width), BF16),
-            pltpu.SemaphoreType.DMA((lat_rows // LANES,)),
+            pltpu.SemaphoreType.DMA((lat_rows // LANES + 2,)),
         ],
-        compiler_params=params(20),
+        compiler_params=params(mib),
         cost_estimate=pl.CostEstimate(
             flops=4 * lat_rows * width, bytes_accessed=6 * lat_rows * width, transcendentals=0
         ),
-    )(after, weights)
-
-
-def forward_kernel(rows_dev, top, dec_ref, enc_ref, unit_ref, turned_ref, *refs):
-    chips = len(refs) - 9
+    )(weights, *extra)
+
+
+def forward_kernel(rows_dev, top, splits, dec_ref, enc_ref, *refs):
+    units, turneds, refs = refs[:splits], refs[splits : 2 * splits], refs[2 * splits :]
+    chips = len(refs) - 8
     pieces = refs[:chips]
-    keep_ref, send_ref, cent_ref, own_ref, codes_ref, base_ref, act_ref, hit_ref, rows_ref = refs[
-        chips:
-    ]
+    contrib_ref, cent_ref, input_ref, codes_ref, base_ref, act_ref, hit_ref, rows_ref = refs[chips:]
     half = chips * rows_dev
-    lat_rows, width = unit_ref.shape
+    width, lat_rows = units[0].shape[1], base_ref.shape[1]
     for k, piece in enumerate(pieces):
         value = piece[...].astype(F32)
         rows_ref[k * rows_dev : (k + 1) * rows_dev, :] = value[:rows_dev]
         rows_ref[half + k * rows_dev : half + (k + 1) * rows_dev, :] = value[rows_dev:]
-    own_ref[...] = rows_ref[:half, :width]
+    input_ref[...] = rows_ref[:, :width].astype(BF16)
     centered = (rows_ref[:, :width] - dec_ref[...]).astype(BF16)
     cent_ref[...] = centered
-    base = jnp.dot(centered, turned_ref[...], preferred_element_type=F32)
+    base = times(centered, turneds)
     base_ref[...] = base
     preact = base + enc_ref[...]
     act = jnp.maximum(preact, 0.0) + jnp.log1p(jnp.exp(-jnp.abs(preact)))
@@ -113,30 +150,38 @@
     hit_ref[...] = hit
     codes = (act * hit).astype(BF16)
     codes_ref[...] = codes
-    contrib = jnp.dot(codes, unit_ref[...], preferred_element_type=F32)
-    keep_ref[...] = contrib[:half]
-    send_ref[...] = contrib[half:]
-
-
-def forward(rows_dev, top, dec, enc, unit, turned, pieces):
-    lat_rows, width = unit.shape
-    half = len(pieces) * rows_dev
-    count = 2 * half
-    return pl.pallas_call(
-        functools.partial(forward_kernel, rows_dev, top),
+    at, contrib = 0, None
+    for unit in units:
+        part = codes[:, at : at + unit.shape[0]]
+        term = jnp.dot(part, unit[...], preferred_element_type=F32)
+        contrib = term if contrib is None else contrib + term
+        at += unit.shape[0]
+    contrib_ref[...] = contrib
+
+
+def times(x, parts):
+    return jnp.concatenate(
+        [jnp.dot(x, part[...], preferred_element_type=F32) for part in parts], axis=1
+    )
+
+
+def forward(rows_dev, top, dec, enc, units, turneds, pieces):
+    lat_rows, width = enc.shape[1], units[0].shape[1]
+    count = 2 * len(pieces) * rows_dev
+    return pl.pallas_call(
+        functools.partial(forward_kernel, rows_dev, top, len(units)),
         name="forward",
         out_shape=(
-            shape((half, width), F32),
-            shape((half, width), F32),
+            shape((count, width), F32),
             shape((count, width), BF16),
-            shape((half, width), F32),
+            shape((count, width), BF16),
             shape((count, lat_rows), BF16),
             shape((count, lat_rows), F32),
             shape((count, lat_rows), F32),
             shape((count, lat_rows), F32),
         ),
-        in_specs=[VMEM] * (4 + len(pieces)),
-        out_specs=(VMEM,) * 8,
+        in_specs=[VMEM] * (2 + 2 * len(units) + len(pieces)),
+        out_specs=(VMEM,) * 7,
         scratch_shapes=[pltpu.VMEM((count, width + LANES), F32)],
         compiler_params=params(20),
         cost_estimate=pl.CostEstimate(
@@ -144,7 +189,7 @@
             bytes_accessed=4 * lat_rows * width,
             transcendentals=2 * count * lat_rows,
         ),
-    )(dec, enc, unit, turned, *pieces)
+    )(dec, enc, *units, *turneds, *pieces)
 
 
 def side_kernel(rows_dev, act_ref, hit_ref, codes_ref, base_ref, enc_ref, *outs):
@@ -210,43 +255,57 @@
     )(act, hit, codes, base, enc)
 
 
-def errors_kernel(rows_dev, dec_ref, own_ref, *refs):
-    parts, (recon_ref, errors_ref) = refs[:-2], refs[-2:]
-    chips = len(parts)
-    total = parts[0][...]
-    for j in range(1, chips):
-        value = parts[j][...]
-        turned = [
-            value[(k ^ j) * rows_dev : ((k ^ j) + 1) * rows_dev] for k in range(chips)
-        ]
+def combine_kernel(mine_ref, mate_ref, sums_ref, sent_ref):
+    half = mine_ref.shape[0] // 2
+    for at, other in ((0, half), (half, 0)):
+        sums = mine_ref[at : at + half, :] + mate_ref[other : other + half, :]
+        sums_ref[at : at + half, :] = sums
+        sent_ref[at : at + half, :] = sums.astype(BF16)
+
+
+def combine(mine, mate):
+    return pl.pallas_call(
+        combine_kernel,
+        name="combine",
+        out_shape=(shape(mine.shape, F32), shape(mine.shape, BF16)),
+        in_specs=[VMEM] * 2,
+        out_specs=(VMEM, VMEM),
+        compiler_params=params(12),
+    )(mine, mate)
+
+
+def errors_kernel(rows_dev, dec_ref, input_ref, sums_ref, parts, recon_ref, errors_ref):
+    chips = len(parts) + 1
+    total = sums_ref[...]
+    for j, part in enumerate(parts, 1):
+        value = part[...].astype(F32)
+        turned = []
+        for k in range(2 * chips):
+            at = (k ^ j) * rows_dev
+            turned.append(value[at : at + rows_dev])
         total = total + jnp.concatenate(turned, axis=0)
     full = total + dec_ref[...]
     recon_ref[...] = full[:rows_dev].astype(BF16)
-    errors_ref[...] = (full - own_ref[...]).astype(BF16)
-
-
-def errors_of(rows_dev, dec, own, parts):
-    half, width = own.shape
-    return pl.pallas_call(
-        functools.partial(errors_kernel, rows_dev),
-        name="errors",
-        out_shape=(shape((rows_dev, width), BF16), shape((half, width), BF16)),
-        in_specs=[VMEM] * (2 + len(parts)),
-        out_specs=(VMEM, VMEM),
-        compiler_params=params(16),
-    )(dec, own, *parts)
-
-
-def backward_kernel(groups, turned_ref, mine_ref, other_ref, cent_ref, *refs):
-    codes_ref, base_ref, gate_ref, second_ref, compact_ref = refs[:5]
-    packets, errors_ref = refs[5:-1], refs[-1]
-    width, lat_rows = turned_ref.shape
-    half = mine_ref.shape[0]
-    count = 2 * half
+    errors_ref[...] = (full - input_ref[...].astype(F32)).astype(BF16)
+
+
+def backward_kernel(groups, rows_dev, splits, *refs):
+    turneds, refs = refs[:splits], refs[splits:]
+    cent_ref, codes_ref, base_ref, gate_ref = refs[:4]
+    refs = refs[4:]
+    second_ref, compact_ref = refs[:2]
+    if rows_dev:
+        chips = cent_ref.shape[0] // (2 * rows_dev)
+        dec_ref, input_ref, sums_ref = refs[2:5]
+        parts, outs = refs[5 : 4 + chips], refs[4 + chips :]
+        recon_ref, packets, errors_ref = outs[0], outs[1:-1], outs[-1]
+        errors_kernel(rows_dev, dec_ref, input_ref, sums_ref, parts, recon_ref, errors_ref)
+    else:
+        errors_ref, packets = refs[2], refs[3:]
+    count, width = cent_ref.shape
+    lat_rows = codes_ref.shape[1]
     cols = width // groups
-    errors_ref[:half, :] = mine_ref[...]
-    errors_ref[half:, :] = other_ref[...]
-    grad = jnp.dot(errors_ref[...], turned_ref[...], preferred_element_type=F32)
+    grad = times(errors_ref[...], turneds)
     pre_grad = (grad * gate_ref[...]).astype(BF16).astype(F32)
     codes = codes_ref[...].astype(F32)
     along = jnp.sum(codes * grad + pre_grad * base_ref[...], axis=0, keepdims=True)
@@ -265,26 +324,32 @@
             packet[rows, :] = terms[:, part * cols : (part + 1) * cols]
 
 
-def backward(groups, turned, mine, other, cent, codes, base, gate, second, compact):
-    width, lat_rows = turned.shape
-    count = cent.shape[0]
+def backward(groups, rows_dev, turneds, cent, rest):
+    count, width = cent.shape
+    lat_rows = rest[0].shape[1]
     cols = width // groups
     packet = shape((2 * count + TERMS * lat_rows // cols, cols), BF16)
-    return pl.pallas_call(
-        functools.partial(backward_kernel, groups),
+    outs = (packet,) * groups
+    scratch = []
+    if rows_dev:
+        outs = (shape((rows_dev, width), BF16),) + outs
+        scratch = [pltpu.VMEM((count, width), BF16)]
+    return pl.pallas_call(
+        functools.partial(backward_kernel, groups, rows_dev, len(turneds)),
         name="backward",
-        out_shape=(packet,) * groups,
-        in_specs=[VMEM] * 9,
-        out_specs=(VMEM,) * groups,
-        scratch_shapes=[pltpu.VMEM((count, width), BF16)],
+        out_shape=outs,
+        in_specs=[VMEM] * (len(turneds) + 1 + len(rest)),
+        out_specs=(VMEM,) * len(outs),
+        scratch_shapes=scratch,
         compiler_params=params(20),
         cost_estimate=pl.CostEstimate(
             flops=2 * count * lat_rows * width, bytes_accessed=2 * lat_rows * width, transcendentals=0
         ),
-    )(turned, mine, other, cent, codes, base, gate, second, compact)
-
-
-def gradient_kernel(count, unit_ref, norms_ref, *refs):
+    )(*turneds, cent, *rest)
+
+
+def gradient_kernel(count, splits, *refs):
+    units, norms, refs = refs[:splits], refs[splits : 2 * splits], refs[2 * splits :]
     out_ref, left_ref, right_ref, held_ref, sems = refs[-5:]
     packets = refs[:-5]
     lat_rows, cols = out_ref.shape
@@ -309,7 +374,10 @@
         along = along + (high + low)
     start = pl.multiple_of(lax.axis_index("dp") * cols, LANES)
     copies = []
+    which, first = 0, 0
     for at in range(lat_rows // LANES):
+        if at * LANES == first + units[which].shape[0]:
+            first, which = at * LANES, which + 1
         rows = pl.ds(at * LANES, LANES)
         outer = lax.dot_general(
             left_ref[:, rows],
@@ -318,8 +386,9 @@
             preferred_element_type=F32,
         )
         column = jnp.broadcast_to(along[:, at * LANES : (at + 1) * LANES], (LANES, LANES)).T
-        unit = unit_ref[rows, pl.ds(start, cols)].astype(F32)
-        inverse = 1.0 / norms_ref[rows, :]
+        part = pl.ds(at * LANES - first, LANES)
+        unit = units[which][part, pl.ds(start, cols)].astype(F32)
+        inverse = 1.0 / norms[which][part, :]
         held_ref[rows, :] = (outer - unit * column[:, :1]) * inverse
         copies.append(pltpu.make_async_copy(held_ref.at[rows], out_ref.at[rows], sems.at[at]))
         copies[-1].start()
@@ -327,15 +396,15 @@
         copy.wait()
 
 
-def gradient(count, unit, norms, packets):
-    lat_rows = unit.shape[0]
+def gradient(count, units, norms, packets):
+    lat_rows = sum(unit.shape[0] for unit in units)
     cols = packets[0].shape[1]
     depth = 2 * count * len(packets)
     return pl.pallas_call(
-        functools.partial(gradient_kernel, count),
+        functools.partial(gradient_kernel, count, len(units)),
         name="gradient",
         out_shape=shape((lat_rows, cols), F32),
-        in_specs=[VMEM] * (2 + len(packets)),
+        in_specs=[VMEM] * (2 * len(units) + len(packets)),
         out_specs=HBM,
         scratch_shapes=[
             pltpu.VMEM((depth, lat_rows), BF16),
@@ -347,7 +416,7 @@
         cost_estimate=pl.CostEstimate(
             flops=2 * depth * lat_rows * cols, bytes_accessed=8 * lat_rows * cols, transcendentals=0
         ),
-    )(unit, norms, *packets)
+    )(*units, *norms, *packets)
 
 
 def local(inputs, blocks, weights, enc_bias, dec_bias):
@@ -358,36 +427,37 @@
     count = 2 * chips * rows_dev
     dec, enc = dec_bias[None, :], enc_bias[None, :]
 
-    both_rows = jnp.concatenate([inputs, swap(inputs, "latent", 1)], axis=0)
-    both_names = jnp.concatenate([blocks, swap(blocks, "latent", 1)], axis=0)
-    lists = jnp.concatenate([both_names // RADIX, both_names % RADIX], axis=1).astype(BF16)
-    lists = jnp.pad(lists, ((0, 0), (0, LANES - lists.shape[1])))
-    both = jnp.concatenate([both_rows, lists], axis=1)
+    mate, mate_names = swap(inputs, "latent", 1), swap(blocks, "latent", 1)
+    *head, own, names = normalize("normalize_a", weights, 0, HEAD, (inputs, blocks), True, 50)
+    both = pack(own, mate, names, mate_names)
     pieces = [both] + [swap(both, "latent", 2 * k) for k in range(1, chips)]
-
-    unit, turned, norms = normalize(both, weights)
-    keep, send, cent, own, codes, base, act, hit = forward(
-        rows_dev, top, dec, enc, unit, turned, pieces
-    )
-    sums = keep + swap(send, "latent", 1)
+    tail = normalize(
+        "normalize_b", weights, HEAD, weights.shape[0] - HEAD, (both, names), False, 44
+    )
+    units, turneds, norms = zip(head, tail)
+    contrib, cent, rows, codes, base, act, hit = forward(
+        rows_dev, top, dec, enc, units, turneds, pieces
+    )
+    sums, sent = combine(contrib, swap(contrib, "latent", 1))
+    block_scores, gate, second, compact = side(rows_dev, act, hit, codes, base, enc)
+    known = (codes, base, gate, second, compact)
     if chips <= DIRECT:
-        parts = [sums] + [swap(sums, "latent", 2 * j) for j in range(1, chips)]
-        recon, errors = errors_of(rows_dev, dec, own, parts)
+        parts = [swap(sent, "latent", 2 * j) for j in range(1, chips)]
+        recon, *packets = backward(
+            groups, rows_dev, turneds, cent, (*known, dec, rows, sums, *parts)
+        )
     else:
         full = dec_bias + sums[:rows_dev]
         for j in range(1, chips):
             full = full + swap(sums[j * rows_dev : (j + 1) * rows_dev], "latent", 2 * j)
         recon = full.astype(BF16)
-        errors = (full - own[:rows_dev]).astype(BF16)
+        errors = (full - rows[:rows_dev].astype(F32)).astype(BF16)
         errors = [errors] + [swap(errors, "latent", 2 * j) for j in range(1, chips)]
         errors = jnp.concatenate(errors, axis=0)
-    block_scores, gate, second, compact = side(rows_dev, act, hit, codes, base, enc)
-    other = swap(errors, "latent", 1)
-    packets = backward(
-        groups, turned, errors, other, cent, codes, base, gate, second, compact
-    )
+        errors = jnp.concatenate([errors, swap(errors, "latent", 1)], axis=0)
+        packets = backward(groups, 0, turneds, cent, (*known, errors))
     packets = [swap(p, "dp", k) if k else p for k, p in enumerate(packets)]
-    grad_weights = gradient(count, unit, norms, packets)
+    grad_weights = gradient(count, units, norms, packets)
     return (recon, grad_weights, block_scores)
 
 

time: 39.1 us -> 36.3 us (0.928)
  waiting for transfers between devices: 12.3 us -> 10.2 us
  Pallas kernels: 9.07 us -> 10.7 us
  other arithmetic: 1.5 us -> 0 us
  local copies, waits for them, and re-layouts: 2.2 us -> 1.39 us
    ppermute x13 -> x12, waiting for transfers between devices: 12.3 us -> 10.2 us  [swap(): return lax.ppermute(x, axis, [(i, i ^ mask) for i in range(size)])]
    pallas_call x5 -> x7, Pallas kernels: 8.1 us -> 9.7 us  [the longest x2 5.29 us: normalize(): pl.pallas_call(functools.partial(normalize_kernel, first_row), name=name,...]
    unnamed x6 -> x8, local copies, waits for them, and re-layouts: 2.2 us -> 1.39 us
    concatenate x2 -> x0, other arithmetic: 0.8 us -> none  [the longest x1 0.72 us: local(): both = jnp.concatenate([both_rows, lists], axis=1)]
    another operation x1 -> x0, other arithmetic: 0.7 us -> none
    ppermute x13 -> x12, starting transfers between devices: 13.1 us -> 13.1 us  [swap(): return lax.ppermute(x, axis, [(i, i ^ mask) for i in range(size)])]
  transfers between devices with their start and end apart: 13 -> 12, of which waited for: 8 -> 7; matrix products, arithmetic and copies ran while one was open for 2% -> 0% of each run, Pallas kernels for 12% -> 17%
where the time goes in v3:
time: 36.3 us; the launch traced here: 36.1 us
  starting transfers between devices  13.1 us (36%)
  Pallas kernels  10.7 us (29%)
  waiting for transfers between devices  10.2 us (28%)
  local copies, waits for them, and re-layouts  1.39 us (4%)
  between operations  0.72 us (2%)
    ppermute x12, starting transfers between devices, swap(): return lax.ppermute(x, axis, [(i, i ^ mask) for i in range(size)])  13.1 us
    ppermute x12, waiting for transfers between devices, swap(): return lax.ppermute(x, axis, [(i, i ^ mask) for i in range(size)])  10.2 us
    pallas_call x2, Pallas kernels, normalize(): pl.pallas_call(functools.partial(normalize_kernel, first_row), name=name,...  5.29 us
    pallas_call x1, Pallas kernels, gradient(): pl.pallas_call(functools.partial(gradient_kernel, count, len(units)), nam...  1.85 us
    unnamed x8, local copies, waits for them, and re-layouts  1.39 us
    pallas_call x1, Pallas kernels, forward(): pl.pallas_call(functools.partial(forward_kernel, rows_dev, top, len(units...  1.29 us
    pallas_call x1, Pallas kernels, backward(): pl.pallas_call(functools.partial(backward_kernel, groups, rows_dev, len(t...  1.16 us
    pallas_call x1, Pallas kernels, side(): pl.pallas_call(functools.partial(side_kernel, rows_dev), name='side', out...  0.97 us
  transfers between devices with their start and end apart: 12, of which 7 were waited for; matrix products, arithmetic and copies ran while one was open for 0% of the time, Pallas kernels for 17%

profile of v3, /device:TPU:0, one launch (start us, length us, event | category | flops | bytes accessed | tf_op | source)
XLA Modules:
  0.0 36.1 jit_solution(11019112955898619370)
XLA Ops:
  0.6 0.5 %collective-permute-start = (bf16[2,2048]{1,0:T(2,128)(2,1)}, bf16[2,2048]{1,0:T(2,128)(2,1)S(1)}, u32[]{:S(2)}, u32[]{:S(2)}) collective-permute-start(bf16[2,2048]{1,0:T(2,128)(2,1)} %refs_1_.1), channel_id=1, source_target_pairs={{0,1},{1,0},{2,3},{3,2},{4,5},{5,4},{6,7},{7,6},{8,9},{9,8},{10,11... | collective-permute-start | bytes 24584 | tf_op jit(solution)/shard_map/ppermute | solution.py:25
  1.1 0.1 collective-permute-start.1
  1.2 0.7 %copy-done.2 = bf16[2,2048]{1,0:T(2,128)(2,1)S(1)} copy-done((bf16[2,2048]{1,0:T(2,128)(2,1)S(1)}, bf16[2,2048]{1,0:T(2,128)(2,1)}, u32[]{:S(2)}) %copy-start.2) | copy-done | bytes 8216
  1.9 0.7 %copy-done.3 = s32[2,4]{1,0:T(2,128)S(1)} copy-done((s32[2,4]{1,0:T(2,128)S(1)}, s32[2,4]{1,0:T(2,128)}, u32[]{:S(2)}) %copy-start.3) | copy-done | bytes 56
  2.6 1.9 %normalize_a.1 = (bf16[256,2048]{1,0:T(8,128)(2,1)S(1)}, bf16[2048,256]{1,0:T(8,128)(2,1)S(1)}, f32[256,1]{1,0:T(8,128)S(1)}, bf16[2,2048]{1,0:T(2,128)(2,1)S(1)}, s32[2,4]{1,0:T(2,128)S(1)}) custom-call(bf16[1024,2048]{1,0:T(8,128)(2,1)} %refs_0_.3, bf16[2,2048]{1,0:T(2,128)(2,1)S(1)} %copy-done.2, s32[2,4]{1,0:T(2,128)S(1)} %copy-done.3), custom_call_target="tpu_custom_call" | custom-call | flops 2097152 | bytes 3145728 | tf_op jit(solution)/shard_map/normalize_a/pallas_call | solution.py:106
  4.5 0.0 copy-start
  4.5 0.0 copy-start.1
  4.5 0.0 collective-permute-done.1.mate_names_ref
  4.5 0.1 pack.1.refs_1_.refs_4_
  4.6 3.9 %collective-permute-start.4 = (bf16[4,2176]{1,0:T(4,128)(2,1)S(1)}, bf16[4,2176]{1,0:T(4,128)(2,1)S(1)}, u32[]{:S(2)}, u32[]{:S(2)}) collective-permute-start(bf16[4,2176]{1,0:T(4,128)(2,1)S(1)} %pack.1.refs_1_.refs_4_), channel_id=1, source_target_pairs={{0,6},{1,7},{2,4},{3,5},{4,2},{5,3},{6,0},{7,1},{8,14},{9,15},{10,... | collective-permute-start | bytes 52232 | tf_op jit(solution)/shard_map/ppermute | solution.py:25
  8.5 0.5 %collective-permute-start.3 = (bf16[4,2176]{1,0:T(4,128)(2,1)S(1)}, bf16[4,2176]{1,0:T(4,128)(2,1)S(1)}, u32[]{:S(2)}, u32[]{:S(2)}) collective-permute-start(bf16[4,2176]{1,0:T(4,128)(2,1)S(1)} %pack.1.refs_1_.refs_4_), channel_id=1, source_target_pairs={{0,4},{1,5},{2,6},{3,7},{4,0},{5,1},{6,2},{7,3},{8,12},{9,13},{10,... | collective-permute-start | bytes 52232 | tf_op jit(solution)/shard_map/ppermute | solution.py:25
  9.1 0.1 collective-permute-start.2
  9.2 3.4 %normalize_b.1 = (bf16[768,2048]{1,0:T(8,128)(2,1)S(1)}, bf16[2048,768]{1,0:T(8,128)(2,1)S(1)}, f32[768,1]{1,0:T(8,128)S(1)}) custom-call(bf16[1024,2048]{1,0:T(8,128)(2,1)} %refs_0_.3, bf16[4,2176]{1,0:T(4,128)(2,1)S(1)} %pack.1.refs_1_.refs_4_, s32[2,4]{1,0:T(2,128)S(1)} %get-tuple-element.31.names_ref.refs_2_), custom_call_target="tpu_custom_call" | custom-call | flops 6291456 | bytes 9437184 | tf_op jit(solution)/shard_map/normalize_b/pallas_call | solution.py:106
  12.6 0.0 collective-permute-done.3.refs_6_
  12.7 0.2 collective-permute-done.2.refs_5_
  12.8 1.3 %forward.1 = (f32[16,2048]{1,0:T(8,128)S(1)}, bf16[16,2048]{1,0:T(8,128)(2,1)S(1)}, bf16[16,2048]{1,0:T(8,128)(2,1)S(1)}, bf16[16,1024]{1,0:T(8,128)(2,1)S(1)}, ...) custom-call(f32[1,2048]{1,0:T(1,128)S(1)} %bitcast.2, f32[1,1024]{1,0:T(1,128)S(1)} %bitcast.4, ...), custom_call_target="tpu_custom_call" | custom-call | flops 134217728 | bytes 8388608 | tf_op jit(solution)/shard_map/forward/pallas_call | solution.py:171
  14.1 0.0 collective-permute-start.5
  14.1 1.3 %collective-permute-done.5.mate_ref = f32[16,2048]{1,0:T(8,128)S(1)} collective-permute-done((f32[16,2048]{1,0:T(8,128)S(1)}, f32[16,2048]{1,0:T(8,128)S(1)}, u32[]{:S(2)}, u32[]{:S(2)}) %collective-permute-start.5) | collective-permute-done | bytes 131104 | tf_op jit(solution)/shard_map/ppermute | solution.py:25
  15.5 2.8 %collective-permute-start.8 = (bf16[16,2048]{1,0:T(8,128)(2,1)S(1)}, bf16[16,2048]{1,0:T(8,128)(2,1)S(1)}, u32[]{:S(2)}, u32[]{:S(2)}) collective-permute-start(bf16[16,2048]{1,0:T(8,128)(2,1)S(1)} %get-tuple-element.46), channel_id=1, source_target_pairs={{0,6},{1,7},{2,4},{3,5},{4,2},{5,3},{6,0},{7,1},{8,14},{9,15},{10,... | collective-permute-start | bytes 196616 | tf_op jit(solution)/shard_map/ppermute | solution.py:25
  18.3 0.5 %collective-permute-start.7 = (bf16[16,2048]{1,0:T(8,128)(2,1)S(1)}, bf16[16,2048]{1,0:T(8,128)(2,1)S(1)}, u32[]{:S(2)}, u32[]{:S(2)}) collective-permute-start(bf16[16,2048]{1,0:T(8,128)(2,1)S(1)} %get-tuple-element.46), channel_id=1, source_target_pairs={{0,4},{1,5},{2,6},{3,7},{4,0},{5,1},{6,2},{7,3},{8,12},{9,13},{10,... | collective-permute-start | bytes 196616 | tf_op jit(solution)/shard_map/ppermute | solution.py:25
  18.8 0.3 collective-permute-start.6
  19.0 1.0 %side.1 = (f32[16,16]{1,0:T(8,128)}, f32[16,1024]{1,0:T(8,128)S(1)}, f32[16,1024]{1,0:T(8,128)S(1)}, f32[4,1024]{1,0:T(4,128)S(1)}) custom-call(f32[16,1024]{1,0:T(8,128)S(1)} %get-tuple-element.38.act_ref, f32[16,1024]{1,0:T(8,128)S(1)} %get-tuple-element.39.hit_ref, bf16[16,1024]{1,0:T(8,128)(2,1)S(1)} %get-tuple-element.36.codes_ref.refs_3_, ...), custom_call_target="tpu_custom_call" | custom-call | flops 8388608 | bytes 524288 | tf_op jit(solution)/shard_map/side/pallas_call | solution.py:240
  20.0 0.7 %collective-permute-done.8.refs_13_ = bf16[16,2048]{1,0:T(8,128)(2,1)S(1)} collective-permute-done((bf16[16,2048]{1,0:T(8,128)(2,1)S(1)}, bf16[16,2048]{1,0:T(8,128)(2,1)S(1)}, u32[]{:S(2)}, u32[]{:S(2)}) %collective-permute-start.8) | collective-permute-done | bytes 65568 | tf_op jit(solution)/shard_map/ppermute | solution.py:25
  20.7 1.8 %collective-permute-done.7.refs_12_ = bf16[16,2048]{1,0:T(8,128)(2,1)S(1)} collective-permute-done((bf16[16,2048]{1,0:T(8,128)(2,1)S(1)}, bf16[16,2048]{1,0:T(8,128)(2,1)S(1)}, u32[]{:S(2)}, u32[]{:S(2)}) %collective-permute-start.7) | collective-permute-done | bytes 65568 | tf_op jit(solution)/shard_map/ppermute | solution.py:25
  22.5 0.5 %collective-permute-done.6.refs_11_ = bf16[16,2048]{1,0:T(8,128)(2,1)S(1)} collective-permute-done((bf16[16,2048]{1,0:T(8,128)(2,1)S(1)}, bf16[16,2048]{1,0:T(8,128)(2,1)S(1)}, u32[]{:S(2)}, u32[]{:S(2)}) %collective-permute-start.6) | collective-permute-done | bytes 65568 | tf_op jit(solution)/shard_map/ppermute | solution.py:25
  23.0 1.2 %backward.1 = (bf16[2,2048]{1,0:T(2,128)(2,1)}, bf16[48,512]{1,0:T(8,128)(2,1)S(1)}, bf16[48,512]{1,0:T(8,128)(2,1)S(1)}, bf16[48,512]{1,0:T(8,128)(2,1)S(1)}, bf16[48,512]{1,0:T(8,128)(2,1)S(1)}) custom-call(bf16[2048,256]{1,0:T(8,128)(2,1)S(1)} %get-tuple-element.29.refs_2_.refs_0_, bf16[2048,768]{1,0:T(8,128)(2,1)S(1)} %get-tuple-element.32.refs_3_.refs_1_, ...), custom_call_target="tpu_custom_call" | custom-call | flops 67108864 | bytes 4194304 | tf_op jit(solution)/shard_map/backward/pallas_call | solution.py:337
  24.2 1.6 %collective-permute-start.9 = (bf16[48,512]{1,0:T(8,128)(2,1)S(1)}, bf16[48,512]{1,0:T(8,128)(2,1)S(1)}, u32[]{:S(2)}, u32[]{:S(2)}) collective-permute-start(bf16[48,512]{1,0:T(8,128)(2,1)S(1)} %get-tuple-element.51), channel_id=1, source_target_pairs={{0,8},{8,0},{16,24},{24,16},{1,9},{9,1},{17,25},{25,17},{2,10},{10... | collective-permute-start | bytes 147464 | tf_op jit(solution)/shard_map/ppermute | solution.py:25
  25.8 2.6 %collective-permute-start.10 = (bf16[48,512]{1,0:T(8,128)(2,1)S(1)}, bf16[48,512]{1,0:T(8,128)(2,1)S(1)}, u32[]{:S(2)}, u32[]{:S(2)}) collective-permute-start(bf16[48,512]{1,0:T(8,128)(2,1)S(1)} %get-tuple-element.52), channel_id=1, source_target_pairs={{0,16},{8,24},{16,0},{24,8},{1,17},{9,25},{17,1},{25,9},{2,18},{10... | collective-permute-start | bytes 147464 | tf_op jit(solution)/shard_map/ppermute | solution.py:25
  28.4 0.2 collective-permute-start.11
  28.6 3.2 %collective-permute-done.10.refs_6_ = bf16[48,512]{1,0:T(8,128)(2,1)S(1)} collective-permute-done((bf16[48,512]{1,0:T(8,128)(2,1)S(1)}, bf16[48,512]{1,0:T(8,128)(2,1)S(1)}, u32[]{:S(2)}, u32[]{:S(2)}) %collective-permute-start.10) | collective-permute-done | bytes 49184 | tf_op jit(solution)/shard_map/ppermute | solution.py:25
  31.8 2.4 %collective-permute-done.11.refs_7_ = bf16[48,512]{1,0:T(8,128)(2,1)S(1)} collective-permute-done((bf16[48,512]{1,0:T(8,128)(2,1)S(1)}, bf16[48,512]{1,0:T(8,128)(2,1)S(1)}, u32[]{:S(2)}, u32[]{:S(2)}) %collective-permute-start.11) | collective-permute-done | bytes 49184 | tf_op jit(solution)/shard_map/ppermute | solution.py:25
  34.3 1.9 %gradient.1 = f32[1024,512]{1,0:T(8,128)} custom-call(bf16[256,2048]{1,0:T(8,128)(2,1)S(1)} %get-tuple-element.33.refs_0_, bf16[768,2048]{1,0:T(8,128)(2,1)S(1)} %get-tuple-element.34.refs_1_, f32[256,1]{1,0:T(8,128)S(1)} %get-tuple-element.48.refs_2_, f32[768,1]{1,0:T(8,128)S(1)} %get-tuple-element.49.refs_3_, ...), custom_call_target="tpu_custom_call" | custom-call | flops 134217728 | bytes 4194304 | tf_op jit(solution)/shard_map/gradient/pallas_call | solution.py:403
  (8 shorter events, 0.0 us)
Async XLA Ops:
  0.6 3.9 %collective-permute-start = (bf16[2,2048]{1,0:T(2,128)(2,1)}, bf16[2,2048]{1,0:T(2,128)(2,1)S(1)}, u32[]{:S(2)}, u32[]{:S(2)}) collective-permute-start(bf16[2,2048]{1,0:T(2,128)(2,1)} %refs_1_.1), channel_id=1, source_target_pairs={{0,1},{1,0},{2,3},{3,2},{4,5},{5,4},{6,7},{7,6},{8,9},{9,8},{10,11... | collective-permute-start | bytes 24584 | tf_op jit(solution)/shard_map/ppermute | solution.py:25
  1.1 3.3 %collective-permute-start.1 = (s32[2,4]{1,0:T(2,128)}, s32[2,4]{1,0:T(2,128)S(1)}, u32[]{:S(2)}, u32[]{:S(2)}) collective-permute-start(s32[2,4]{1,0:T(2,128)} %refs_2_.1), channel_id=1, source_target_pairs={{0,1},{1,0},{2,3},{3,2},{4,5},{5,4},{6,7},{7,6},{8,9},{9,8},{10,11... | collective-permute-start | bytes 104 | tf_op jit(solution)/shard_map/ppermute | solution.py:25
  1.2 0.7 %copy-start.2 = (bf16[2,2048]{1,0:T(2,128)(2,1)S(1)}, bf16[2,2048]{1,0:T(2,128)(2,1)}, u32[]{:S(2)}) copy-start(bf16[2,2048]{1,0:T(2,128)(2,1)} %refs_1_.1) | copy-start | bytes 24580
  1.9 0.7 %copy-start.3 = (s32[2,4]{1,0:T(2,128)S(1)}, s32[2,4]{1,0:T(2,128)}, u32[]{:S(2)}) copy-start(s32[2,4]{1,0:T(2,128)} %refs_2_.1) | copy-start | bytes 100
  4.5 8.3 %copy-start = (f32[2048]{0:T(1024)S(1)}, f32[2048]{0:T(1024)}, u32[]{:S(2)}) copy-start(f32[2048]{0:T(1024)} %param.9) | copy-start | bytes 24580
  4.5 8.3 %copy-start.1 = (f32[1024]{0:T(1024)S(1)}, f32[1024]{0:T(1024)}, u32[]{:S(2)}) copy-start(f32[1024]{0:T(1024)} %param.8) | copy-start | bytes 12292
  4.6 8.0 %collective-permute-start.4 = (bf16[4,2176]{1,0:T(4,128)(2,1)S(1)}, bf16[4,2176]{1,0:T(4,128)(2,1)S(1)}, u32[]{:S(2)}, u32[]{:S(2)}) collective-permute-start(bf16[4,2176]{1,0:T(4,128)(2,1)S(1)} %pack.1.refs_1_.refs_4_), channel_id=1, source_target_pairs={{0,6},{1,7},{2,4},{3,5},{4,2},{5,3},{6,0},{7,1},{8,14},{9,15},{10,... | collective-permute-start | bytes 52232 | tf_op jit(solution)/shard_map/ppermute | solution.py:25
  8.5 4.1 %collective-permute-start.3 = (bf16[4,2176]{1,0:T(4,128)(2,1)S(1)}, bf16[4,2176]{1,0:T(4,128)(2,1)S(1)}, u32[]{:S(2)}, u32[]{:S(2)}) collective-permute-start(bf16[4,2176]{1,0:T(4,128)(2,1)S(1)} %pack.1.refs_1_.refs_4_), channel_id=1, source_target_pairs={{0,4},{1,5},{2,6},{3,7},{4,0},{5,1},{6,2},{7,3},{8,12},{9,13},{10,... | collective-permute-start | bytes 52232 | tf_op jit(solution)/shard_map/ppermute | solution.py:25
  9.1 3.8 %collective-permute-start.2 = (bf16[4,2176]{1,0:T(4,128)(2,1)S(1)}, bf16[4,2176]{1,0:T(4,128)(2,1)S(1)}, u32[]{:S(2)}, u32[]{:S(2)}) collective-permute-start(bf16[4,2176]{1,0:T(4,128)(2,1)S(1)} %pack.1.refs_1_.refs_4_), channel_id=1, source_target_pairs={{0,2},{1,3},{2,0},{3,1},{4,6},{5,7},{6,4},{7,5},{8,10},{9,11},{10,... | collective-permute-start | bytes 52232 | tf_op jit(solution)/shard_map/ppermute | solution.py:25
  14.1 1.4 %collective-permute-start.5 = (f32[16,2048]{1,0:T(8,128)S(1)}, f32[16,2048]{1,0:T(8,128)S(1)}, u32[]{:S(2)}, u32[]{:S(2)}) collective-permute-start(f32[16,2048]{1,0:T(8,128)S(1)} %get-tuple-element.44.mine_ref), channel_id=1, source_target_pairs={{0,1},{1,0},{2,3},{3,2},{4,5},{5,4},{6,7},{7,6},{8,9},{9,8},{10,11... | collective-permute-start | bytes 393224 | tf_op jit(solution)/shard_map/ppermute | solution.py:25
  15.5 5.2 %collective-permute-start.8 = (bf16[16,2048]{1,0:T(8,128)(2,1)S(1)}, bf16[16,2048]{1,0:T(8,128)(2,1)S(1)}, u32[]{:S(2)}, u32[]{:S(2)}) collective-permute-start(bf16[16,2048]{1,0:T(8,128)(2,1)S(1)} %get-tuple-element.46), channel_id=1, source_target_pairs={{0,6},{1,7},{2,4},{3,5},{4,2},{5,3},{6,0},{7,1},{8,14},{9,15},{10,... | collective-permute-start | bytes 196616 | tf_op jit(solution)/shard_map/ppermute | solution.py:25
  18.3 4.3 %collective-permute-start.7 = (bf16[16,2048]{1,0:T(8,128)(2,1)S(1)}, bf16[16,2048]{1,0:T(8,128)(2,1)S(1)}, u32[]{:S(2)}, u32[]{:S(2)}) collective-permute-start(bf16[16,2048]{1,0:T(8,128)(2,1)S(1)} %get-tuple-element.46), channel_id=1, source_target_pairs={{0,4},{1,5},{2,6},{3,7},{4,0},{5,1},{6,2},{7,3},{8,12},{9,13},{10,... | collective-permute-start | bytes 196616 | tf_op jit(solution)/shard_map/ppermute | solution.py:25
  18.8 4.3 %collective-permute-start.6 = (bf16[16,2048]{1,0:T(8,128)(2,1)S(1)}, bf16[16,2048]{1,0:T(8,128)(2,1)S(1)}, u32[]{:S(2)}, u32[]{:S(2)}) collective-permute-start(bf16[16,2048]{1,0:T(8,128)(2,1)S(1)} %get-tuple-element.46), channel_id=1, source_target_pairs={{0,2},{1,3},{2,0},{3,1},{4,6},{5,7},{6,4},{7,5},{8,10},{9,11},{10,... | collective-permute-start | bytes 196616 | tf_op jit(solution)/shard_map/ppermute | solution.py:25
  24.2 4.4 %collective-permute-start.9 = (bf16[48,512]{1,0:T(8,128)(2,1)S(1)}, bf16[48,512]{1,0:T(8,128)(2,1)S(1)}, u32[]{:S(2)}, u32[]{:S(2)}) collective-permute-start(bf16[48,512]{1,0:T(8,128)(2,1)S(1)} %get-tuple-element.51), channel_id=1, source_target_pairs={{0,8},{8,0},{16,24},{24,16},{1,9},{9,1},{17,25},{25,17},{2,10},{10... | collective-permute-start | bytes 147464 | tf_op jit(solution)/shard_map/ppermute | solution.py:25
  25.8 6.0 %collective-permute-start.10 = (bf16[48,512]{1,0:T(8,128)(2,1)S(1)}, bf16[48,512]{1,0:T(8,128)(2,1)S(1)}, u32[]{:S(2)}, u32[]{:S(2)}) collective-permute-start(bf16[48,512]{1,0:T(8,128)(2,1)S(1)} %get-tuple-element.52), channel_id=1, source_target_pairs={{0,16},{8,24},{16,0},{24,8},{1,17},{9,25},{17,1},{25,9},{2,18},{10... | collective-permute-start | bytes 147464 | tf_op jit(solution)/shard_map/ppermute | solution.py:25
  28.4 5.9 %collective-permute-start.11 = (bf16[48,512]{1,0:T(8,128)(2,1)S(1)}, bf16[48,512]{1,0:T(8,128)(2,1)S(1)}, u32[]{:S(2)}, u32[]{:S(2)}) collective-permute-start(bf16[48,512]{1,0:T(8,128)(2,1)S(1)} %get-tuple-element.53), channel_id=1, source_target_pairs={{0,24},{8,16},{16,8},{24,0},{1,25},{9,17},{17,9},{25,1},{2,26},{10... | collective-permute-start | bytes 147464 | tf_op jit(solution)/shard_map/ppermute | solution.py:25

commit v4 on v3

--- a/solution.py
+++ b/solution.py
@@ -13,11 +13,11 @@
 LANES = 128
 DIRECT = 4
 TERMS = 8
-HEAD = 256
 VMEM = pl.BlockSpec(memory_space=pltpu.VMEM)
 HBM = pl.BlockSpec(memory_space=pltpu.MemorySpace.HBM)
 ANY = pl.BlockSpec(memory_space=pl.ANY)
 F32, BF16 = jnp.float32, jnp.bfloat16
+COST = pl.CostEstimate(flops=2**34, bytes_accessed=16 * 2**20, transcendentals=2**24)
 
 
 def swap(x, axis, mask):
@@ -33,91 +33,93 @@
     return jax.ShapeDtypeStruct(dims, dtype)
 
 
-def pack_kernel(own_ref, mate_ref, names_ref, mate_names_ref, out_ref):
-    rows_dev, width = own_ref.shape
-    out_ref[:rows_dev, :width] = own_ref[...]
+def stage_kernel(rows_ref, names_ref, out_ref):
+    rows_dev, width = rows_ref.shape
+    lane = lax.broadcasted_iota(jnp.int32, (rows_dev, LANES), 1)
+    out_ref[:, :width] = rows_ref[...]
+    out_ref[:, width:] = coded(names_ref[...], lane).astype(F32).astype(BF16)
+
+
+def stage(rows, names):
+    rows_dev, width = rows.shape
+    return pl.pallas_call(
+        stage_kernel,
+        name="stage",
+        out_shape=shape((rows_dev, width + LANES), BF16),
+        in_specs=[VMEM] * 2,
+        out_specs=VMEM,
+        compiler_params=params(4),
+        cost_estimate=COST,
+    )(rows, names)
+
+
+def pack_kernel(own_ref, mate_ref, mate_names_ref, out_ref):
+    rows_dev, width = mate_ref.shape
+    lane = lax.broadcasted_iota(jnp.int32, (rows_dev, LANES), 1)
+    out_ref[:rows_dev, :] = own_ref[...]
     out_ref[rows_dev:, :width] = mate_ref[...]
-    lane = lax.broadcasted_iota(jnp.int32, (rows_dev, LANES), 1)
-    for at, ref in enumerate((names_ref, mate_names_ref)):
-        names = ref[...]
-        top = names.shape[1]
-        coded = jnp.zeros((rows_dev, LANES), jnp.int32)
-        for k in range(top):
-            name = names[:, k : k + 1]
-            coded = jnp.where(lane == k, name // RADIX, coded)
-            coded = jnp.where(lane == top + k, name % RADIX, coded)
-        out_ref[at * rows_dev : (at + 1) * rows_dev, width:] = coded.astype(F32).astype(BF16)
-
-
-def pack(own, mate, names, mate_names):
-    rows_dev, width = own.shape
+    out_ref[rows_dev:, width:] = coded(mate_names_ref[...], lane).astype(F32).astype(BF16)
+
+
+def coded(names, lane):
+    top = names.shape[1]
+    value = jnp.zeros(lane.shape, jnp.int32)
+    for k in range(top):
+        name = names[:, k : k + 1]
+        value = jnp.where(lane == k, name // RADIX, value)
+        value = jnp.where(lane == top + k, name % RADIX, value)
+    return value
+
+
+def pack(own, mate, mate_names):
+    rows_dev, width = mate.shape
     return pl.pallas_call(
         pack_kernel,
         name="pack",
         out_shape=shape((2 * rows_dev, width + LANES), BF16),
-        in_specs=[VMEM] * 4,
+        in_specs=[VMEM] * 3,
         out_specs=VMEM,
         compiler_params=params(4),
-    )(own, mate, names, mate_names)
-
-
-def normalize_kernel(first_row, *refs):
-    weights_ref, extra = refs[0], refs[1:3]
-    unit_ref, turned_ref, norms_ref = refs[3:6]
-    held_ref, sems = refs[-2:]
-    lat_rows, width = unit_ref.shape
-    copies = []
-    for at in range(lat_rows // LANES):
-        rows = pl.ds(at * LANES, LANES)
-        source = weights_ref.at[pl.ds(first_row + at * LANES, LANES)]
-        copies.append(pltpu.make_async_copy(source, held_ref.at[rows], sems.at[at]))
-        copies[-1].start()
-    for ref, out in zip(extra, refs[6:-2]):
-        copies.append(pltpu.make_async_copy(ref, out, sems.at[len(copies)]))
-        copies[-1].start()
-    for at in range(lat_rows // LANES):
-        copies[at].wait()
-        rows = pl.ds(at * LANES, LANES)
+        cost_estimate=COST,
+    )(own, mate, mate_names)
+
+
+def normalize_kernel(after_ref, weights_ref, unit_ref, turned_ref, norms_ref):
+    del after_ref
+    lat_rows, width = weights_ref.shape
+    for top in range(0, lat_rows, LANES):
+        rows = pl.ds(top, LANES)
         squares = jnp.zeros((LANES, LANES), F32)
         for left in range(0, width, LANES):
-            tile = held_ref[rows, left : left + LANES].astype(F32)
+            tile = weights_ref[rows, left : left + LANES].astype(F32)
             squares = squares + tile * tile
         norms = jnp.sqrt(jnp.sum(squares, axis=1, keepdims=True) + 1e-06)
         norms_ref[rows, :] = norms
         scale = jnp.broadcast_to(1.0 / norms, (LANES, LANES))
         for left in range(0, width, LANES):
-            tile = held_ref[rows, left : left + LANES].astype(F32)
+            tile = weights_ref[rows, left : left + LANES].astype(F32)
             unit = (tile * scale).astype(BF16)
             unit_ref[rows, left : left + LANES] = unit
             turned_ref[left : left + LANES, rows] = unit.T
-    for copy in copies[lat_rows // LANES :]:
-        copy.wait()
-
-
-def normalize(name, weights, first_row, lat_rows, extra, brought, mib):
-    width = weights.shape[1]
-    outs = (
-        shape((lat_rows, width), BF16),
-        shape((width, lat_rows), BF16),
-        shape((lat_rows, 1), F32),
-    )
-    if brought:
-        outs += tuple(shape(x.shape, x.dtype) for x in extra)
-    return pl.pallas_call(
-        functools.partial(normalize_kernel, first_row),
-        name=name,
-        out_shape=outs,
-        in_specs=[HBM, ANY, ANY],
-        out_specs=(VMEM,) * len(outs),
-        scratch_shapes=[
-            pltpu.VMEM((lat_rows, width), BF16),
-            pltpu.SemaphoreType.DMA((lat_rows // LANES + 2,)),
-        ],
-        compiler_params=params(mib),
+
+
+def normalize(after, weights):
+    lat_rows, width = weights.shape
+    return pl.pallas_call(
+        normalize_kernel,
+        name="normalize",
+        out_shape=(
+            shape((lat_rows, width), BF16),
+            shape((width, lat_rows), BF16),
+            shape((lat_rows, 1), F32),
+        ),
+        in_specs=[ANY, VMEM],
+        out_specs=(VMEM,) * 3,
+        compiler_params=params(20),
         cost_estimate=pl.CostEstimate(
             flops=4 * lat_rows * width, bytes_accessed=6 * lat_rows * width, transcendentals=0
         ),
-    )(weights, *extra)
+    )(after, weights)
 
 
 def forward_kernel(rows_dev, top, splits, dec_ref, enc_ref, *refs):
@@ -428,13 +430,9 @@
     dec, enc = dec_bias[None, :], enc_bias[None, :]
 
     mate, mate_names = swap(inputs, "latent", 1), swap(blocks, "latent", 1)
-    *head, own, names = normalize("normalize_a", weights, 0, HEAD, (inputs, blocks), True, 50)
-    both = pack(own, mate, names, mate_names)
+    both = pack(stage(inputs, blocks), mate, mate_names)
     pieces = [both] + [swap(both, "latent", 2 * k) for k in range(1, chips)]
-    tail = normalize(
-        "normalize_b", weights, HEAD, weights.shape[0] - HEAD, (both, names), False, 44
-    )
-    units, turneds, norms = zip(head, tail)
+    units, turneds, norms = ([x] for x in normalize(both, weights))
     contrib, cent, rows, codes, base, act, hit = forward(
         rows_dev, top, dec, enc, units, turneds, pieces
     )

time: 36.3 us -> 33.6 us (0.926)
  Pallas kernels: 10.7 us -> 7.95 us
    pallas_call x2, Pallas kernels: 5.29 us -> 2.62 us  [the longest x1 2.53 us: normalize(): pl.pallas_call(normalize_kernel, name='normalize', out_shape=(shape((lat_...]
    unnamed x8 -> x10, local copies, waits for them, and re-layouts: 1.39 us -> 1.39 us
  transfers between devices with their start and end apart: 12 -> 12, of which waited for: 7 -> 8; matrix products, arithmetic and copies ran while one was open for 0% -> 0% of each run, Pallas kernels for 17% -> 11%
where the time goes in v4:
time: 33.6 us; the launch traced here: 33.4 us
  starting transfers between devices  13.1 us (39%)
  waiting for transfers between devices  10.3 us (31%)
  Pallas kernels  7.95 us (24%)
  local copies, waits for them, and re-layouts  1.39 us (4%)
  between operations  0.7 us (2%)
    ppermute x12, starting transfers between devices, swap(): return lax.ppermute(x, axis, [(i, i ^ mask) for i in range(size)])  13.1 us
    ppermute x12, waiting for transfers between devices, swap(): return lax.ppermute(x, axis, [(i, i ^ mask) for i in range(size)])  10.3 us
    pallas_call x1, Pallas kernels, normalize(): pl.pallas_call(normalize_kernel, name='normalize', out_shape=(shape((lat_...  2.53 us
    pallas_call x1, Pallas kernels, gradient(): pl.pallas_call(functools.partial(gradient_kernel, count, len(units)), nam...  1.85 us
    unnamed x10, local copies, waits for them, and re-layouts  1.39 us
    pallas_call x1, Pallas kernels, forward(): pl.pallas_call(functools.partial(forward_kernel, rows_dev, top, len(units...  1.26 us
    pallas_call x1, Pallas kernels, backward(): pl.pallas_call(functools.partial(backward_kernel, groups, rows_dev, len(t...  1.15 us
    pallas_call x1, Pallas kernels, side(): pl.pallas_call(functools.partial(side_kernel, rows_dev), name='side', out...  0.97 us
  transfers between devices with their start and end apart: 12, of which 8 were waited for; matrix products, arithmetic and copies ran while one was open for 0% of the time, Pallas kernels for 11%

profile of v4, /device:TPU:0, one launch (start us, length us, event | category | flops | bytes accessed | tf_op | source)
XLA Modules:
  0.0 33.4 jit_solution(2321167325856084859)
XLA Ops:
  0.6 0.5 %collective-permute-start.1 = (s32[2,4]{1,0:T(2,128)}, s32[2,4]{1,0:T(2,128)S(1)}, u32[]{:S(2)}, u32[]{:S(2)}) collective-permute-start(s32[2,4]{1,0:T(2,128)} %names_ref.1), channel_id=1, source_target_pairs={{0,1},{1,0},{2,3},{3,2},{4,5},{5,4},{6,7},{7,6},{8,9},{9,8},{10,11... | collective-permute-start | bytes 104 | tf_op jit(solution)/shard_map/ppermute | solution.py:25
  1.1 0.1 collective-permute-start
  1.2 0.7 %copy-done.3 = bf16[2,2048]{1,0:T(2,128)(2,1)S(1)} copy-done((bf16[2,2048]{1,0:T(2,128)(2,1)S(1)}, bf16[2,2048]{1,0:T(2,128)(2,1)}, u32[]{:S(2)}) %copy-start.3) | copy-done | bytes 8216
  1.9 0.7 %copy-done.4 = s32[2,4]{1,0:T(2,128)S(1)} copy-done((s32[2,4]{1,0:T(2,128)S(1)}, s32[2,4]{1,0:T(2,128)}, u32[]{:S(2)}) %copy-start.4) | copy-done | bytes 56
  2.6 0.1 stage.1.own_ref
  2.7 0.0 collective-permute-done.1.mate_names_ref
  2.7 0.0 collective-permute-done.mate_ref
  2.7 0.1 pack.1.after_ref.refs_2_
  2.8 0.0 copy-start.2
  2.8 3.9 %collective-permute-start.4 = (bf16[4,2176]{1,0:T(4,128)(2,1)S(1)}, bf16[4,2176]{1,0:T(4,128)(2,1)S(1)}, u32[]{:S(2)}, u32[]{:S(2)}) collective-permute-start(bf16[4,2176]{1,0:T(4,128)(2,1)S(1)} %pack.1.after_ref.refs_2_), channel_id=1, source_target_pairs={{0,6},{1,7},{2,4},{3,5},{4,2},{5,3},{6,0},{7,1},{8,14},{9,15},{10,... | collective-permute-start | bytes 52232 | tf_op jit(solution)/shard_map/ppermute | solution.py:25
  6.8 0.5 %collective-permute-start.3 = (bf16[4,2176]{1,0:T(4,128)(2,1)S(1)}, bf16[4,2176]{1,0:T(4,128)(2,1)S(1)}, u32[]{:S(2)}, u32[]{:S(2)}) collective-permute-start(bf16[4,2176]{1,0:T(4,128)(2,1)S(1)} %pack.1.after_ref.refs_2_), channel_id=1, source_target_pairs={{0,4},{1,5},{2,6},{3,7},{4,0},{5,1},{6,2},{7,3},{8,12},{9,13},{10,... | collective-permute-start | bytes 52232 | tf_op jit(solution)/shard_map/ppermute | solution.py:25
  7.3 0.1 collective-permute-start.2
  7.4 2.5 %normalize.1 = (bf16[1024,2048]{1,0:T(8,128)(2,1)S(1)}, bf16[2048,1024]{1,0:T(8,128)(2,1)S(1)}, f32[1024,1]{1,0:T(8,128)S(1)}) custom-call(bf16[4,2176]{1,0:T(4,128)(2,1)S(1)} %pack.1.after_ref.refs_2_, bf16[1024,2048]{1,0:T(8,128)(2,1)S(1)} %copy-done), custom_call_target="tpu_custom_call" | custom-call | flops 8388608 | bytes 12582912 | tf_op jit(solution)/shard_map/normalize/pallas_call | solution.py:108
  10.0 0.6 %collective-permute-done.3.refs_4_ = bf16[4,2176]{1,0:T(4,128)(2,1)S(1)} collective-permute-done((bf16[4,2176]{1,0:T(4,128)(2,1)S(1)}, bf16[4,2176]{1,0:T(4,128)(2,1)S(1)}, u32[]{:S(2)}, u32[]{:S(2)}) %collective-permute-start.3) | collective-permute-done | bytes 17440 | tf_op jit(solution)/shard_map/ppermute | solution.py:25
  10.5 0.5 %collective-permute-done.2.refs_3_ = bf16[4,2176]{1,0:T(4,128)(2,1)S(1)} collective-permute-done((bf16[4,2176]{1,0:T(4,128)(2,1)S(1)}, bf16[4,2176]{1,0:T(4,128)(2,1)S(1)}, u32[]{:S(2)}, u32[]{:S(2)}) %collective-permute-start.2) | collective-permute-done | bytes 17440 | tf_op jit(solution)/shard_map/ppermute | solution.py:25
  11.0 1.3 %forward.1 = (f32[16,2048]{1,0:T(8,128)S(1)}, bf16[16,2048]{1,0:T(8,128)(2,1)S(1)}, bf16[16,2048]{1,0:T(8,128)(2,1)S(1)}, bf16[16,1024]{1,0:T(8,128)(2,1)S(1)}, ...) custom-call(f32[1,2048]{1,0:T(1,128)S(1)} %bitcast.2, f32[1,1024]{1,0:T(1,128)S(1)} %bitcast.4, ...), custom_call_target="tpu_custom_call" | custom-call | flops 134217728 | bytes 8388608 | tf_op jit(solution)/shard_map/forward/pallas_call | solution.py:173
  12.3 0.0 collective-permute-start.5
  12.3 1.4 %collective-permute-done.5.mate_ref = f32[16,2048]{1,0:T(8,128)S(1)} collective-permute-done((f32[16,2048]{1,0:T(8,128)S(1)}, f32[16,2048]{1,0:T(8,128)S(1)}, u32[]{:S(2)}, u32[]{:S(2)}) %collective-permute-start.5) | collective-permute-done | bytes 131104 | tf_op jit(solution)/shard_map/ppermute | solution.py:25
  13.7 1.9 %collective-permute-start.8 = (bf16[16,2048]{1,0:T(8,128)(2,1)S(1)}, bf16[16,2048]{1,0:T(8,128)(2,1)S(1)}, u32[]{:S(2)}, u32[]{:S(2)}) collective-permute-start(bf16[16,2048]{1,0:T(8,128)(2,1)S(1)} %get-tuple-element.37), channel_id=1, source_target_pairs={{0,6},{1,7},{2,4},{3,5},{4,2},{5,3},{6,0},{7,1},{8,14},{9,15},{10,... | collective-permute-start | bytes 196616 | tf_op jit(solution)/shard_map/ppermute | solution.py:25
  15.6 0.5 %collective-permute-start.7 = (bf16[16,2048]{1,0:T(8,128)(2,1)S(1)}, bf16[16,2048]{1,0:T(8,128)(2,1)S(1)}, u32[]{:S(2)}, u32[]{:S(2)}) collective-permute-start(bf16[16,2048]{1,0:T(8,128)(2,1)S(1)} %get-tuple-element.37), channel_id=1, source_target_pairs={{0,4},{1,5},{2,6},{3,7},{4,0},{5,1},{6,2},{7,3},{8,12},{9,13},{10,... | collective-permute-start | bytes 196616 | tf_op jit(solution)/shard_map/ppermute | solution.py:25
  16.1 1.2 %collective-permute-start.6 = (bf16[16,2048]{1,0:T(8,128)(2,1)S(1)}, bf16[16,2048]{1,0:T(8,128)(2,1)S(1)}, u32[]{:S(2)}, u32[]{:S(2)}) collective-permute-start(bf16[16,2048]{1,0:T(8,128)(2,1)S(1)} %get-tuple-element.37), channel_id=1, source_target_pairs={{0,2},{1,3},{2,0},{3,1},{4,6},{5,7},{6,4},{7,5},{8,10},{9,11},{10,... | collective-permute-start | bytes 196616 | tf_op jit(solution)/shard_map/ppermute | solution.py:25
  17.2 1.0 %side.1 = (f32[16,16]{1,0:T(8,128)}, f32[16,1024]{1,0:T(8,128)S(1)}, f32[16,1024]{1,0:T(8,128)S(1)}, f32[4,1024]{1,0:T(4,128)S(1)}) custom-call(f32[16,1024]{1,0:T(8,128)S(1)} %get-tuple-element.29.act_ref, f32[16,1024]{1,0:T(8,128)S(1)} %get-tuple-element.30.hit_ref, bf16[16,1024]{1,0:T(8,128)(2,1)S(1)} %get-tuple-element.27.codes_ref.refs_2_, ...), custom_call_target="tpu_custom_call" | custom-call | flops 8388608 | bytes 524288 | tf_op jit(solution)/shard_map/side/pallas_call | solution.py:242
  18.2 0.8 %collective-permute-done.8.refs_12_ = bf16[16,2048]{1,0:T(8,128)(2,1)S(1)} collective-permute-done((bf16[16,2048]{1,0:T(8,128)(2,1)S(1)}, bf16[16,2048]{1,0:T(8,128)(2,1)S(1)}, u32[]{:S(2)}, u32[]{:S(2)}) %collective-permute-start.8) | collective-permute-done | bytes 65568 | tf_op jit(solution)/shard_map/ppermute | solution.py:25
  18.9 1.2 %collective-permute-done.7.refs_11_ = bf16[16,2048]{1,0:T(8,128)(2,1)S(1)} collective-permute-done((bf16[16,2048]{1,0:T(8,128)(2,1)S(1)}, bf16[16,2048]{1,0:T(8,128)(2,1)S(1)}, u32[]{:S(2)}, u32[]{:S(2)}) %collective-permute-start.7) | collective-permute-done | bytes 65568 | tf_op jit(solution)/shard_map/ppermute | solution.py:25
  20.2 0.2 collective-permute-done.6.refs_10_
  20.3 1.2 %backward.1 = (bf16[2,2048]{1,0:T(2,128)(2,1)}, bf16[48,512]{1,0:T(8,128)(2,1)S(1)}, bf16[48,512]{1,0:T(8,128)(2,1)S(1)}, bf16[48,512]{1,0:T(8,128)(2,1)S(1)}, bf16[48,512]{1,0:T(8,128)(2,1)S(1)}) custom-call(bf16[2048,1024]{1,0:T(8,128)(2,1)S(1)} %get-tuple-element.24.refs_1_.refs_0_, bf16[16,2048]{1,0:T(8,128)(2,1)S(1)} %get-tuple-element.26.refs_1_, ...), custom_call_target="tpu_custom_call" | custom-call | flops 67108864 | bytes 4194304 | tf_op jit(solution)/shard_map/backward/pallas_call | solution.py:339
  21.5 1.6 %collective-permute-start.9 = (bf16[48,512]{1,0:T(8,128)(2,1)S(1)}, bf16[48,512]{1,0:T(8,128)(2,1)S(1)}, u32[]{:S(2)}, u32[]{:S(2)}) collective-permute-start(bf16[48,512]{1,0:T(8,128)(2,1)S(1)} %get-tuple-element.41), channel_id=1, source_target_pairs={{0,8},{8,0},{16,24},{24,16},{1,9},{9,1},{17,25},{25,17},{2,10},{10... | collective-permute-start | bytes 147464 | tf_op jit(solution)/shard_map/ppermute | solution.py:25
  23.1 2.6 %collective-permute-start.10 = (bf16[48,512]{1,0:T(8,128)(2,1)S(1)}, bf16[48,512]{1,0:T(8,128)(2,1)S(1)}, u32[]{:S(2)}, u32[]{:S(2)}) collective-permute-start(bf16[48,512]{1,0:T(8,128)(2,1)S(1)} %get-tuple-element.42), channel_id=1, source_target_pairs={{0,16},{8,24},{16,0},{24,8},{1,17},{9,25},{17,1},{25,9},{2,18},{10... | collective-permute-start | bytes 147464 | tf_op jit(solution)/shard_map/ppermute | solution.py:25
  25.7 0.2 collective-permute-start.11
  25.9 2.9 %collective-permute-done.10.refs_4_ = bf16[48,512]{1,0:T(8,128)(2,1)S(1)} collective-permute-done((bf16[48,512]{1,0:T(8,128)(2,1)S(1)}, bf16[48,512]{1,0:T(8,128)(2,1)S(1)}, u32[]{:S(2)}, u32[]{:S(2)}) %collective-permute-start.10) | collective-permute-done | bytes 49184 | tf_op jit(solution)/shard_map/ppermute | solution.py:25
  28.8 2.8 %collective-permute-done.11.refs_5_ = bf16[48,512]{1,0:T(8,128)(2,1)S(1)} collective-permute-done((bf16[48,512]{1,0:T(8,128)(2,1)S(1)}, bf16[48,512]{1,0:T(8,128)(2,1)S(1)}, u32[]{:S(2)}, u32[]{:S(2)}) %collective-permute-start.11) | collective-permute-done | bytes 49184 | tf_op jit(solution)/shard_map/ppermute | solution.py:25
  31.6 1.9 %gradient.1 = f32[1024,512]{1,0:T(8,128)} custom-call(bf16[1024,2048]{1,0:T(8,128)(2,1)S(1)} %get-tuple-element.25.refs_0_, f32[1024,1]{1,0:T(8,128)S(1)} %get-tuple-element.39.refs_1_, bf16[48,512]{1,0:T(8,128)(2,1)S(1)} %get-tuple-element.40.refs_2_, bf16[48,512]{1,0:T(8,128)(2,1)S(1)} %collective-permute-done.9.refs_3_, ...), custom_call_target="tpu_custom_call" | custom-call | flops 134217728 | bytes 4194304 | tf_op jit(solution)/shard_map/gradient/pallas_call | solution.py:405
  (10 shorter events, 0.0 us)
Async XLA Ops:
  0.6 2.1 %collective-permute-start.1 = (s32[2,4]{1,0:T(2,128)}, s32[2,4]{1,0:T(2,128)S(1)}, u32[]{:S(2)}, u32[]{:S(2)}) collective-permute-start(s32[2,4]{1,0:T(2,128)} %names_ref.1), channel_id=1, source_target_pairs={{0,1},{1,0},{2,3},{3,2},{4,5},{5,4},{6,7},{7,6},{8,9},{9,8},{10,11... | collective-permute-start | bytes 104 | tf_op jit(solution)/shard_map/ppermute | solution.py:25
  1.1 1.6 %collective-permute-start = (bf16[2,2048]{1,0:T(2,128)(2,1)}, bf16[2,2048]{1,0:T(2,128)(2,1)S(1)}, u32[]{:S(2)}, u32[]{:S(2)}) collective-permute-start(bf16[2,2048]{1,0:T(2,128)(2,1)} %rows_ref.1), channel_id=1, source_target_pairs={{0,1},{1,0},{2,3},{3,2},{4,5},{5,4},{6,7},{7,6},{8,9},{9,8},{10,11... | collective-permute-start | bytes 24584 | tf_op jit(solution)/shard_map/ppermute | solution.py:25
  1.2 0.7 %copy-start.3 = (bf16[2,2048]{1,0:T(2,128)(2,1)S(1)}, bf16[2,2048]{1,0:T(2,128)(2,1)}, u32[]{:S(2)}) copy-start(bf16[2,2048]{1,0:T(2,128)(2,1)} %rows_ref.1) | copy-start | bytes 24580
  1.9 0.7 %copy-start.4 = (s32[2,4]{1,0:T(2,128)S(1)}, s32[2,4]{1,0:T(2,128)}, u32[]{:S(2)}) copy-start(s32[2,4]{1,0:T(2,128)} %names_ref.1) | copy-start | bytes 100
  2.7 4.7 %copy-start = (bf16[1024,2048]{1,0:T(8,128)(2,1)S(1)}, bf16[1024,2048]{1,0:T(8,128)(2,1)}, u32[]{:S(2)}) copy-start(bf16[1024,2048]{1,0:T(8,128)(2,1)} %weights_ref.1) | copy-start | bytes 12582916
  2.8 8.2 %copy-start.1 = (f32[2048]{0:T(1024)S(1)}, f32[2048]{0:T(1024)}, u32[]{:S(2)}) copy-start(f32[2048]{0:T(1024)} %param.9) | copy-start | bytes 24580
  2.8 8.2 %copy-start.2 = (f32[1024]{0:T(1024)S(1)}, f32[1024]{0:T(1024)}, u32[]{:S(2)}) copy-start(f32[1024]{0:T(1024)} %param.8) | copy-start | bytes 12292
  2.8 7.1 %collective-permute-start.4 = (bf16[4,2176]{1,0:T(4,128)(2,1)S(1)}, bf16[4,2176]{1,0:T(4,128)(2,1)S(1)}, u32[]{:S(2)}, u32[]{:S(2)}) collective-permute-start(bf16[4,2176]{1,0:T(4,128)(2,1)S(1)} %pack.1.after_ref.refs_2_), channel_id=1, source_target_pairs={{0,6},{1,7},{2,4},{3,5},{4,2},{5,3},{6,0},{7,1},{8,14},{9,15},{10,... | collective-permute-start | bytes 52232 | tf_op jit(solution)/shard_map/ppermute | solution.py:25
  6.8 3.8 %collective-permute-start.3 = (bf16[4,2176]{1,0:T(4,128)(2,1)S(1)}, bf16[4,2176]{1,0:T(4,128)(2,1)S(1)}, u32[]{:S(2)}, u32[]{:S(2)}) collective-permute-start(bf16[4,2176]{1,0:T(4,128)(2,1)S(1)} %pack.1.after_ref.refs_2_), channel_id=1, source_target_pairs={{0,4},{1,5},{2,6},{3,7},{4,0},{5,1},{6,2},{7,3},{8,12},{9,13},{10,... | collective-permute-start | bytes 52232 | tf_op jit(solution)/shard_map/ppermute | solution.py:25
  7.3 3.8 %collective-permute-start.2 = (bf16[4,2176]{1,0:T(4,128)(2,1)S(1)}, bf16[4,2176]{1,0:T(4,128)(2,1)S(1)}, u32[]{:S(2)}, u32[]{:S(2)}) collective-permute-start(bf16[4,2176]{1,0:T(4,128)(2,1)S(1)} %pack.1.after_ref.refs_2_), channel_id=1, source_target_pairs={{0,2},{1,3},{2,0},{3,1},{4,6},{5,7},{6,4},{7,5},{8,10},{9,11},{10,... | collective-permute-start | bytes 52232 | tf_op jit(solution)/shard_map/ppermute | solution.py:25
  12.3 1.4 %collective-permute-start.5 = (f32[16,2048]{1,0:T(8,128)S(1)}, f32[16,2048]{1,0:T(8,128)S(1)}, u32[]{:S(2)}, u32[]{:S(2)}) collective-permute-start(f32[16,2048]{1,0:T(8,128)S(1)} %get-tuple-element.35.mine_ref), channel_id=1, source_target_pairs={{0,1},{1,0},{2,3},{3,2},{4,5},{5,4},{6,7},{7,6},{8,9},{9,8},{10,11... | collective-permute-start | bytes 393224 | tf_op jit(solution)/shard_map/ppermute | solution.py:25
  13.7 5.3 %collective-permute-start.8 = (bf16[16,2048]{1,0:T(8,128)(2,1)S(1)}, bf16[16,2048]{1,0:T(8,128)(2,1)S(1)}, u32[]{:S(2)}, u32[]{:S(2)}) collective-permute-start(bf16[16,2048]{1,0:T(8,128)(2,1)S(1)} %get-tuple-element.37), channel_id=1, source_target_pairs={{0,6},{1,7},{2,4},{3,5},{4,2},{5,3},{6,0},{7,1},{8,14},{9,15},{10,... | collective-permute-start | bytes 196616 | tf_op jit(solution)/shard_map/ppermute | solution.py:25
  15.6 4.6 %collective-permute-start.7 = (bf16[16,2048]{1,0:T(8,128)(2,1)S(1)}, bf16[16,2048]{1,0:T(8,128)(2,1)S(1)}, u32[]{:S(2)}, u32[]{:S(2)}) collective-permute-start(bf16[16,2048]{1,0:T(8,128)(2,1)S(1)} %get-tuple-element.37), channel_id=1, source_target_pairs={{0,4},{1,5},{2,6},{3,7},{4,0},{5,1},{6,2},{7,3},{8,12},{9,13},{10,... | collective-permute-start | bytes 196616 | tf_op jit(solution)/shard_map/ppermute | solution.py:25
  16.1 4.3 %collective-permute-start.6 = (bf16[16,2048]{1,0:T(8,128)(2,1)S(1)}, bf16[16,2048]{1,0:T(8,128)(2,1)S(1)}, u32[]{:S(2)}, u32[]{:S(2)}) collective-permute-start(bf16[16,2048]{1,0:T(8,128)(2,1)S(1)} %get-tuple-element.37), channel_id=1, source_target_pairs={{0,2},{1,3},{2,0},{3,1},{4,6},{5,7},{6,4},{7,5},{8,10},{9,11},{10,... | collective-permute-start | bytes 196616 | tf_op jit(solution)/shard_map/ppermute | solution.py:25
  21.5 4.4 %collective-permute-start.9 = (bf16[48,512]{1,0:T(8,128)(2,1)S(1)}, bf16[48,512]{1,0:T(8,128)(2,1)S(1)}, u32[]{:S(2)}, u32[]{:S(2)}) collective-permute-start(bf16[48,512]{1,0:T(8,128)(2,1)S(1)} %get-tuple-element.41), channel_id=1, source_target_pairs={{0,8},{8,0},{16,24},{24,16},{1,9},{9,1},{17,25},{25,17},{2,10},{10... | collective-permute-start | bytes 147464 | tf_op jit(solution)/shard_map/ppermute | solution.py:25
  23.1 5.7 %collective-permute-start.10 = (bf16[48,512]{1,0:T(8,128)(2,1)S(1)}, bf16[48,512]{1,0:T(8,128)(2,1)S(1)}, u32[]{:S(2)}, u32[]{:S(2)}) collective-permute-start(bf16[48,512]{1,0:T(8,128)(2,1)S(1)} %get-tuple-element.42), channel_id=1, source_target_pairs={{0,16},{8,24},{16,0},{24,8},{1,17},{9,25},{17,1},{25,9},{2,18},{10... | collective-permute-start | bytes 147464 | tf_op jit(solution)/shard_map/ppermute | solution.py:25
  25.7 5.9 %collective-permute-start.11 = (bf16[48,512]{1,0:T(8,128)(2,1)S(1)}, bf16[48,512]{1,0:T(8,128)(2,1)S(1)}, u32[]{:S(2)}, u32[]{:S(2)}) collective-permute-start(bf16[48,512]{1,0:T(8,128)(2,1)S(1)} %get-tuple-element.43), channel_id=1, source_target_pairs={{0,24},{8,16},{16,8},{24,0},{1,25},{9,17},{17,9},{25,1},{2,26},{10... | collective-permute-start | bytes 147464 | tf_op jit(solution)/shard_map/ppermute | solution.py:25

commit v5 on v4

--- a/solution.py
+++ b/solution.py
@@ -13,6 +13,8 @@
 LANES = 128
 DIRECT = 4
 TERMS = 8
+ORDER = (0, 1, 2, 3)
+ORDER_DP = (0, 1, 3, 2)
 VMEM = pl.BlockSpec(memory_space=pltpu.VMEM)
 HBM = pl.BlockSpec(memory_space=pltpu.MemorySpace.HBM)
 ANY = pl.BlockSpec(memory_space=pl.ANY)
@@ -23,6 +25,23 @@
 def swap(x, axis, mask):
     size = lax.axis_size(axis)
     return lax.ppermute(x, axis, [(i, i ^ mask) for i in range(size)])
+
+
+def swaps(xs, axis, step):
+    return [swap(x, axis, step * k) if k else x for k, x in enumerate(xs)]
+
+
+def taken(order, xs):
+    return tuple(xs[k] for k in ranked(order, len(xs)))
+
+
+def ranked(order, count):
+    return order if len(order) == count else tuple(range(count))
+
+
+def restored(order, refs):
+    order = ranked(order, len(refs))
+    return [refs[order.index(k)] for k in range(len(refs))]
 
 
 def params(mib):
@@ -125,14 +144,12 @@
 def forward_kernel(rows_dev, top, splits, dec_ref, enc_ref, *refs):
     units, turneds, refs = refs[:splits], refs[splits : 2 * splits], refs[2 * splits :]
     chips = len(refs) - 8
-    pieces = refs[:chips]
+    pieces = restored(ORDER, refs[:chips])
     contrib_ref, cent_ref, input_ref, codes_ref, base_ref, act_ref, hit_ref, rows_ref = refs[chips:]
-    half = chips * rows_dev
+    count = 2 * chips * rows_dev
     width, lat_rows = units[0].shape[1], base_ref.shape[1]
     for k, piece in enumerate(pieces):
-        value = piece[...].astype(F32)
-        rows_ref[k * rows_dev : (k + 1) * rows_dev, :] = value[:rows_dev]
-        rows_ref[half + k * rows_dev : half + (k + 1) * rows_dev, :] = value[rows_dev:]
+        rows_ref[2 * k * rows_dev : 2 * (k + 1) * rows_dev, :] = piece[...].astype(F32)
     input_ref[...] = rows_ref[:, :width].astype(BF16)
     centered = (rows_ref[:, :width] - dec_ref[...]).astype(BF16)
     cent_ref[...] = centered
@@ -142,10 +159,10 @@
     act = jnp.maximum(preact, 0.0) + jnp.log1p(jnp.exp(-jnp.abs(preact)))
     act_ref[...] = act
     first = lax.axis_index("latent") * (lat_rows // BLK)
-    lat = lax.broadcasted_iota(jnp.int32, (2 * half, lat_rows), 1)
+    lat = lax.broadcasted_iota(jnp.int32, (count, lat_rows), 1)
     block_of = (first + lat // BLK).astype(F32)
     names = rows_ref[:, width:]
-    hit = jnp.zeros((2 * half, lat_rows), F32)
+    hit = jnp.zeros((count, lat_rows), F32)
     for k in range(top):
         name = names[:, k : k + 1] * RADIX + names[:, top + k : top + k + 1]
         hit = jnp.where(name == block_of, 1.0, hit)
@@ -191,14 +208,13 @@
             bytes_accessed=4 * lat_rows * width,
             transcendentals=2 * count * lat_rows,
         ),
-    )(dec, enc, *units, *turneds, *pieces)
+    )(dec, enc, *units, *turneds, *taken(ORDER, pieces))
 
 
 def side_kernel(rows_dev, act_ref, hit_ref, codes_ref, base_ref, enc_ref, *outs):
     scores_ref, gate_ref, second_ref, compact_ref = outs
     count, lat_rows = act_ref.shape
     block_count = lat_rows // BLK
-    half = count // 2
     me = lax.axis_index("latent")
     latent = lax.broadcasted_iota(jnp.int32, (block_count, lat_rows), 1)
     block = lax.broadcasted_iota(jnp.int32, (block_count, lat_rows), 0)
@@ -212,8 +228,7 @@
     )
     at = lax.broadcasted_iota(jnp.int32, (count, count), 0)
     place = lax.broadcasted_iota(jnp.int32, (count, count), 1)
-    owner = (place // rows_dev) ^ me
-    relative = (owner % 2) * half + (owner // 2) * rows_dev + place % rows_dev
+    relative = ((place // rows_dev) ^ me) * rows_dev + place % rows_dev
     order = jnp.where(relative == at, 1.0, 0.0).astype(F32)
     scores_ref[...] = jnp.dot(
         means, order, preferred_element_type=F32, precision=lax.Precision.HIGHEST
@@ -257,17 +272,22 @@
     )(act, hit, codes, base, enc)
 
 
-def combine_kernel(mine_ref, mate_ref, sums_ref, sent_ref):
-    half = mine_ref.shape[0] // 2
-    for at, other in ((0, half), (half, 0)):
-        sums = mine_ref[at : at + half, :] + mate_ref[other : other + half, :]
-        sums_ref[at : at + half, :] = sums
-        sent_ref[at : at + half, :] = sums.astype(BF16)
-
-
-def combine(mine, mate):
-    return pl.pallas_call(
-        combine_kernel,
+def exchanged(value, step, mask):
+    blocks = range(value.shape[0] // step)
+    return jnp.concatenate(
+        [value[(k ^ mask) * step : ((k ^ mask) + 1) * step] for k in blocks], axis=0
+    )
+
+
+def combine_kernel(rows_dev, mine_ref, mate_ref, sums_ref, sent_ref):
+    sums = mine_ref[...] + exchanged(mate_ref[...], rows_dev, 1)
+    sums_ref[...] = sums
+    sent_ref[...] = sums.astype(BF16)
+
+
+def combine(rows_dev, mine, mate):
+    return pl.pallas_call(
+        functools.partial(combine_kernel, rows_dev),
         name="combine",
         out_shape=(shape(mine.shape, F32), shape(mine.shape, BF16)),
         in_specs=[VMEM] * 2,
@@ -276,18 +296,12 @@
     )(mine, mate)
 
 
-def errors_kernel(rows_dev, dec_ref, input_ref, sums_ref, parts, recon_ref, errors_ref):
-    chips = len(parts) + 1
-    total = sums_ref[...]
-    for j, part in enumerate(parts, 1):
-        value = part[...].astype(F32)
-        turned = []
-        for k in range(2 * chips):
-            at = (k ^ j) * rows_dev
-            turned.append(value[at : at + rows_dev])
-        total = total + jnp.concatenate(turned, axis=0)
+def errors_kernel(rows_dev, dec_ref, input_ref, parts, recon_ref, errors_ref):
+    total = parts[0][...]
+    for j in range(1, len(parts)):
+        total = total + exchanged(parts[j][...].astype(F32), 2 * rows_dev, j)
     full = total + dec_ref[...]
-    recon_ref[...] = full[:rows_dev].astype(BF16)
+    recon_ref[...] = full[:rows_dev]
     errors_ref[...] = (full - input_ref[...].astype(F32)).astype(BF16)
 
 
@@ -298,10 +312,10 @@
     second_ref, compact_ref = refs[:2]
     if rows_dev:
         chips = cent_ref.shape[0] // (2 * rows_dev)
-        dec_ref, input_ref, sums_ref = refs[2:5]
-        parts, outs = refs[5 : 4 + chips], refs[4 + chips :]
+        dec_ref, input_ref = refs[2:4]
+        parts, outs = restored(ORDER, refs[4 : 4 + chips]), refs[4 + chips :]
         recon_ref, packets, errors_ref = outs[0], outs[1:-1], outs[-1]
-        errors_kernel(rows_dev, dec_ref, input_ref, sums_ref, parts, recon_ref, errors_ref)
+        errors_kernel(rows_dev, dec_ref, input_ref, parts, recon_ref, errors_ref)
     else:
         errors_ref, packets = refs[2], refs[3:]
     count, width = cent_ref.shape
@@ -334,7 +348,7 @@
     outs = (packet,) * groups
     scratch = []
     if rows_dev:
-        outs = (shape((rows_dev, width), BF16),) + outs
+        outs = (shape((rows_dev, width), F32),) + outs
         scratch = [pltpu.VMEM((count, width), BF16)]
     return pl.pallas_call(
         functools.partial(backward_kernel, groups, rows_dev, len(turneds)),
@@ -350,10 +364,25 @@
     )(*turneds, cent, *rest)
 
 
+def rounded_kernel(value_ref, out_ref):
+    out_ref[...] = value_ref[...].astype(BF16)
+
+
+def rounded(value):
+    return pl.pallas_call(
+        rounded_kernel,
+        name="rounded",
+        out_shape=shape(value.shape, BF16),
+        in_specs=[VMEM],
+        out_specs=VMEM,
+        compiler_params=params(4),
+    )(value)
+
+
 def gradient_kernel(count, splits, *refs):
     units, norms, refs = refs[:splits], refs[splits : 2 * splits], refs[2 * splits :]
     out_ref, left_ref, right_ref, held_ref, sems = refs[-5:]
-    packets = refs[:-5]
+    packets = restored(ORDER_DP, refs[:-5])
     lat_rows, cols = out_ref.shape
     along = jnp.zeros((1, lat_rows), F32)
     number = (lax.broadcasted_iota(jnp.int32, (count, lat_rows), 0) + 1).astype(F32)
@@ -418,7 +447,7 @@
         cost_estimate=pl.CostEstimate(
             flops=2 * depth * lat_rows * cols, bytes_accessed=8 * lat_rows * cols, transcendentals=0
         ),
-    )(*units, *norms, *packets)
+    )(*units, *norms, *taken(ORDER_DP, packets))
 
 
 def local(inputs, blocks, weights, enc_bias, dec_bias):
@@ -431,32 +460,32 @@
 
     mate, mate_names = swap(inputs, "latent", 1), swap(blocks, "latent", 1)
     both = pack(stage(inputs, blocks), mate, mate_names)
-    pieces = [both] + [swap(both, "latent", 2 * k) for k in range(1, chips)]
+    pieces = swaps([both] * chips, "latent", 2)
     units, turneds, norms = ([x] for x in normalize(both, weights))
     contrib, cent, rows, codes, base, act, hit = forward(
         rows_dev, top, dec, enc, units, turneds, pieces
     )
-    sums, sent = combine(contrib, swap(contrib, "latent", 1))
+    sums, sent = combine(rows_dev, contrib, swap(contrib, "latent", 1))
     block_scores, gate, second, compact = side(rows_dev, act, hit, codes, base, enc)
     known = (codes, base, gate, second, compact)
     if chips <= DIRECT:
-        parts = [swap(sent, "latent", 2 * j) for j in range(1, chips)]
+        parts = [sums] + swaps([sent] * chips, "latent", 2)[1:]
         recon, *packets = backward(
-            groups, rows_dev, turneds, cent, (*known, dec, rows, sums, *parts)
+            groups, rows_dev, turneds, cent, (*known, dec, rows, *taken(ORDER, parts))
         )
     else:
         full = dec_bias + sums[:rows_dev]
         for j in range(1, chips):
-            full = full + swap(sums[j * rows_dev : (j + 1) * rows_dev], "latent", 2 * j)
-        recon = full.astype(BF16)
+            at = 2 * j * rows_dev
+            full = full + swap(sums[at : at + rows_dev], "latent", 2 * j)
+        recon = full
         errors = (full - rows[:rows_dev].astype(F32)).astype(BF16)
-        errors = [errors] + [swap(errors, "latent", 2 * j) for j in range(1, chips)]
-        errors = jnp.concatenate(errors, axis=0)
         errors = jnp.concatenate([errors, swap(errors, "latent", 1)], axis=0)
+        errors = jnp.concatenate(swaps([errors] * chips, "latent", 2), axis=0)
         packets = backward(groups, 0, turneds, cent, (*known, errors))
-    packets = [swap(p, "dp", k) if k else p for k, p in enumerate(packets)]
+    packets = swaps(packets, "dp", 1)
     grad_weights = gradient(count, units, norms, packets)
-    return (recon, grad_weights, block_scores)
+    return (rounded(recon), grad_weights, block_scores)
 
 
 def solution(mesh):

time: 33.6 us -> 32.8 us (0.976)
  waiting for transfers between devices: 10.3 us -> 9.36 us
    ppermute x12, waiting for transfers between devices: 10.3 us -> 9.36 us  [swap(): return lax.ppermute(x, axis, [(i, i ^ mask) for i in range(size)])]
    pallas_call x1 -> x2, Pallas kernels: 0.02 us -> 0.65 us  [the longest x1 0.61 us: rounded(): pl.pallas_call(rounded_kernel, name='rounded', out_shape=shape(value.shap...]
    pallas_call x1, Pallas kernels: 1.15 us -> 0.7 us  [backward(): pl.pallas_call(functools.partial(backward_kernel, groups, rows_dev, len(t...]
  transfers between devices with their start and end apart: 12 -> 12, of which waited for: 8 -> 8; matrix products, arithmetic and copies ran while one was open for 0% -> 0% of each run, Pallas kernels for 11% -> 13%
where the time goes in v5:
time: 32.8 us; the launch traced here: 32.6 us
  starting transfers between devices  13 us (40%)
  waiting for transfers between devices  9.36 us (29%)
  Pallas kernels  8.13 us (25%)
  local copies, waits for them, and re-layouts  1.39 us (4%)
  between operations  0.71 us (2%)
    ppermute x12, starting transfers between devices, swap(): return lax.ppermute(x, axis, [(i, i ^ mask) for i in range(size)])  13 us
    ppermute x12, waiting for transfers between devices, swap(): return lax.ppermute(x, axis, [(i, i ^ mask) for i in range(size)])  9.36 us
    pallas_call x1, Pallas kernels, normalize(): pl.pallas_call(normalize_kernel, name='normalize', out_shape=(shape((lat_...  2.53 us
    pallas_call x1, Pallas kernels, gradient(): pl.pallas_call(functools.partial(gradient_kernel, count, len(units)), nam...  1.85 us
    unnamed x10, local copies, waits for them, and re-layouts  1.39 us
    pallas_call x1, Pallas kernels, forward(): pl.pallas_call(functools.partial(forward_kernel, rows_dev, top, len(units...  1.25 us
    pallas_call x1, Pallas kernels, side(): pl.pallas_call(functools.partial(side_kernel, rows_dev), name='side', out...  0.97 us
    pallas_call x1, Pallas kernels, backward(): pl.pallas_call(functools.partial(backward_kernel, groups, rows_dev, len(t...  0.7 us
  transfers between devices with their start and end apart: 12, of which 8 were waited for; matrix products, arithmetic and copies ran while one was open for 0% of the time, Pallas kernels for 13%

profile of v5, /device:TPU:0, one launch (start us, length us, event | category | flops | bytes accessed | tf_op | source)
XLA Modules:
  0.0 32.6 jit_solution(17685041740300268738)
XLA Ops:
  0.6 0.5 %collective-permute-start.1 = (s32[2,4]{1,0:T(2,128)}, s32[2,4]{1,0:T(2,128)S(1)}, u32[]{:S(2)}, u32[]{:S(2)}) collective-permute-start(s32[2,4]{1,0:T(2,128)} %names_ref.1), channel_id=1, source_target_pairs={{0,1},{1,0},{2,3},{3,2},{4,5},{5,4},{6,7},{7,6},{8,9},{9,8},{10,11... | collective-permute-start | bytes 104 | tf_op jit(solution)/shard_map/ppermute | solution.py:27
  1.1 0.1 collective-permute-start
  1.2 0.7 %copy-done.3 = bf16[2,2048]{1,0:T(2,128)(2,1)S(1)} copy-done((bf16[2,2048]{1,0:T(2,128)(2,1)S(1)}, bf16[2,2048]{1,0:T(2,128)(2,1)}, u32[]{:S(2)}) %copy-start.3) | copy-done | bytes 8216
  1.9 0.7 %copy-done.4 = s32[2,4]{1,0:T(2,128)S(1)} copy-done((s32[2,4]{1,0:T(2,128)S(1)}, s32[2,4]{1,0:T(2,128)}, u32[]{:S(2)}) %copy-start.4) | copy-done | bytes 56
  2.6 0.1 stage.1.own_ref
  2.7 0.1 pack.1.after_ref.refs_2_
  2.8 0.0 copy-start.2
  2.8 3.9 %collective-permute-start.4 = (bf16[4,2176]{1,0:T(4,128)(2,1)S(1)}, bf16[4,2176]{1,0:T(4,128)(2,1)S(1)}, u32[]{:S(2)}, u32[]{:S(2)}) collective-permute-start(bf16[4,2176]{1,0:T(4,128)(2,1)S(1)} %pack.1.after_ref.refs_2_), channel_id=1, source_target_pairs={{0,6},{1,7},{2,4},{3,5},{4,2},{5,3},{6,0},{7,1},{8,14},{9,15},{10,... | collective-permute-start | bytes 52232 | tf_op jit(solution)/shard_map/ppermute | solution.py:27
  6.8 0.5 %collective-permute-start.3 = (bf16[4,2176]{1,0:T(4,128)(2,1)S(1)}, bf16[4,2176]{1,0:T(4,128)(2,1)S(1)}, u32[]{:S(2)}, u32[]{:S(2)}) collective-permute-start(bf16[4,2176]{1,0:T(4,128)(2,1)S(1)} %pack.1.after_ref.refs_2_), channel_id=1, source_target_pairs={{0,4},{1,5},{2,6},{3,7},{4,0},{5,1},{6,2},{7,3},{8,12},{9,13},{10,... | collective-permute-start | bytes 52232 | tf_op jit(solution)/shard_map/ppermute | solution.py:27
  7.3 0.1 collective-permute-start.2
  7.4 2.5 %normalize.1 = (bf16[1024,2048]{1,0:T(8,128)(2,1)S(1)}, bf16[2048,1024]{1,0:T(8,128)(2,1)S(1)}, f32[1024,1]{1,0:T(8,128)S(1)}) custom-call(bf16[4,2176]{1,0:T(4,128)(2,1)S(1)} %pack.1.after_ref.refs_2_, bf16[1024,2048]{1,0:T(8,128)(2,1)S(1)} %copy-done), custom_call_target="tpu_custom_call" | custom-call | flops 8388608 | bytes 12582912 | tf_op jit(solution)/shard_map/normalize/pallas_call | solution.py:127
  9.9 0.0 collective-permute-done.4.refs_5_
  10.0 0.6 %collective-permute-done.3.refs_4_ = bf16[4,2176]{1,0:T(4,128)(2,1)S(1)} collective-permute-done((bf16[4,2176]{1,0:T(4,128)(2,1)S(1)}, bf16[4,2176]{1,0:T(4,128)(2,1)S(1)}, u32[]{:S(2)}, u32[]{:S(2)}) %collective-permute-start.3) | collective-permute-done | bytes 17440 | tf_op jit(solution)/shard_map/ppermute | solution.py:27
  10.5 0.5 %collective-permute-done.2.refs_3_ = bf16[4,2176]{1,0:T(4,128)(2,1)S(1)} collective-permute-done((bf16[4,2176]{1,0:T(4,128)(2,1)S(1)}, bf16[4,2176]{1,0:T(4,128)(2,1)S(1)}, u32[]{:S(2)}, u32[]{:S(2)}) %collective-permute-start.2) | collective-permute-done | bytes 17440 | tf_op jit(solution)/shard_map/ppermute | solution.py:27
  11.0 1.3 %forward.1 = (f32[16,2048]{1,0:T(8,128)S(1)}, bf16[16,2048]{1,0:T(8,128)(2,1)S(1)}, bf16[16,2048]{1,0:T(8,128)(2,1)S(1)}, bf16[16,1024]{1,0:T(8,128)(2,1)S(1)}, ...) custom-call(f32[1,2048]{1,0:T(1,128)S(1)} %bitcast.2, f32[1,1024]{1,0:T(1,128)S(1)} %bitcast.4, ...), custom_call_target="tpu_custom_call" | custom-call | flops 134217728 | bytes 8388608 | tf_op jit(solution)/shard_map/forward/pallas_call | solution.py:190
  12.3 0.0 collective-permute-start.5
  12.3 1.4 %collective-permute-done.5.mate_ref = f32[16,2048]{1,0:T(8,128)S(1)} collective-permute-done((f32[16,2048]{1,0:T(8,128)S(1)}, f32[16,2048]{1,0:T(8,128)S(1)}, u32[]{:S(2)}, u32[]{:S(2)}) %collective-permute-start.5) | collective-permute-done | bytes 131104 | tf_op jit(solution)/shard_map/ppermute | solution.py:27
  13.7 1.9 %collective-permute-start.8 = (bf16[16,2048]{1,0:T(8,128)(2,1)S(1)}, bf16[16,2048]{1,0:T(8,128)(2,1)S(1)}, u32[]{:S(2)}, u32[]{:S(2)}) collective-permute-start(bf16[16,2048]{1,0:T(8,128)(2,1)S(1)} %get-tuple-element.37), channel_id=1, source_target_pairs={{0,6},{1,7},{2,4},{3,5},{4,2},{5,3},{6,0},{7,1},{8,14},{9,15},{10,... | collective-permute-start | bytes 196616 | tf_op jit(solution)/shard_map/ppermute | solution.py:27
  15.6 0.5 %collective-permute-start.7 = (bf16[16,2048]{1,0:T(8,128)(2,1)S(1)}, bf16[16,2048]{1,0:T(8,128)(2,1)S(1)}, u32[]{:S(2)}, u32[]{:S(2)}) collective-permute-start(bf16[16,2048]{1,0:T(8,128)(2,1)S(1)} %get-tuple-element.37), channel_id=1, source_target_pairs={{0,4},{1,5},{2,6},{3,7},{4,0},{5,1},{6,2},{7,3},{8,12},{9,13},{10,... | collective-permute-start | bytes 196616 | tf_op jit(solution)/shard_map/ppermute | solution.py:27
  16.1 1.2 %collective-permute-start.6 = (bf16[16,2048]{1,0:T(8,128)(2,1)S(1)}, bf16[16,2048]{1,0:T(8,128)(2,1)S(1)}, u32[]{:S(2)}, u32[]{:S(2)}) collective-permute-start(bf16[16,2048]{1,0:T(8,128)(2,1)S(1)} %get-tuple-element.37), channel_id=1, source_target_pairs={{0,2},{1,3},{2,0},{3,1},{4,6},{5,7},{6,4},{7,5},{8,10},{9,11},{10,... | collective-permute-start | bytes 196616 | tf_op jit(solution)/shard_map/ppermute | solution.py:27
  17.2 1.0 %side.1 = (f32[16,16]{1,0:T(8,128)}, f32[16,1024]{1,0:T(8,128)S(1)}, f32[16,1024]{1,0:T(8,128)S(1)}, f32[4,1024]{1,0:T(4,128)S(1)}) custom-call(f32[16,1024]{1,0:T(8,128)S(1)} %get-tuple-element.29.act_ref, f32[16,1024]{1,0:T(8,128)S(1)} %get-tuple-element.30.hit_ref, bf16[16,1024]{1,0:T(8,128)(2,1)S(1)} %get-tuple-element.27.codes_ref.refs_2_, ...), custom_call_target="tpu_custom_call" | custom-call | flops 8388608 | bytes 524288 | tf_op jit(solution)/shard_map/side/pallas_call | solution.py:257
  18.2 0.8 %collective-permute-done.8.refs_12_ = bf16[16,2048]{1,0:T(8,128)(2,1)S(1)} collective-permute-done((bf16[16,2048]{1,0:T(8,128)(2,1)S(1)}, bf16[16,2048]{1,0:T(8,128)(2,1)S(1)}, u32[]{:S(2)}, u32[]{:S(2)}) %collective-permute-start.8) | collective-permute-done | bytes 65568 | tf_op jit(solution)/shard_map/ppermute | solution.py:27
  19.0 1.2 %collective-permute-done.7.refs_11_ = bf16[16,2048]{1,0:T(8,128)(2,1)S(1)} collective-permute-done((bf16[16,2048]{1,0:T(8,128)(2,1)S(1)}, bf16[16,2048]{1,0:T(8,128)(2,1)S(1)}, u32[]{:S(2)}, u32[]{:S(2)}) %collective-permute-start.7) | collective-permute-done | bytes 65568 | tf_op jit(solution)/shard_map/ppermute | solution.py:27
  20.2 0.2 collective-permute-done.6.refs_10_
  20.4 0.7 %backward.1 = (f32[2,2048]{1,0:T(2,128)S(1)}, bf16[48,512]{1,0:T(8,128)(2,1)S(1)}, bf16[48,512]{1,0:T(8,128)(2,1)S(1)}, bf16[48,512]{1,0:T(8,128)(2,1)S(1)}, bf16[48,512]{1,0:T(8,128)(2,1)S(1)}) custom-call(bf16[2048,1024]{1,0:T(8,128)(2,1)S(1)} %get-tuple-element.24.refs_1_.refs_0_, bf16[16,2048]{1,0:T(8,128)(2,1)S(1)} %get-tuple-element.26.refs_1_, ...), custom_call_target="tpu_custom_call" | custom-call | flops 67108864 | bytes 4194304 | tf_op jit(solution)/shard_map/backward/pallas_call | solution.py:353
  21.1 1.6 %collective-permute-start.9 = (bf16[48,512]{1,0:T(8,128)(2,1)S(1)}, bf16[48,512]{1,0:T(8,128)(2,1)S(1)}, u32[]{:S(2)}, u32[]{:S(2)}) collective-permute-start(bf16[48,512]{1,0:T(8,128)(2,1)S(1)} %get-tuple-element.41), channel_id=1, source_target_pairs={{0,8},{8,0},{16,24},{24,16},{1,9},{9,1},{17,25},{25,17},{2,10},{10... | collective-permute-start | bytes 147464 | tf_op jit(solution)/shard_map/ppermute | solution.py:27
  22.7 2.5 %collective-permute-start.10 = (bf16[48,512]{1,0:T(8,128)(2,1)S(1)}, bf16[48,512]{1,0:T(8,128)(2,1)S(1)}, u32[]{:S(2)}, u32[]{:S(2)}) collective-permute-start(bf16[48,512]{1,0:T(8,128)(2,1)S(1)} %get-tuple-element.42), channel_id=1, source_target_pairs={{0,24},{8,16},{16,8},{24,0},{1,25},{9,17},{17,9},{25,1},{2,26},{10... | collective-permute-start | bytes 147464 | tf_op jit(solution)/shard_map/ppermute | solution.py:27
  25.2 0.1 collective-permute-start.11
  25.3 0.6 %rounded.1 = bf16[2,2048]{1,0:T(2,128)(2,1)} custom-call(f32[2,2048]{1,0:T(2,128)S(1)} %get-tuple-element.38.value_ref), custom_call_target="tpu_custom_call" | custom-call | tf_op jit(solution)/shard_map/rounded/pallas_call | solution.py:372
  25.9 3.1 %collective-permute-done.10.refs_4_ = bf16[48,512]{1,0:T(8,128)(2,1)S(1)} collective-permute-done((bf16[48,512]{1,0:T(8,128)(2,1)S(1)}, bf16[48,512]{1,0:T(8,128)(2,1)S(1)}, u32[]{:S(2)}, u32[]{:S(2)}) %collective-permute-start.10) | collective-permute-done | bytes 49184 | tf_op jit(solution)/shard_map/ppermute | solution.py:27
  29.0 1.7 %collective-permute-done.11.refs_5_ = bf16[48,512]{1,0:T(8,128)(2,1)S(1)} collective-permute-done((bf16[48,512]{1,0:T(8,128)(2,1)S(1)}, bf16[48,512]{1,0:T(8,128)(2,1)S(1)}, u32[]{:S(2)}, u32[]{:S(2)}) %collective-permute-start.11) | collective-permute-done | bytes 49184 | tf_op jit(solution)/shard_map/ppermute | solution.py:27
  30.7 1.9 %gradient.1 = f32[1024,512]{1,0:T(8,128)} custom-call(bf16[1024,2048]{1,0:T(8,128)(2,1)S(1)} %get-tuple-element.25.refs_0_, f32[1024,1]{1,0:T(8,128)S(1)} %get-tuple-element.39.refs_1_, bf16[48,512]{1,0:T(8,128)(2,1)S(1)} %get-tuple-element.40.refs_2_, bf16[48,512]{1,0:T(8,128)(2,1)S(1)} %collective-permute-done.9.refs_3_, ...), custom_call_target="tpu_custom_call" | custom-call | flops 134217728 | bytes 4194304 | tf_op jit(solution)/shard_map/gradient/pallas_call | solution.py:434
  (11 shorter events, 0.1 us)
Async XLA Ops:
  0.6 2.1 %collective-permute-start.1 = (s32[2,4]{1,0:T(2,128)}, s32[2,4]{1,0:T(2,128)S(1)}, u32[]{:S(2)}, u32[]{:S(2)}) collective-permute-start(s32[2,4]{1,0:T(2,128)} %names_ref.1), channel_id=1, source_target_pairs={{0,1},{1,0},{2,3},{3,2},{4,5},{5,4},{6,7},{7,6},{8,9},{9,8},{10,11... | collective-permute-start | bytes 104 | tf_op jit(solution)/shard_map/ppermute | solution.py:27
  1.1 1.6 %collective-permute-start = (bf16[2,2048]{1,0:T(2,128)(2,1)}, bf16[2,2048]{1,0:T(2,128)(2,1)S(1)}, u32[]{:S(2)}, u32[]{:S(2)}) collective-permute-start(bf16[2,2048]{1,0:T(2,128)(2,1)} %rows_ref.1), channel_id=1, source_target_pairs={{0,1},{1,0},{2,3},{3,2},{4,5},{5,4},{6,7},{7,6},{8,9},{9,8},{10,11... | collective-permute-start | bytes 24584 | tf_op jit(solution)/shard_map/ppermute | solution.py:27
  1.2 0.7 %copy-start.3 = (bf16[2,2048]{1,0:T(2,128)(2,1)S(1)}, bf16[2,2048]{1,0:T(2,128)(2,1)}, u32[]{:S(2)}) copy-start(bf16[2,2048]{1,0:T(2,128)(2,1)} %rows_ref.1) | copy-start | bytes 24580
  1.9 0.7 %copy-start.4 = (s32[2,4]{1,0:T(2,128)S(1)}, s32[2,4]{1,0:T(2,128)}, u32[]{:S(2)}) copy-start(s32[2,4]{1,0:T(2,128)} %names_ref.1) | copy-start | bytes 100
  2.7 4.7 %copy-start = (bf16[1024,2048]{1,0:T(8,128)(2,1)S(1)}, bf16[1024,2048]{1,0:T(8,128)(2,1)}, u32[]{:S(2)}) copy-start(bf16[1024,2048]{1,0:T(8,128)(2,1)} %weights_ref.1) | copy-start | bytes 12582916
  2.8 8.2 %copy-start.1 = (f32[2048]{0:T(1024)S(1)}, f32[2048]{0:T(1024)}, u32[]{:S(2)}) copy-start(f32[2048]{0:T(1024)} %param.9) | copy-start | bytes 24580
  2.8 8.2 %copy-start.2 = (f32[1024]{0:T(1024)S(1)}, f32[1024]{0:T(1024)}, u32[]{:S(2)}) copy-start(f32[1024]{0:T(1024)} %param.8) | copy-start | bytes 12292
  2.8 7.1 %collective-permute-start.4 = (bf16[4,2176]{1,0:T(4,128)(2,1)S(1)}, bf16[4,2176]{1,0:T(4,128)(2,1)S(1)}, u32[]{:S(2)}, u32[]{:S(2)}) collective-permute-start(bf16[4,2176]{1,0:T(4,128)(2,1)S(1)} %pack.1.after_ref.refs_2_), channel_id=1, source_target_pairs={{0,6},{1,7},{2,4},{3,5},{4,2},{5,3},{6,0},{7,1},{8,14},{9,15},{10,... | collective-permute-start | bytes 52232 | tf_op jit(solution)/shard_map/ppermute | solution.py:27
  6.8 3.8 %collective-permute-start.3 = (bf16[4,2176]{1,0:T(4,128)(2,1)S(1)}, bf16[4,2176]{1,0:T(4,128)(2,1)S(1)}, u32[]{:S(2)}, u32[]{:S(2)}) collective-permute-start(bf16[4,2176]{1,0:T(4,128)(2,1)S(1)} %pack.1.after_ref.refs_2_), channel_id=1, source_target_pairs={{0,4},{1,5},{2,6},{3,7},{4,0},{5,1},{6,2},{7,3},{8,12},{9,13},{10,... | collective-permute-start | bytes 52232 | tf_op jit(solution)/shard_map/ppermute | solution.py:27
  7.3 3.8 %collective-permute-start.2 = (bf16[4,2176]{1,0:T(4,128)(2,1)S(1)}, bf16[4,2176]{1,0:T(4,128)(2,1)S(1)}, u32[]{:S(2)}, u32[]{:S(2)}) collective-permute-start(bf16[4,2176]{1,0:T(4,128)(2,1)S(1)} %pack.1.after_ref.refs_2_), channel_id=1, source_target_pairs={{0,2},{1,3},{2,0},{3,1},{4,6},{5,7},{6,4},{7,5},{8,10},{9,11},{10,... | collective-permute-start | bytes 52232 | tf_op jit(solution)/shard_map/ppermute | solution.py:27
  12.3 1.4 %collective-permute-start.5 = (f32[16,2048]{1,0:T(8,128)S(1)}, f32[16,2048]{1,0:T(8,128)S(1)}, u32[]{:S(2)}, u32[]{:S(2)}) collective-permute-start(f32[16,2048]{1,0:T(8,128)S(1)} %get-tuple-element.35.mine_ref), channel_id=1, source_target_pairs={{0,1},{1,0},{2,3},{3,2},{4,5},{5,4},{6,7},{7,6},{8,9},{9,8},{10,11... | collective-permute-start | bytes 393224 | tf_op jit(solution)/shard_map/ppermute | solution.py:27
  13.7 5.3 %collective-permute-start.8 = (bf16[16,2048]{1,0:T(8,128)(2,1)S(1)}, bf16[16,2048]{1,0:T(8,128)(2,1)S(1)}, u32[]{:S(2)}, u32[]{:S(2)}) collective-permute-start(bf16[16,2048]{1,0:T(8,128)(2,1)S(1)} %get-tuple-element.37), channel_id=1, source_target_pairs={{0,6},{1,7},{2,4},{3,5},{4,2},{5,3},{6,0},{7,1},{8,14},{9,15},{10,... | collective-permute-start | bytes 196616 | tf_op jit(solution)/shard_map/ppermute | solution.py:27
  15.6 4.6 %collective-permute-start.7 = (bf16[16,2048]{1,0:T(8,128)(2,1)S(1)}, bf16[16,2048]{1,0:T(8,128)(2,1)S(1)}, u32[]{:S(2)}, u32[]{:S(2)}) collective-permute-start(bf16[16,2048]{1,0:T(8,128)(2,1)S(1)} %get-tuple-element.37), channel_id=1, source_target_pairs={{0,4},{1,5},{2,6},{3,7},{4,0},{5,1},{6,2},{7,3},{8,12},{9,13},{10,... | collective-permute-start | bytes 196616 | tf_op jit(solution)/shard_map/ppermute | solution.py:27
  16.1 4.3 %collective-permute-start.6 = (bf16[16,2048]{1,0:T(8,128)(2,1)S(1)}, bf16[16,2048]{1,0:T(8,128)(2,1)S(1)}, u32[]{:S(2)}, u32[]{:S(2)}) collective-permute-start(bf16[16,2048]{1,0:T(8,128)(2,1)S(1)} %get-tuple-element.37), channel_id=1, source_target_pairs={{0,2},{1,3},{2,0},{3,1},{4,6},{5,7},{6,4},{7,5},{8,10},{9,11},{10,... | collective-permute-start | bytes 196616 | tf_op jit(solution)/shard_map/ppermute | solution.py:27
  21.1 4.9 %collective-permute-start.9 = (bf16[48,512]{1,0:T(8,128)(2,1)S(1)}, bf16[48,512]{1,0:T(8,128)(2,1)S(1)}, u32[]{:S(2)}, u32[]{:S(2)}) collective-permute-start(bf16[48,512]{1,0:T(8,128)(2,1)S(1)} %get-tuple-element.41), channel_id=1, source_target_pairs={{0,8},{8,0},{16,24},{24,16},{1,9},{9,1},{17,25},{25,17},{2,10},{10... | collective-permute-start | bytes 147464 | tf_op jit(solution)/shard_map/ppermute | solution.py:27
  22.7 6.3 %collective-permute-start.10 = (bf16[48,512]{1,0:T(8,128)(2,1)S(1)}, bf16[48,512]{1,0:T(8,128)(2,1)S(1)}, u32[]{:S(2)}, u32[]{:S(2)}) collective-permute-start(bf16[48,512]{1,0:T(8,128)(2,1)S(1)} %get-tuple-element.42), channel_id=1, source_target_pairs={{0,24},{8,16},{16,8},{24,0},{1,25},{9,17},{17,9},{25,1},{2,26},{10... | collective-permute-start | bytes 147464 | tf_op jit(solution)/shard_map/ppermute | solution.py:27
  25.2 5.5 %collective-permute-start.11 = (bf16[48,512]{1,0:T(8,128)(2,1)S(1)}, bf16[48,512]{1,0:T(8,128)(2,1)S(1)}, u32[]{:S(2)}, u32[]{:S(2)}) collective-permute-start(bf16[48,512]{1,0:T(8,128)(2,1)S(1)} %get-tuple-element.43), channel_id=1, source_target_pairs={{0,16},{8,24},{16,0},{24,8},{1,17},{9,25},{17,1},{25,9},{2,18},{10... | collective-permute-start | bytes 147464 | tf_op jit(solution)/shard_map/ppermute | solution.py:27

commit v6 on v5

--- a/solution.py
+++ b/solution.py
@@ -9,7 +9,8 @@
 
 BLK = 64
 CAP = 2
-RADIX = 32
+SHIFT = 5
+RADIX = 1 << SHIFT
 LANES = 128
 DIRECT = 4
 TERMS = 8
@@ -50,26 +51,6 @@
 
 def shape(dims, dtype):
     return jax.ShapeDtypeStruct(dims, dtype)
-
-
-def stage_kernel(rows_ref, names_ref, out_ref):
-    rows_dev, width = rows_ref.shape
-    lane = lax.broadcasted_iota(jnp.int32, (rows_dev, LANES), 1)
-    out_ref[:, :width] = rows_ref[...]
-    out_ref[:, width:] = coded(names_ref[...], lane).astype(F32).astype(BF16)
-
-
-def stage(rows, names):
-    rows_dev, width = rows.shape
-    return pl.pallas_call(
-        stage_kernel,
-        name="stage",
-        out_shape=shape((rows_dev, width + LANES), BF16),
-        in_specs=[VMEM] * 2,
-        out_specs=VMEM,
-        compiler_params=params(4),
-        cost_estimate=COST,
-    )(rows, names)
 
 
 def pack_kernel(own_ref, mate_ref, mate_names_ref, out_ref):
@@ -459,7 +440,13 @@
     dec, enc = dec_bias[None, :], enc_bias[None, :]
 
     mate, mate_names = swap(inputs, "latent", 1), swap(blocks, "latent", 1)
-    both = pack(stage(inputs, blocks), mate, mate_names)
+    width = inputs.shape[1]
+    lane = lax.broadcasted_iota(jnp.int32, (rows_dev, width + LANES), 1)
+    high = jnp.pad(blocks, ((0, 0), (width, LANES - top)))
+    low = jnp.pad(blocks, ((0, 0), (width + top, LANES - 2 * top)))
+    lists = jnp.where(lane < width + top, high >> SHIFT, low & (RADIX - 1))
+    own = jnp.where(lane < width, jnp.pad(inputs, ((0, 0), (0, LANES))), lists.astype(BF16))
+    both = pack(own, mate, mate_names)
     pieces = swaps([both] * chips, "latent", 2)
     units, turneds, norms = ([x] for x in normalize(both, weights))
     contrib, cent, rows, codes, base, act, hit = forward(

time: 32.8 us -> 32.3 us (0.985)
  local copies, waits for them, and re-layouts: 1.39 us -> 0.01 us
  other arithmetic: 0 us -> 0.85 us
  waiting for transfers between devices: 9.36 us -> 9.81 us
    unnamed x10 -> x6, local copies, waits for them, and re-layouts: 1.39 us -> 0.01 us
    select_n x0 -> x1, other arithmetic: none -> 0.84 us  [local(): jnp.where(lane < width, jnp.pad(inputs, ((0, 0), (0, LANES))), lists.asty...]
    ppermute x12, waiting for transfers between devices: 9.36 us -> 9.81 us  [swap(): return lax.ppermute(x, axis, [(i, i ^ mask) for i in range(size)])]
  transfers between devices with their start and end apart: 12 -> 12, of which waited for: 8 -> 10; matrix products, arithmetic and copies ran while one was open for 0% -> 3% of each run, Pallas kernels for 13% -> 13%
where the time goes in v6:
time: 32.3 us; the launch traced here: 32.1 us
  starting transfers between devices  12.7 us (39%)
  waiting for transfers between devices  9.81 us (30%)
  Pallas kernels  8.04 us (25%)
  other arithmetic  0.85 us (3%)
  between operations  0.69 us (2%)
    ppermute x12, starting transfers between devices, swap(): return lax.ppermute(x, axis, [(i, i ^ mask) for i in range(size)])  12.7 us
    ppermute x12, waiting for transfers between devices, swap(): return lax.ppermute(x, axis, [(i, i ^ mask) for i in range(size)])  9.81 us
    pallas_call x1, Pallas kernels, normalize(): pl.pallas_call(normalize_kernel, name='normalize', out_shape=(shape((lat_...  2.53 us
    pallas_call x1, Pallas kernels, gradient(): pl.pallas_call(functools.partial(gradient_kernel, count, len(units)), nam...  1.85 us
    pallas_call x1, Pallas kernels, forward(): pl.pallas_call(functools.partial(forward_kernel, rows_dev, top, len(units...  1.25 us
    pallas_call x1, Pallas kernels, side(): pl.pallas_call(functools.partial(side_kernel, rows_dev), name='side', out...  0.97 us
    select_n x1, other arithmetic, local(): jnp.where(lane < width, jnp.pad(inputs, ((0, 0), (0, LANES))), lists.asty...  0.84 us
    pallas_call x1, Pallas kernels, backward(): pl.pallas_call(functools.partial(backward_kernel, groups, rows_dev, len(t...  0.7 us
  transfers between devices with their start and end apart: 12, of which 10 were waited for; matrix products, arithmetic and copies ran while one was open for 3% of the time, Pallas kernels for 13%

profile of v6, /device:TPU:0, one launch (start us, length us, event | category | flops | bytes accessed | tf_op | source)
XLA Modules:
  0.0 32.1 jit_solution(9006053687771323401)
XLA Ops:
  0.6 0.5 %collective-permute-start.1 = (s32[2,4]{1,0:T(2,128)}, s32[2,4]{1,0:T(2,128)S(1)}, u32[]{:S(2)}, u32[]{:S(2)}) collective-permute-start(s32[2,4]{1,0:T(2,128)} %param.6), channel_id=1, source_target_pairs={{0,1},{1,0},{2,3},{3,2},{4,5},{5,4},{6,7},{7,6},{8,9},{9,8},{10,11... | collective-permute-start | bytes 104 | tf_op jit(solution)/shard_map/ppermute | solution.py:28
  1.1 0.1 collective-permute-start
  1.2 0.8 %broadcast_select_fusion.own_ref = bf16[2,2176]{1,0:T(2,128)(2,1)S(1)} fusion(pred[2176]{0:T(1024)(128)(4,1)S(1)} %get-tuple-element.46, s32[2,4]{1,0:T(2,128)} %param.6, pred[2176]{0:T(1024)(128)(4,1)S(1)} %get-tuple-element.45, bf16[2,2048]{1,0:T(2,128)(2,1)} %param.5), kind=kLoop, calls=%fused_computation.1 | loop fusion | flops 21760 | bytes 21280 | tf_op jit(solution)/shard_map/jit(_where)/select_n | solution.py:448
  2.1 0.1 collective-permute-done.1.mate_names_ref
  2.2 0.4 %collective-permute-done.mate_ref = bf16[2,2048]{1,0:T(2,128)(2,1)S(1)} collective-permute-done((bf16[2,2048]{1,0:T(2,128)(2,1)}, bf16[2,2048]{1,0:T(2,128)(2,1)S(1)}, u32[]{:S(2)}, u32[]{:S(2)}) %collective-permute-start) | collective-permute-done | bytes 8224 | tf_op jit(solution)/shard_map/ppermute | solution.py:28
  2.5 0.1 pack.1.after_ref.refs_2_
  2.6 0.0 copy-start.2
  2.6 3.7 %collective-permute-start.4 = (bf16[4,2176]{1,0:T(4,128)(2,1)S(1)}, bf16[4,2176]{1,0:T(4,128)(2,1)S(1)}, u32[]{:S(2)}, u32[]{:S(2)}) collective-permute-start(bf16[4,2176]{1,0:T(4,128)(2,1)S(1)} %pack.1.after_ref.refs_2_), channel_id=1, source_target_pairs={{0,6},{1,7},{2,4},{3,5},{4,2},{5,3},{6,0},{7,1},{8,14},{9,15},{10,... | collective-permute-start | bytes 52232 | tf_op jit(solution)/shard_map/ppermute | solution.py:28
  6.3 0.5 %collective-permute-start.3 = (bf16[4,2176]{1,0:T(4,128)(2,1)S(1)}, bf16[4,2176]{1,0:T(4,128)(2,1)S(1)}, u32[]{:S(2)}, u32[]{:S(2)}) collective-permute-start(bf16[4,2176]{1,0:T(4,128)(2,1)S(1)} %pack.1.after_ref.refs_2_), channel_id=1, source_target_pairs={{0,4},{1,5},{2,6},{3,7},{4,0},{5,1},{6,2},{7,3},{8,12},{9,13},{10,... | collective-permute-start | bytes 52232 | tf_op jit(solution)/shard_map/ppermute | solution.py:28
  6.8 0.1 collective-permute-start.2
  7.0 2.5 %normalize.1 = (bf16[1024,2048]{1,0:T(8,128)(2,1)S(1)}, bf16[2048,1024]{1,0:T(8,128)(2,1)S(1)}, f32[1024,1]{1,0:T(8,128)S(1)}) custom-call(bf16[4,2176]{1,0:T(4,128)(2,1)S(1)} %pack.1.after_ref.refs_2_, bf16[1024,2048]{1,0:T(8,128)(2,1)S(1)} %copy-done), custom_call_target="tpu_custom_call" | custom-call | flops 8388608 | bytes 12582912 | tf_op jit(solution)/shard_map/normalize/pallas_call | solution.py:108
  9.5 0.0 collective-permute-done.4.refs_5_
  9.5 0.6 %collective-permute-done.3.refs_4_ = bf16[4,2176]{1,0:T(4,128)(2,1)S(1)} collective-permute-done((bf16[4,2176]{1,0:T(4,128)(2,1)S(1)}, bf16[4,2176]{1,0:T(4,128)(2,1)S(1)}, u32[]{:S(2)}, u32[]{:S(2)}) %collective-permute-start.3) | collective-permute-done | bytes 17440 | tf_op jit(solution)/shard_map/ppermute | solution.py:28
  10.1 0.5 %collective-permute-done.2.refs_3_ = bf16[4,2176]{1,0:T(4,128)(2,1)S(1)} collective-permute-done((bf16[4,2176]{1,0:T(4,128)(2,1)S(1)}, bf16[4,2176]{1,0:T(4,128)(2,1)S(1)}, u32[]{:S(2)}, u32[]{:S(2)}) %collective-permute-start.2) | collective-permute-done | bytes 17440 | tf_op jit(solution)/shard_map/ppermute | solution.py:28
  10.6 1.3 %forward.1 = (f32[16,2048]{1,0:T(8,128)S(1)}, bf16[16,2048]{1,0:T(8,128)(2,1)S(1)}, bf16[16,2048]{1,0:T(8,128)(2,1)S(1)}, bf16[16,1024]{1,0:T(8,128)(2,1)S(1)}, ...) custom-call(f32[1,2048]{1,0:T(1,128)S(1)} %bitcast.2, f32[1,1024]{1,0:T(1,128)S(1)} %bitcast.4, ...), custom_call_target="tpu_custom_call" | custom-call | flops 134217728 | bytes 8388608 | tf_op jit(solution)/shard_map/forward/pallas_call | solution.py:171
  11.8 0.0 collective-permute-start.5
  11.8 1.4 %collective-permute-done.5.mate_ref = f32[16,2048]{1,0:T(8,128)S(1)} collective-permute-done((f32[16,2048]{1,0:T(8,128)S(1)}, f32[16,2048]{1,0:T(8,128)S(1)}, u32[]{:S(2)}, u32[]{:S(2)}) %collective-permute-start.5) | collective-permute-done | bytes 131104 | tf_op jit(solution)/shard_map/ppermute | solution.py:28
  13.2 1.9 %collective-permute-start.8 = (bf16[16,2048]{1,0:T(8,128)(2,1)S(1)}, bf16[16,2048]{1,0:T(8,128)(2,1)S(1)}, u32[]{:S(2)}, u32[]{:S(2)}) collective-permute-start(bf16[16,2048]{1,0:T(8,128)(2,1)S(1)} %get-tuple-element.37), channel_id=1, source_target_pairs={{0,6},{1,7},{2,4},{3,5},{4,2},{5,3},{6,0},{7,1},{8,14},{9,15},{10,... | collective-permute-start | bytes 196616 | tf_op jit(solution)/shard_map/ppermute | solution.py:28
  15.1 0.5 %collective-permute-start.7 = (bf16[16,2048]{1,0:T(8,128)(2,1)S(1)}, bf16[16,2048]{1,0:T(8,128)(2,1)S(1)}, u32[]{:S(2)}, u32[]{:S(2)}) collective-permute-start(bf16[16,2048]{1,0:T(8,128)(2,1)S(1)} %get-tuple-element.37), channel_id=1, source_target_pairs={{0,4},{1,5},{2,6},{3,7},{4,0},{5,1},{6,2},{7,3},{8,12},{9,13},{10,... | collective-permute-start | bytes 196616 | tf_op jit(solution)/shard_map/ppermute | solution.py:28
  15.6 1.2 %collective-permute-start.6 = (bf16[16,2048]{1,0:T(8,128)(2,1)S(1)}, bf16[16,2048]{1,0:T(8,128)(2,1)S(1)}, u32[]{:S(2)}, u32[]{:S(2)}) collective-permute-start(bf16[16,2048]{1,0:T(8,128)(2,1)S(1)} %get-tuple-element.37), channel_id=1, source_target_pairs={{0,2},{1,3},{2,0},{3,1},{4,6},{5,7},{6,4},{7,5},{8,10},{9,11},{10,... | collective-permute-start | bytes 196616 | tf_op jit(solution)/shard_map/ppermute | solution.py:28
  16.8 1.0 %side.1 = (f32[16,16]{1,0:T(8,128)}, f32[16,1024]{1,0:T(8,128)S(1)}, f32[16,1024]{1,0:T(8,128)S(1)}, f32[4,1024]{1,0:T(4,128)S(1)}) custom-call(f32[16,1024]{1,0:T(8,128)S(1)} %get-tuple-element.29.act_ref, f32[16,1024]{1,0:T(8,128)S(1)} %get-tuple-element.30.hit_ref, bf16[16,1024]{1,0:T(8,128)(2,1)S(1)} %get-tuple-element.27.codes_ref.refs_2_, ...), custom_call_target="tpu_custom_call" | custom-call | flops 8388608 | bytes 524288 | tf_op jit(solution)/shard_map/side/pallas_call | solution.py:238
  17.7 0.8 %collective-permute-done.8.refs_12_ = bf16[16,2048]{1,0:T(8,128)(2,1)S(1)} collective-permute-done((bf16[16,2048]{1,0:T(8,128)(2,1)S(1)}, bf16[16,2048]{1,0:T(8,128)(2,1)S(1)}, u32[]{:S(2)}, u32[]{:S(2)}) %collective-permute-start.8) | collective-permute-done | bytes 65568 | tf_op jit(solution)/shard_map/ppermute | solution.py:28
  18.5 1.2 %collective-permute-done.7.refs_11_ = bf16[16,2048]{1,0:T(8,128)(2,1)S(1)} collective-permute-done((bf16[16,2048]{1,0:T(8,128)(2,1)S(1)}, bf16[16,2048]{1,0:T(8,128)(2,1)S(1)}, u32[]{:S(2)}, u32[]{:S(2)}) %collective-permute-start.7) | collective-permute-done | bytes 65568 | tf_op jit(solution)/shard_map/ppermute | solution.py:28
  19.7 0.2 collective-permute-done.6.refs_10_
  19.9 0.7 %backward.1 = (f32[2,2048]{1,0:T(2,128)S(1)}, bf16[48,512]{1,0:T(8,128)(2,1)S(1)}, bf16[48,512]{1,0:T(8,128)(2,1)S(1)}, bf16[48,512]{1,0:T(8,128)(2,1)S(1)}, bf16[48,512]{1,0:T(8,128)(2,1)S(1)}) custom-call(bf16[2048,1024]{1,0:T(8,128)(2,1)S(1)} %get-tuple-element.24.refs_1_.refs_0_, bf16[16,2048]{1,0:T(8,128)(2,1)S(1)} %get-tuple-element.26.refs_1_, ...), custom_call_target="tpu_custom_call" | custom-call | flops 67108864 | bytes 4194304 | tf_op jit(solution)/shard_map/backward/pallas_call | solution.py:334
  20.6 1.6 %collective-permute-start.9 = (bf16[48,512]{1,0:T(8,128)(2,1)S(1)}, bf16[48,512]{1,0:T(8,128)(2,1)S(1)}, u32[]{:S(2)}, u32[]{:S(2)}) collective-permute-start(bf16[48,512]{1,0:T(8,128)(2,1)S(1)} %get-tuple-element.41), channel_id=1, source_target_pairs={{0,8},{8,0},{16,24},{24,16},{1,9},{9,1},{17,25},{25,17},{2,10},{10... | collective-permute-start | bytes 147464 | tf_op jit(solution)/shard_map/ppermute | solution.py:28
  22.3 2.5 %collective-permute-start.10 = (bf16[48,512]{1,0:T(8,128)(2,1)S(1)}, bf16[48,512]{1,0:T(8,128)(2,1)S(1)}, u32[]{:S(2)}, u32[]{:S(2)}) collective-permute-start(bf16[48,512]{1,0:T(8,128)(2,1)S(1)} %get-tuple-element.42), channel_id=1, source_target_pairs={{0,24},{8,16},{16,8},{24,0},{1,25},{9,17},{17,9},{25,1},{2,26},{10... | collective-permute-start | bytes 147464 | tf_op jit(solution)/shard_map/ppermute | solution.py:28
  24.7 0.1 collective-permute-start.11
  24.9 0.6 %rounded.1 = bf16[2,2048]{1,0:T(2,128)(2,1)} custom-call(f32[2,2048]{1,0:T(2,128)S(1)} %get-tuple-element.38.value_ref), custom_call_target="tpu_custom_call" | custom-call | tf_op jit(solution)/shard_map/rounded/pallas_call | solution.py:353
  25.5 3.1 %collective-permute-done.10.refs_4_ = bf16[48,512]{1,0:T(8,128)(2,1)S(1)} collective-permute-done((bf16[48,512]{1,0:T(8,128)(2,1)S(1)}, bf16[48,512]{1,0:T(8,128)(2,1)S(1)}, u32[]{:S(2)}, u32[]{:S(2)}) %collective-permute-start.10) | collective-permute-done | bytes 49184 | tf_op jit(solution)/shard_map/ppermute | solution.py:28
  28.5 1.7 %collective-permute-done.11.refs_5_ = bf16[48,512]{1,0:T(8,128)(2,1)S(1)} collective-permute-done((bf16[48,512]{1,0:T(8,128)(2,1)S(1)}, bf16[48,512]{1,0:T(8,128)(2,1)S(1)}, u32[]{:S(2)}, u32[]{:S(2)}) %collective-permute-start.11) | collective-permute-done | bytes 49184 | tf_op jit(solution)/shard_map/ppermute | solution.py:28
  30.3 1.9 %gradient.1 = f32[1024,512]{1,0:T(8,128)} custom-call(bf16[1024,2048]{1,0:T(8,128)(2,1)S(1)} %get-tuple-element.25.refs_0_, f32[1024,1]{1,0:T(8,128)S(1)} %get-tuple-element.39.refs_1_, bf16[48,512]{1,0:T(8,128)(2,1)S(1)} %get-tuple-element.40.refs_2_, bf16[48,512]{1,0:T(8,128)(2,1)S(1)} %collective-permute-done.9.refs_3_, ...), custom_call_target="tpu_custom_call" | custom-call | flops 134217728 | bytes 4194304 | tf_op jit(solution)/shard_map/gradient/pallas_call | solution.py:415
  (8 shorter events, 0.1 us)
Async XLA Ops:
  0.6 1.5 %collective-permute-start.1 = (s32[2,4]{1,0:T(2,128)}, s32[2,4]{1,0:T(2,128)S(1)}, u32[]{:S(2)}, u32[]{:S(2)}) collective-permute-start(s32[2,4]{1,0:T(2,128)} %param.6), channel_id=1, source_target_pairs={{0,1},{1,0},{2,3},{3,2},{4,5},{5,4},{6,7},{7,6},{8,9},{9,8},{10,11... | collective-permute-start | bytes 104 | tf_op jit(solution)/shard_map/ppermute | solution.py:28
  1.1 1.4 %collective-permute-start = (bf16[2,2048]{1,0:T(2,128)(2,1)}, bf16[2,2048]{1,0:T(2,128)(2,1)S(1)}, u32[]{:S(2)}, u32[]{:S(2)}) collective-permute-start(bf16[2,2048]{1,0:T(2,128)(2,1)} %param.5), channel_id=1, source_target_pairs={{0,1},{1,0},{2,3},{3,2},{4,5},{5,4},{6,7},{7,6},{8,9},{9,8},{10,11... | collective-permute-start | bytes 24584 | tf_op jit(solution)/shard_map/ppermute | solution.py:28
  2.1 4.9 %copy-start = (bf16[1024,2048]{1,0:T(8,128)(2,1)S(1)}, bf16[1024,2048]{1,0:T(8,128)(2,1)}, u32[]{:S(2)}) copy-start(bf16[1024,2048]{1,0:T(8,128)(2,1)} %weights_ref.1) | copy-start | bytes 12582916
  2.6 8.0 %copy-start.1 = (f32[2048]{0:T(1024)S(1)}, f32[2048]{0:T(1024)}, u32[]{:S(2)}) copy-start(f32[2048]{0:T(1024)} %param.9) | copy-start | bytes 24580
  2.6 7.9 %copy-start.2 = (f32[1024]{0:T(1024)S(1)}, f32[1024]{0:T(1024)}, u32[]{:S(2)}) copy-start(f32[1024]{0:T(1024)} %param.8) | copy-start | bytes 12292
  2.6 6.9 %collective-permute-start.4 = (bf16[4,2176]{1,0:T(4,128)(2,1)S(1)}, bf16[4,2176]{1,0:T(4,128)(2,1)S(1)}, u32[]{:S(2)}, u32[]{:S(2)}) collective-permute-start(bf16[4,2176]{1,0:T(4,128)(2,1)S(1)} %pack.1.after_ref.refs_2_), channel_id=1, source_target_pairs={{0,6},{1,7},{2,4},{3,5},{4,2},{5,3},{6,0},{7,1},{8,14},{9,15},{10,... | collective-permute-start | bytes 52232 | tf_op jit(solution)/shard_map/ppermute | solution.py:28
  6.3 3.8 %collective-permute-start.3 = (bf16[4,2176]{1,0:T(4,128)(2,1)S(1)}, bf16[4,2176]{1,0:T(4,128)(2,1)S(1)}, u32[]{:S(2)}, u32[]{:S(2)}) collective-permute-start(bf16[4,2176]{1,0:T(4,128)(2,1)S(1)} %pack.1.after_ref.refs_2_), channel_id=1, source_target_pairs={{0,4},{1,5},{2,6},{3,7},{4,0},{5,1},{6,2},{7,3},{8,12},{9,13},{10,... | collective-permute-start | bytes 52232 | tf_op jit(solution)/shard_map/ppermute | solution.py:28
  6.8 3.8 %collective-permute-start.2 = (bf16[4,2176]{1,0:T(4,128)(2,1)S(1)}, bf16[4,2176]{1,0:T(4,128)(2,1)S(1)}, u32[]{:S(2)}, u32[]{:S(2)}) collective-permute-start(bf16[4,2176]{1,0:T(4,128)(2,1)S(1)} %pack.1.after_ref.refs_2_), channel_id=1, source_target_pairs={{0,2},{1,3},{2,0},{3,1},{4,6},{5,7},{6,4},{7,5},{8,10},{9,11},{10,... | collective-permute-start | bytes 52232 | tf_op jit(solution)/shard_map/ppermute | solution.py:28
  11.8 1.4 %collective-permute-start.5 = (f32[16,2048]{1,0:T(8,128)S(1)}, f32[16,2048]{1,0:T(8,128)S(1)}, u32[]{:S(2)}, u32[]{:S(2)}) collective-permute-start(f32[16,2048]{1,0:T(8,128)S(1)} %get-tuple-element.35.mine_ref), channel_id=1, source_target_pairs={{0,1},{1,0},{2,3},{3,2},{4,5},{5,4},{6,7},{7,6},{8,9},{9,8},{10,11... | collective-permute-start | bytes 393224 | tf_op jit(solution)/shard_map/ppermute | solution.py:28
  13.2 5.3 %collective-permute-start.8 = (bf16[16,2048]{1,0:T(8,128)(2,1)S(1)}, bf16[16,2048]{1,0:T(8,128)(2,1)S(1)}, u32[]{:S(2)}, u32[]{:S(2)}) collective-permute-start(bf16[16,2048]{1,0:T(8,128)(2,1)S(1)} %get-tuple-element.37), channel_id=1, source_target_pairs={{0,6},{1,7},{2,4},{3,5},{4,2},{5,3},{6,0},{7,1},{8,14},{9,15},{10,... | collective-permute-start | bytes 196616 | tf_op jit(solution)/shard_map/ppermute | solution.py:28
  15.1 4.6 %collective-permute-start.7 = (bf16[16,2048]{1,0:T(8,128)(2,1)S(1)}, bf16[16,2048]{1,0:T(8,128)(2,1)S(1)}, u32[]{:S(2)}, u32[]{:S(2)}) collective-permute-start(bf16[16,2048]{1,0:T(8,128)(2,1)S(1)} %get-tuple-element.37), channel_id=1, source_target_pairs={{0,4},{1,5},{2,6},{3,7},{4,0},{5,1},{6,2},{7,3},{8,12},{9,13},{10,... | collective-permute-start | bytes 196616 | tf_op jit(solution)/shard_map/ppermute | solution.py:28
  15.6 4.3 %collective-permute-start.6 = (bf16[16,2048]{1,0:T(8,128)(2,1)S(1)}, bf16[16,2048]{1,0:T(8,128)(2,1)S(1)}, u32[]{:S(2)}, u32[]{:S(2)}) collective-permute-start(bf16[16,2048]{1,0:T(8,128)(2,1)S(1)} %get-tuple-element.37), channel_id=1, source_target_pairs={{0,2},{1,3},{2,0},{3,1},{4,6},{5,7},{6,4},{7,5},{8,10},{9,11},{10,... | collective-permute-start | bytes 196616 | tf_op jit(solution)/shard_map/ppermute | solution.py:28
  20.6 4.9 %collective-permute-start.9 = (bf16[48,512]{1,0:T(8,128)(2,1)S(1)}, bf16[48,512]{1,0:T(8,128)(2,1)S(1)}, u32[]{:S(2)}, u32[]{:S(2)}) collective-permute-start(bf16[48,512]{1,0:T(8,128)(2,1)S(1)} %get-tuple-element.41), channel_id=1, source_target_pairs={{0,8},{8,0},{16,24},{24,16},{1,9},{9,1},{17,25},{25,17},{2,10},{10... | collective-permute-start | bytes 147464 | tf_op jit(solution)/shard_map/ppermute | solution.py:28
  22.3 6.3 %collective-permute-start.10 = (bf16[48,512]{1,0:T(8,128)(2,1)S(1)}, bf16[48,512]{1,0:T(8,128)(2,1)S(1)}, u32[]{:S(2)}, u32[]{:S(2)}) collective-permute-start(bf16[48,512]{1,0:T(8,128)(2,1)S(1)} %get-tuple-element.42), channel_id=1, source_target_pairs={{0,24},{8,16},{16,8},{24,0},{1,25},{9,17},{17,9},{25,1},{2,26},{10... | collective-permute-start | bytes 147464 | tf_op jit(solution)/shard_map/ppermute | solution.py:28
  24.7 5.5 %collective-permute-start.11 = (bf16[48,512]{1,0:T(8,128)(2,1)S(1)}, bf16[48,512]{1,0:T(8,128)(2,1)S(1)}, u32[]{:S(2)}, u32[]{:S(2)}) collective-permute-start(bf16[48,512]{1,0:T(8,128)(2,1)S(1)} %get-tuple-element.43), channel_id=1, source_target_pairs={{0,16},{8,24},{16,0},{24,8},{1,17},{9,25},{17,1},{25,9},{2,18},{10... | collective-permute-start | bytes 147464 | tf_op jit(solution)/shard_map/ppermute | solution.py:28

commit v7 on v6

--- a/solution.py
+++ b/solution.py
@@ -15,7 +15,7 @@
 DIRECT = 4
 TERMS = 8
 ORDER = (0, 1, 2, 3)
-ORDER_DP = (0, 1, 3, 2)
+LATE = 2
 VMEM = pl.BlockSpec(memory_space=pltpu.VMEM)
 HBM = pl.BlockSpec(memory_space=pltpu.MemorySpace.HBM)
 ANY = pl.BlockSpec(memory_space=pl.ANY)
@@ -84,7 +84,7 @@
     )(own, mate, mate_names)
 
 
-def normalize_kernel(after_ref, weights_ref, unit_ref, turned_ref, norms_ref):
+def normalize_kernel(after_ref, weights_ref, unit_ref, turned_ref, inverse_ref):
     del after_ref
     lat_rows, width = weights_ref.shape
     for top in range(0, lat_rows, LANES):
@@ -94,8 +94,8 @@
             tile = weights_ref[rows, left : left + LANES].astype(F32)
             squares = squares + tile * tile
         norms = jnp.sqrt(jnp.sum(squares, axis=1, keepdims=True) + 1e-06)
-        norms_ref[rows, :] = norms
         scale = jnp.broadcast_to(1.0 / norms, (LANES, LANES))
+        inverse_ref[rows, :] = scale
         for left in range(0, width, LANES):
             tile = weights_ref[rows, left : left + LANES].astype(F32)
             unit = (tile * scale).astype(BF16)
@@ -111,7 +111,7 @@
         out_shape=(
             shape((lat_rows, width), BF16),
             shape((width, lat_rows), BF16),
-            shape((lat_rows, 1), F32),
+            shape((lat_rows, LANES), F32),
         ),
         in_specs=[ANY, VMEM],
         out_specs=(VMEM,) * 3,
@@ -360,36 +360,38 @@
     )(value)
 
 
-def gradient_kernel(count, splits, *refs):
-    units, norms, refs = refs[:splits], refs[splits : 2 * splits], refs[2 * splits :]
+def gradient_kernel(count, given, unit_ref, inverse_ref, *refs):
     out_ref, left_ref, right_ref, held_ref, sems = refs[-5:]
-    packets = restored(ORDER_DP, refs[:-5])
+    packets, before_refs = refs[:given], refs[given:-5]
     lat_rows, cols = out_ref.shape
-    along = jnp.zeros((1, lat_rows), F32)
+    depth = 2 * count * len(packets)
+    extra = left_ref.shape[0] - depth
+    along = []
     number = (lax.broadcasted_iota(jnp.int32, (count, lat_rows), 0) + 1).astype(F32)
     for g, packet in enumerate(packets):
         base = g * 2 * count
-        right_ref[base : base + 2 * count, :] = packet[: 2 * count, :]
+        right_ref[base : base + 2 * count, :cols] = packet[: 2 * count, :]
         parts = [
             packet[2 * count + p * TERMS : 2 * count + (p + 1) * TERMS, :].astype(F32)
             for p in range(lat_rows // cols)
         ]
         terms = jnp.concatenate(parts, axis=1)
-        code0, code1, row0, row1, grad0, grad1, high, low = [
-            terms[t : t + 1] for t in range(TERMS)
-        ]
+        code0, code1, row0, row1, grad0, grad1 = [terms[t : t + 1] for t in range(TERMS - 2)]
         at0, at1 = number == row0, number == row1
         code = jnp.where(at0, code0, jnp.where(at1, code1, 0.0))
         grad = jnp.where(at0, grad0, jnp.where(at1, grad1, 0.0))
         left_ref[base : base + count, :] = code.astype(BF16)
         left_ref[base + count : base + 2 * count, :] = grad.astype(BF16)
-        along = along + (high + low)
+        along.append(terms[TERMS - 2 :])
+    if extra > 2 * len(packets):
+        along.append(jnp.zeros((extra - 2 * len(packets), lat_rows), F32))
+    left_ref[depth:, :] = jnp.concatenate(along, axis=0).astype(BF16)
+    right_ref[depth:, :cols] = jnp.zeros((extra, cols), BF16)
+    right_ref[:depth, cols:] = jnp.zeros((depth, LANES), BF16)
+    right_ref[depth:, cols:] = jnp.ones((extra, LANES), BF16)
     start = pl.multiple_of(lax.axis_index("dp") * cols, LANES)
     copies = []
-    which, first = 0, 0
     for at in range(lat_rows // LANES):
-        if at * LANES == first + units[which].shape[0]:
-            first, which = at * LANES, which + 1
         rows = pl.ds(at * LANES, LANES)
         outer = lax.dot_general(
             left_ref[:, rows],
@@ -397,38 +399,44 @@
             (((0,), (0,)), ((), ())),
             preferred_element_type=F32,
         )
-        column = jnp.broadcast_to(along[:, at * LANES : (at + 1) * LANES], (LANES, LANES)).T
-        part = pl.ds(at * LANES - first, LANES)
-        unit = units[which][part, pl.ds(start, cols)].astype(F32)
-        inverse = 1.0 / norms[which][part, :]
-        held_ref[rows, :] = (outer - unit * column[:, :1]) * inverse
-        copies.append(pltpu.make_async_copy(held_ref.at[rows], out_ref.at[rows], sems.at[at]))
-        copies[-1].start()
+        unit = unit_ref[rows, pl.ds(start, cols)].astype(F32)
+        inverse, total = inverse_ref[rows, :], outer[:, cols:]
+        for tile in range(0, cols, LANES):
+            part = slice(tile, tile + LANES)
+            value = (outer[:, part] - unit[:, part] * total) * inverse
+            if before_refs:
+                held_ref[rows, part] = before_refs[0][rows, part] + value
+            else:
+                out_ref[rows, part] = value
+        if before_refs:
+            copies.append(pltpu.make_async_copy(held_ref.at[rows], out_ref.at[rows], sems.at[at]))
+            copies[-1].start()
     for copy in copies:
         copy.wait()
 
 
-def gradient(count, units, norms, packets):
-    lat_rows = sum(unit.shape[0] for unit in units)
+def gradient(name, count, unit, inverse, packets, before):
+    lat_rows = unit.shape[0]
     cols = packets[0].shape[1]
     depth = 2 * count * len(packets)
-    return pl.pallas_call(
-        functools.partial(gradient_kernel, count, len(units)),
-        name="gradient",
+    rows = depth + max(16, 2 * len(packets))
+    return pl.pallas_call(
+        functools.partial(gradient_kernel, count, len(packets)),
+        name=name,
         out_shape=shape((lat_rows, cols), F32),
-        in_specs=[VMEM] * (2 * len(units) + len(packets)),
-        out_specs=HBM,
+        in_specs=[VMEM] * (2 + len(packets) + len(before)),
+        out_specs=HBM if before else VMEM,
         scratch_shapes=[
-            pltpu.VMEM((depth, lat_rows), BF16),
-            pltpu.VMEM((depth, cols), BF16),
-            pltpu.VMEM((lat_rows, cols), F32),
+            pltpu.VMEM((rows, lat_rows), BF16),
+            pltpu.VMEM((rows, cols + LANES), BF16),
+            pltpu.VMEM((lat_rows, cols) if before else (8, LANES), F32),
             pltpu.SemaphoreType.DMA((lat_rows // LANES,)),
         ],
         compiler_params=params(24),
         cost_estimate=pl.CostEstimate(
             flops=2 * depth * lat_rows * cols, bytes_accessed=8 * lat_rows * cols, transcendentals=0
         ),
-    )(*units, *norms, *taken(ORDER_DP, packets))
+    )(unit, inverse, *packets, *before)
 
 
 def local(inputs, blocks, weights, enc_bias, dec_bias):
@@ -448,7 +456,8 @@
     own = jnp.where(lane < width, jnp.pad(inputs, ((0, 0), (0, LANES))), lists.astype(BF16))
     both = pack(own, mate, mate_names)
     pieces = swaps([both] * chips, "latent", 2)
-    units, turneds, norms = ([x] for x in normalize(both, weights))
+    unit, turned, inverse = normalize(both, weights)
+    units, turneds = [unit], [turned]
     contrib, cent, rows, codes, base, act, hit = forward(
         rows_dev, top, dec, enc, units, turneds, pieces
     )
@@ -471,7 +480,10 @@
         errors = jnp.concatenate(swaps([errors] * chips, "latent", 2), axis=0)
         packets = backward(groups, 0, turneds, cent, (*known, errors))
     packets = swaps(packets, "dp", 1)
-    grad_weights = gradient(count, units, norms, packets)
+    late = LATE if groups == len(ORDER) else groups - 1
+    early = [p for k, p in enumerate(packets) if k != late]
+    partial = gradient("early", count, unit, inverse, early, [])
+    grad_weights = gradient("gradient", count, unit, inverse, [packets[late]], [partial])
     return (rounded(recon), grad_weights, block_scores)
 
 

time: 32.3 us -> 32.1 us (level)
  waiting for transfers between devices: 9.81 us -> 9.07 us
  Pallas kernels: 8.04 us -> 8.55 us
    ppermute x12, waiting for transfers between devices: 9.81 us -> 9.07 us  [swap(): return lax.ppermute(x, axis, [(i, i ^ mask) for i in range(size)])]
    pallas_call x1 -> x2, Pallas kernels: 1.85 us -> 2.39 us  [gradient(): pl.pallas_call(functools.partial(gradient_kernel, count, len(packets)), n...]
  transfers between devices with their start and end apart: 12 -> 12, of which waited for: 10 -> 10; matrix products, arithmetic and copies ran while one was open for 3% -> 3% of each run, Pallas kernels for 13% -> 15%
where the time goes in v7:
time: 32.1 us; the launch traced here: 31.9 us
  starting transfers between devices  12.7 us (40%)
  waiting for transfers between devices  9.07 us (28%)
  Pallas kernels  8.55 us (27%)
  other arithmetic  0.85 us (3%)
  between operations  0.69 us (2%)
    ppermute x12, starting transfers between devices, swap(): return lax.ppermute(x, axis, [(i, i ^ mask) for i in range(size)])  12.7 us
    ppermute x12, waiting for transfers between devices, swap(): return lax.ppermute(x, axis, [(i, i ^ mask) for i in range(size)])  9.07 us
    pallas_call x1, Pallas kernels, normalize(): pl.pallas_call(normalize_kernel, name='normalize', out_shape=(shape((lat_...  2.51 us
    pallas_call x2, Pallas kernels, gradient(): pl.pallas_call(functools.partial(gradient_kernel, count, len(packets)), n...  2.39 us
    pallas_call x1, Pallas kernels, forward(): pl.pallas_call(functools.partial(forward_kernel, rows_dev, top, len(units...  1.25 us
    pallas_call x1, Pallas kernels, side(): pl.pallas_call(functools.partial(side_kernel, rows_dev), name='side', out...  0.97 us
    select_n x1, other arithmetic, local(): jnp.where(lane < width, jnp.pad(inputs, ((0, 0), (0, LANES))), lists.asty...  0.84 us
    pallas_call x1, Pallas kernels, backward(): pl.pallas_call(functools.partial(backward_kernel, groups, rows_dev, len(t...  0.7 us
  transfers between devices with their start and end apart: 12, of which 10 were waited for; matrix products, arithmetic and copies ran while one was open for 3% of the time, Pallas kernels for 15%

profile of v7, /device:TPU:0, one launch (start us, length us, event | category | flops | bytes accessed | tf_op | source)
XLA Modules:
  0.0 31.9 jit_solution(7240594821278783675)
XLA Ops:
  0.6 0.5 %collective-permute-start.1 = (s32[2,4]{1,0:T(2,128)}, s32[2,4]{1,0:T(2,128)S(1)}, u32[]{:S(2)}, u32[]{:S(2)}) collective-permute-start(s32[2,4]{1,0:T(2,128)} %param.6), channel_id=1, source_target_pairs={{0,1},{1,0},{2,3},{3,2},{4,5},{5,4},{6,7},{7,6},{8,9},{9,8},{10,11... | collective-permute-start | bytes 104 | tf_op jit(solution)/shard_map/ppermute | solution.py:28
  1.1 0.1 collective-permute-start
  1.2 0.8 %broadcast_select_fusion.own_ref = bf16[2,2176]{1,0:T(2,128)(2,1)S(1)} fusion(pred[2176]{0:T(1024)(128)(4,1)S(1)} %get-tuple-element.46, s32[2,4]{1,0:T(2,128)} %param.6, pred[2176]{0:T(1024)(128)(4,1)S(1)} %get-tuple-element.45, bf16[2,2048]{1,0:T(2,128)(2,1)} %param.5), kind=kLoop, calls=%fused_computation.1 | loop fusion | flops 21760 | bytes 21280 | tf_op jit(solution)/shard_map/jit(_where)/select_n | solution.py:456
  2.1 0.1 collective-permute-done.1.mate_names_ref
  2.2 0.4 %collective-permute-done.mate_ref = bf16[2,2048]{1,0:T(2,128)(2,1)S(1)} collective-permute-done((bf16[2,2048]{1,0:T(2,128)(2,1)}, bf16[2,2048]{1,0:T(2,128)(2,1)S(1)}, u32[]{:S(2)}, u32[]{:S(2)}) %collective-permute-start) | collective-permute-done | bytes 8224 | tf_op jit(solution)/shard_map/ppermute | solution.py:28
  2.5 0.1 pack.1.after_ref.refs_2_
  2.6 0.0 copy-start.2
  2.6 3.7 %collective-permute-start.4 = (bf16[4,2176]{1,0:T(4,128)(2,1)S(1)}, bf16[4,2176]{1,0:T(4,128)(2,1)S(1)}, u32[]{:S(2)}, u32[]{:S(2)}) collective-permute-start(bf16[4,2176]{1,0:T(4,128)(2,1)S(1)} %pack.1.after_ref.refs_2_), channel_id=1, source_target_pairs={{0,6},{1,7},{2,4},{3,5},{4,2},{5,3},{6,0},{7,1},{8,14},{9,15},{10,... | collective-permute-start | bytes 52232 | tf_op jit(solution)/shard_map/ppermute | solution.py:28
  6.3 0.5 %collective-permute-start.3 = (bf16[4,2176]{1,0:T(4,128)(2,1)S(1)}, bf16[4,2176]{1,0:T(4,128)(2,1)S(1)}, u32[]{:S(2)}, u32[]{:S(2)}) collective-permute-start(bf16[4,2176]{1,0:T(4,128)(2,1)S(1)} %pack.1.after_ref.refs_2_), channel_id=1, source_target_pairs={{0,4},{1,5},{2,6},{3,7},{4,0},{5,1},{6,2},{7,3},{8,12},{9,13},{10,... | collective-permute-start | bytes 52232 | tf_op jit(solution)/shard_map/ppermute | solution.py:28
  6.8 0.1 collective-permute-start.2
  7.0 2.5 %normalize.1 = (bf16[1024,2048]{1,0:T(8,128)(2,1)S(1)}, bf16[2048,1024]{1,0:T(8,128)(2,1)S(1)}, f32[1024,128]{1,0:T(8,128)S(1)}) custom-call(bf16[4,2176]{1,0:T(4,128)(2,1)S(1)} %pack.1.after_ref.refs_2_, bf16[1024,2048]{1,0:T(8,128)(2,1)S(1)} %copy-done), custom_call_target="tpu_custom_call" | custom-call | flops 8388608 | bytes 12582912 | tf_op jit(solution)/shard_map/normalize/pallas_call | solution.py:108
  9.5 0.0 collective-permute-done.4.refs_5_
  9.5 0.6 %collective-permute-done.3.refs_4_ = bf16[4,2176]{1,0:T(4,128)(2,1)S(1)} collective-permute-done((bf16[4,2176]{1,0:T(4,128)(2,1)S(1)}, bf16[4,2176]{1,0:T(4,128)(2,1)S(1)}, u32[]{:S(2)}, u32[]{:S(2)}) %collective-permute-start.3) | collective-permute-done | bytes 17440 | tf_op jit(solution)/shard_map/ppermute | solution.py:28
  10.1 0.5 %collective-permute-done.2.refs_3_ = bf16[4,2176]{1,0:T(4,128)(2,1)S(1)} collective-permute-done((bf16[4,2176]{1,0:T(4,128)(2,1)S(1)}, bf16[4,2176]{1,0:T(4,128)(2,1)S(1)}, u32[]{:S(2)}, u32[]{:S(2)}) %collective-permute-start.2) | collective-permute-done | bytes 17440 | tf_op jit(solution)/shard_map/ppermute | solution.py:28
  10.6 1.3 %forward.1 = (f32[16,2048]{1,0:T(8,128)S(1)}, bf16[16,2048]{1,0:T(8,128)(2,1)S(1)}, bf16[16,2048]{1,0:T(8,128)(2,1)S(1)}, bf16[16,1024]{1,0:T(8,128)(2,1)S(1)}, ...) custom-call(f32[1,2048]{1,0:T(1,128)S(1)} %bitcast.2, f32[1,1024]{1,0:T(1,128)S(1)} %bitcast.4, ...), custom_call_target="tpu_custom_call" | custom-call | flops 134217728 | bytes 8388608 | tf_op jit(solution)/shard_map/forward/pallas_call | solution.py:171
  11.8 1.4 %collective-permute-done.5.mate_ref = f32[16,2048]{1,0:T(8,128)S(1)} collective-permute-done((f32[16,2048]{1,0:T(8,128)S(1)}, f32[16,2048]{1,0:T(8,128)S(1)}, u32[]{:S(2)}, u32[]{:S(2)}) %collective-permute-start.5) | collective-permute-done | bytes 131104 | tf_op jit(solution)/shard_map/ppermute | solution.py:28
  13.2 1.9 %collective-permute-start.8 = (bf16[16,2048]{1,0:T(8,128)(2,1)S(1)}, bf16[16,2048]{1,0:T(8,128)(2,1)S(1)}, u32[]{:S(2)}, u32[]{:S(2)}) collective-permute-start(bf16[16,2048]{1,0:T(8,128)(2,1)S(1)} %get-tuple-element.37), channel_id=1, source_target_pairs={{0,6},{1,7},{2,4},{3,5},{4,2},{5,3},{6,0},{7,1},{8,14},{9,15},{10,... | collective-permute-start | bytes 196616 | tf_op jit(solution)/shard_map/ppermute | solution.py:28
  15.1 0.5 %collective-permute-start.7 = (bf16[16,2048]{1,0:T(8,128)(2,1)S(1)}, bf16[16,2048]{1,0:T(8,128)(2,1)S(1)}, u32[]{:S(2)}, u32[]{:S(2)}) collective-permute-start(bf16[16,2048]{1,0:T(8,128)(2,1)S(1)} %get-tuple-element.37), channel_id=1, source_target_pairs={{0,4},{1,5},{2,6},{3,7},{4,0},{5,1},{6,2},{7,3},{8,12},{9,13},{10,... | collective-permute-start | bytes 196616 | tf_op jit(solution)/shard_map/ppermute | solution.py:28
  15.6 1.2 %collective-permute-start.6 = (bf16[16,2048]{1,0:T(8,128)(2,1)S(1)}, bf16[16,2048]{1,0:T(8,128)(2,1)S(1)}, u32[]{:S(2)}, u32[]{:S(2)}) collective-permute-start(bf16[16,2048]{1,0:T(8,128)(2,1)S(1)} %get-tuple-element.37), channel_id=1, source_target_pairs={{0,2},{1,3},{2,0},{3,1},{4,6},{5,7},{6,4},{7,5},{8,10},{9,11},{10,... | collective-permute-start | bytes 196616 | tf_op jit(solution)/shard_map/ppermute | solution.py:28
  16.8 1.0 %side.1 = (f32[16,16]{1,0:T(8,128)}, f32[16,1024]{1,0:T(8,128)S(1)}, f32[16,1024]{1,0:T(8,128)S(1)}, f32[4,1024]{1,0:T(4,128)S(1)}) custom-call(f32[16,1024]{1,0:T(8,128)S(1)} %get-tuple-element.29.act_ref, f32[16,1024]{1,0:T(8,128)S(1)} %get-tuple-element.30.hit_ref, bf16[16,1024]{1,0:T(8,128)(2,1)S(1)} %get-tuple-element.27.codes_ref.refs_2_, ...), custom_call_target="tpu_custom_call" | custom-call | flops 8388608 | bytes 524288 | tf_op jit(solution)/shard_map/side/pallas_call | solution.py:238
  17.7 0.8 %collective-permute-done.8.refs_12_ = bf16[16,2048]{1,0:T(8,128)(2,1)S(1)} collective-permute-done((bf16[16,2048]{1,0:T(8,128)(2,1)S(1)}, bf16[16,2048]{1,0:T(8,128)(2,1)S(1)}, u32[]{:S(2)}, u32[]{:S(2)}) %collective-permute-start.8) | collective-permute-done | bytes 65568 | tf_op jit(solution)/shard_map/ppermute | solution.py:28
  18.5 1.2 %collective-permute-done.7.refs_11_ = bf16[16,2048]{1,0:T(8,128)(2,1)S(1)} collective-permute-done((bf16[16,2048]{1,0:T(8,128)(2,1)S(1)}, bf16[16,2048]{1,0:T(8,128)(2,1)S(1)}, u32[]{:S(2)}, u32[]{:S(2)}) %collective-permute-start.7) | collective-permute-done | bytes 65568 | tf_op jit(solution)/shard_map/ppermute | solution.py:28
  19.7 0.1 collective-permute-done.6.refs_10_
  19.9 0.7 %backward.1 = (f32[2,2048]{1,0:T(2,128)S(1)}, bf16[48,512]{1,0:T(8,128)(2,1)S(1)}, bf16[48,512]{1,0:T(8,128)(2,1)S(1)}, bf16[48,512]{1,0:T(8,128)(2,1)S(1)}, bf16[48,512]{1,0:T(8,128)(2,1)S(1)}) custom-call(bf16[2048,1024]{1,0:T(8,128)(2,1)S(1)} %get-tuple-element.24.refs_1_.refs_0_, bf16[16,2048]{1,0:T(8,128)(2,1)S(1)} %get-tuple-element.26.refs_1_, ...), custom_call_target="tpu_custom_call" | custom-call | flops 67108864 | bytes 4194304 | tf_op jit(solution)/shard_map/backward/pallas_call | solution.py:334
  20.6 1.6 %collective-permute-start.10 = (bf16[48,512]{1,0:T(8,128)(2,1)S(1)}, bf16[48,512]{1,0:T(8,128)(2,1)S(1)}, u32[]{:S(2)}, u32[]{:S(2)}) collective-permute-start(bf16[48,512]{1,0:T(8,128)(2,1)S(1)} %get-tuple-element.42), channel_id=1, source_target_pairs={{0,8},{8,0},{16,24},{24,16},{1,9},{9,1},{17,25},{25,17},{2,10},{10... | collective-permute-start | bytes 147464 | tf_op jit(solution)/shard_map/ppermute | solution.py:28
  22.2 2.5 %collective-permute-start.11 = (bf16[48,512]{1,0:T(8,128)(2,1)S(1)}, bf16[48,512]{1,0:T(8,128)(2,1)S(1)}, u32[]{:S(2)}, u32[]{:S(2)}) collective-permute-start(bf16[48,512]{1,0:T(8,128)(2,1)S(1)} %get-tuple-element.43), channel_id=1, source_target_pairs={{0,24},{8,16},{16,8},{24,0},{1,25},{9,17},{17,9},{25,1},{2,26},{10... | collective-permute-start | bytes 147464 | tf_op jit(solution)/shard_map/ppermute | solution.py:28
  24.7 0.1 collective-permute-start.9
  24.8 0.6 %rounded.1 = bf16[2,2048]{1,0:T(2,128)(2,1)} custom-call(f32[2,2048]{1,0:T(2,128)S(1)} %get-tuple-element.38.value_ref), custom_call_target="tpu_custom_call" | custom-call | tf_op jit(solution)/shard_map/rounded/pallas_call | solution.py:353
  25.4 3.1 %collective-permute-done.11.refs_2_ = bf16[48,512]{1,0:T(8,128)(2,1)S(1)} collective-permute-done((bf16[48,512]{1,0:T(8,128)(2,1)S(1)}, bf16[48,512]{1,0:T(8,128)(2,1)S(1)}, u32[]{:S(2)}, u32[]{:S(2)}) %collective-permute-start.11) | collective-permute-done | bytes 49184 | tf_op jit(solution)/shard_map/ppermute | solution.py:28
  28.6 0.7 %early.1.refs_1_ = f32[1024,512]{1,0:T(8,128)S(1)} custom-call(bf16[1024,2048]{1,0:T(8,128)(2,1)S(1)} %get-tuple-element.25.refs_0_.unit_ref, f32[1024,128]{1,0:T(8,128)S(1)} %get-tuple-element.39.inverse_ref, bf16[48,512]{1,0:T(8,128)(2,1)S(1)} %get-tuple-element.41.refs_0_, bf16[48,512]{1,0:T(8,128)(2,1)S(1)} %collective-permute-done.10.refs_1_, ...), custom_call_target="tpu_custom_call" | custom-call | flops 100663296 | bytes 4194304 | tf_op jit(solution)/shard_map/early/pallas_call | solution.py:423
  29.3 0.9 %collective-permute-done.9.refs_0_ = bf16[48,512]{1,0:T(8,128)(2,1)S(1)} collective-permute-done((bf16[48,512]{1,0:T(8,128)(2,1)S(1)}, bf16[48,512]{1,0:T(8,128)(2,1)S(1)}, u32[]{:S(2)}, u32[]{:S(2)}) %collective-permute-start.9) | collective-permute-done | bytes 49184 | tf_op jit(solution)/shard_map/ppermute | solution.py:28
  30.2 1.7 %gradient.1 = f32[1024,512]{1,0:T(8,128)} custom-call(bf16[1024,2048]{1,0:T(8,128)(2,1)S(1)} %get-tuple-element.25.refs_0_.unit_ref, f32[1024,128]{1,0:T(8,128)S(1)} %get-tuple-element.39.inverse_ref, bf16[48,512]{1,0:T(8,128)(2,1)S(1)} %collective-permute-done.9.refs_0_, f32[1024,512]{1,0:T(8,128)S(1)} %early.1.refs_1_), custom_call_target="tpu_custom_call" | custom-call | flops 33554432 | bytes 4194304 | tf_op jit(solution)/shard_map/gradient/pallas_call | solution.py:423
  (9 shorter events, 0.1 us)
Async XLA Ops:
  0.6 1.5 %collective-permute-start.1 = (s32[2,4]{1,0:T(2,128)}, s32[2,4]{1,0:T(2,128)S(1)}, u32[]{:S(2)}, u32[]{:S(2)}) collective-permute-start(s32[2,4]{1,0:T(2,128)} %param.6), channel_id=1, source_target_pairs={{0,1},{1,0},{2,3},{3,2},{4,5},{5,4},{6,7},{7,6},{8,9},{9,8},{10,11... | collective-permute-start | bytes 104 | tf_op jit(solution)/shard_map/ppermute | solution.py:28
  1.1 1.4 %collective-permute-start = (bf16[2,2048]{1,0:T(2,128)(2,1)}, bf16[2,2048]{1,0:T(2,128)(2,1)S(1)}, u32[]{:S(2)}, u32[]{:S(2)}) collective-permute-start(bf16[2,2048]{1,0:T(2,128)(2,1)} %param.5), channel_id=1, source_target_pairs={{0,1},{1,0},{2,3},{3,2},{4,5},{5,4},{6,7},{7,6},{8,9},{9,8},{10,11... | collective-permute-start | bytes 24584 | tf_op jit(solution)/shard_map/ppermute | solution.py:28
  2.1 4.9 %copy-start = (bf16[1024,2048]{1,0:T(8,128)(2,1)S(1)}, bf16[1024,2048]{1,0:T(8,128)(2,1)}, u32[]{:S(2)}) copy-start(bf16[1024,2048]{1,0:T(8,128)(2,1)} %weights_ref.1) | copy-start | bytes 12582916
  2.6 8.0 %copy-start.1 = (f32[2048]{0:T(1024)S(1)}, f32[2048]{0:T(1024)}, u32[]{:S(2)}) copy-start(f32[2048]{0:T(1024)} %param.9) | copy-start | bytes 24580
  2.6 7.9 %copy-start.2 = (f32[1024]{0:T(1024)S(1)}, f32[1024]{0:T(1024)}, u32[]{:S(2)}) copy-start(f32[1024]{0:T(1024)} %param.8) | copy-start | bytes 12292
  2.6 6.8 %collective-permute-start.4 = (bf16[4,2176]{1,0:T(4,128)(2,1)S(1)}, bf16[4,2176]{1,0:T(4,128)(2,1)S(1)}, u32[]{:S(2)}, u32[]{:S(2)}) collective-permute-start(bf16[4,2176]{1,0:T(4,128)(2,1)S(1)} %pack.1.after_ref.refs_2_), channel_id=1, source_target_pairs={{0,6},{1,7},{2,4},{3,5},{4,2},{5,3},{6,0},{7,1},{8,14},{9,15},{10,... | collective-permute-start | bytes 52232 | tf_op jit(solution)/shard_map/ppermute | solution.py:28
  6.3 3.8 %collective-permute-start.3 = (bf16[4,2176]{1,0:T(4,128)(2,1)S(1)}, bf16[4,2176]{1,0:T(4,128)(2,1)S(1)}, u32[]{:S(2)}, u32[]{:S(2)}) collective-permute-start(bf16[4,2176]{1,0:T(4,128)(2,1)S(1)} %pack.1.after_ref.refs_2_), channel_id=1, source_target_pairs={{0,4},{1,5},{2,6},{3,7},{4,0},{5,1},{6,2},{7,3},{8,12},{9,13},{10,... | collective-permute-start | bytes 52232 | tf_op jit(solution)/shard_map/ppermute | solution.py:28
  6.8 3.8 %collective-permute-start.2 = (bf16[4,2176]{1,0:T(4,128)(2,1)S(1)}, bf16[4,2176]{1,0:T(4,128)(2,1)S(1)}, u32[]{:S(2)}, u32[]{:S(2)}) collective-permute-start(bf16[4,2176]{1,0:T(4,128)(2,1)S(1)} %pack.1.after_ref.refs_2_), channel_id=1, source_target_pairs={{0,2},{1,3},{2,0},{3,1},{4,6},{5,7},{6,4},{7,5},{8,10},{9,11},{10,... | collective-permute-start | bytes 52232 | tf_op jit(solution)/shard_map/ppermute | solution.py:28
  11.8 1.4 %collective-permute-start.5 = (f32[16,2048]{1,0:T(8,128)S(1)}, f32[16,2048]{1,0:T(8,128)S(1)}, u32[]{:S(2)}, u32[]{:S(2)}) collective-permute-start(f32[16,2048]{1,0:T(8,128)S(1)} %get-tuple-element.35.mine_ref), channel_id=1, source_target_pairs={{0,1},{1,0},{2,3},{3,2},{4,5},{5,4},{6,7},{7,6},{8,9},{9,8},{10,11... | collective-permute-start | bytes 393224 | tf_op jit(solution)/shard_map/ppermute | solution.py:28
  13.2 5.3 %collective-permute-start.8 = (bf16[16,2048]{1,0:T(8,128)(2,1)S(1)}, bf16[16,2048]{1,0:T(8,128)(2,1)S(1)}, u32[]{:S(2)}, u32[]{:S(2)}) collective-permute-start(bf16[16,2048]{1,0:T(8,128)(2,1)S(1)} %get-tuple-element.37), channel_id=1, source_target_pairs={{0,6},{1,7},{2,4},{3,5},{4,2},{5,3},{6,0},{7,1},{8,14},{9,15},{10,... | collective-permute-start | bytes 196616 | tf_op jit(solution)/shard_map/ppermute | solution.py:28
  15.1 4.6 %collective-permute-start.7 = (bf16[16,2048]{1,0:T(8,128)(2,1)S(1)}, bf16[16,2048]{1,0:T(8,128)(2,1)S(1)}, u32[]{:S(2)}, u32[]{:S(2)}) collective-permute-start(bf16[16,2048]{1,0:T(8,128)(2,1)S(1)} %get-tuple-element.37), channel_id=1, source_target_pairs={{0,4},{1,5},{2,6},{3,7},{4,0},{5,1},{6,2},{7,3},{8,12},{9,13},{10,... | collective-permute-start | bytes 196616 | tf_op jit(solution)/shard_map/ppermute | solution.py:28
  15.6 4.3 %collective-permute-start.6 = (bf16[16,2048]{1,0:T(8,128)(2,1)S(1)}, bf16[16,2048]{1,0:T(8,128)(2,1)S(1)}, u32[]{:S(2)}, u32[]{:S(2)}) collective-permute-start(bf16[16,2048]{1,0:T(8,128)(2,1)S(1)} %get-tuple-element.37), channel_id=1, source_target_pairs={{0,2},{1,3},{2,0},{3,1},{4,6},{5,7},{6,4},{7,5},{8,10},{9,11},{10,... | collective-permute-start | bytes 196616 | tf_op jit(solution)/shard_map/ppermute | solution.py:28
  20.6 4.9 %collective-permute-start.10 = (bf16[48,512]{1,0:T(8,128)(2,1)S(1)}, bf16[48,512]{1,0:T(8,128)(2,1)S(1)}, u32[]{:S(2)}, u32[]{:S(2)}) collective-permute-start(bf16[48,512]{1,0:T(8,128)(2,1)S(1)} %get-tuple-element.42), channel_id=1, source_target_pairs={{0,8},{8,0},{16,24},{24,16},{1,9},{9,1},{17,25},{25,17},{2,10},{10... | collective-permute-start | bytes 147464 | tf_op jit(solution)/shard_map/ppermute | solution.py:28
  22.2 6.3 %collective-permute-start.11 = (bf16[48,512]{1,0:T(8,128)(2,1)S(1)}, bf16[48,512]{1,0:T(8,128)(2,1)S(1)}, u32[]{:S(2)}, u32[]{:S(2)}) collective-permute-start(bf16[48,512]{1,0:T(8,128)(2,1)S(1)} %get-tuple-element.43), channel_id=1, source_target_pairs={{0,24},{8,16},{16,8},{24,0},{1,25},{9,17},{17,9},{25,1},{2,26},{10... | collective-permute-start | bytes 147464 | tf_op jit(solution)/shard_map/ppermute | solution.py:28
  24.7 5.5 %collective-permute-start.9 = (bf16[48,512]{1,0:T(8,128)(2,1)S(1)}, bf16[48,512]{1,0:T(8,128)(2,1)S(1)}, u32[]{:S(2)}, u32[]{:S(2)}) collective-permute-start(bf16[48,512]{1,0:T(8,128)(2,1)S(1)} %get-tuple-element.40), channel_id=1, source_target_pairs={{0,16},{8,24},{16,0},{24,8},{1,17},{9,25},{17,1},{25,9},{2,18},{10... | collective-permute-start | bytes 147464 | tf_op jit(solution)/shard_map/ppermute | solution.py:28

commit v8 on v7

--- a/solution.py
+++ b/solution.py
@@ -13,9 +13,9 @@
 RADIX = 1 << SHIFT
 LANES = 128
 DIRECT = 4
-TERMS = 8
+TERMS = 4
 ORDER = (0, 1, 2, 3)
-LATE = 2
+LATE = 1
 VMEM = pl.BlockSpec(memory_space=pltpu.VMEM)
 HBM = pl.BlockSpec(memory_space=pltpu.MemorySpace.HBM)
 ANY = pl.BlockSpec(memory_space=pl.ANY)
@@ -192,8 +192,61 @@
     )(dec, enc, *units, *turneds, *taken(ORDER, pieces))
 
 
-def side_kernel(rows_dev, act_ref, hit_ref, codes_ref, base_ref, enc_ref, *outs):
-    scores_ref, gate_ref, second_ref, compact_ref = outs
+def side_kernel(groups, hit_ref, codes_ref, base_ref, enc_ref, cent_ref, *outs):
+    gate_ref, second_ref, packets = outs[0], outs[1], outs[2:]
+    count, lat_rows = hit_ref.shape
+    hit = hit_ref[...]
+    preact = base_ref[...] + enc_ref[...]
+    gate_ref[...] = hit * jax.nn.sigmoid(preact)
+    at = lax.broadcasted_iota(jnp.int32, (count, count), 0)
+    place = lax.broadcasted_iota(jnp.int32, (count, count), 1)
+    earlier = jnp.where(place < at, 1.0, 0.0).astype(BF16)
+    before = jnp.dot(earlier, hit.astype(BF16), preferred_element_type=F32)
+    second = jnp.where(before == 1.0, hit, 0.0)
+    first = jnp.where(before == 0.0, hit, 0.0)
+    second_ref[...] = second
+    codes = codes_ref[...].astype(F32)
+    number = (lax.broadcasted_iota(jnp.int32, (count, lat_rows), 0) + 1).astype(F32)
+    terms = [jnp.sum(slot * codes, axis=0, keepdims=True) for slot in (first, second)]
+    terms += [jnp.sum(slot * number, axis=0, keepdims=True) for slot in (first, second)]
+    fill(groups, packets, cent_ref, jnp.concatenate(terms, axis=0))
+
+
+def fill(groups, packets, rows_ref, terms):
+    count, width = rows_ref.shape
+    cols = width // groups
+    group = lax.axis_index("dp")
+    parts = [terms[:, at : at + cols] for at in range(0, terms.shape[1], cols)]
+    terms = jnp.concatenate(parts, axis=0).astype(BF16)
+    for k, packet in enumerate(packets):
+        at = pl.ds(pl.multiple_of((group ^ k) * cols, LANES), cols)
+        packet[:count, :] = rows_ref[:, at]
+        packet[count:, :] = terms
+
+
+def packet_shape(groups, cent, lat_rows):
+    cols = cent.shape[1] // groups
+    return shape((cent.shape[0] + TERMS * lat_rows // cols, cols), BF16)
+
+
+def side(groups, hit, codes, base, enc, cent):
+    count, lat_rows = hit.shape
+    return pl.pallas_call(
+        functools.partial(side_kernel, groups),
+        name="side",
+        out_shape=(shape((count, lat_rows), F32),) * 2
+        + (packet_shape(groups, cent, lat_rows),) * groups,
+        in_specs=[VMEM] * 5,
+        out_specs=(VMEM,) * (2 + groups),
+        compiler_params=params(20),
+        cost_estimate=pl.CostEstimate(
+            flops=8 * count * lat_rows * 64, bytes_accessed=32 * count * lat_rows, transcendentals=0
+        ),
+    )(hit, codes, base, enc, cent)
+
+
+def scores_kernel(rows_dev, act_ref, scores_ref, token_ref):
+    token_ref[...] = jnp.zeros_like(token_ref)
     count, lat_rows = act_ref.shape
     block_count = lat_rows // BLK
     me = lax.axis_index("latent")
@@ -214,43 +267,18 @@
     scores_ref[...] = jnp.dot(
         means, order, preferred_element_type=F32, precision=lax.Precision.HIGHEST
     )
-    hit = hit_ref[...]
-    preact = base_ref[...] + enc_ref[...]
-    gate_ref[...] = hit * jax.nn.sigmoid(preact)
-    earlier = jnp.where(place < at, 1.0, 0.0).astype(BF16)
-    before = jnp.dot(earlier, hit.astype(BF16), preferred_element_type=F32)
-    second = jnp.where(before == 1.0, hit, 0.0)
-    first = jnp.where(before == 0.0, hit, 0.0)
-    second_ref[...] = second
-    codes = codes_ref[...].astype(F32)
-    number = (lax.broadcasted_iota(jnp.int32, (count, lat_rows), 0) + 1).astype(F32)
-    rows = []
-    for slot in (first, second):
-        rows.append(jnp.sum(slot * codes, axis=0, keepdims=True))
-    for slot in (first, second):
-        rows.append(jnp.sum(slot * number, axis=0, keepdims=True))
-    for at, row in enumerate(rows):
-        compact_ref[at : at + 1, :] = row
-
-
-def side(rows_dev, act, hit, codes, base, enc):
+
+
+def scores(rows_dev, act):
     count, lat_rows = act.shape
     return pl.pallas_call(
-        functools.partial(side_kernel, rows_dev),
-        name="side",
-        out_shape=(
-            shape((lat_rows // BLK, count), F32),
-            shape((count, lat_rows), F32),
-            shape((count, lat_rows), F32),
-            shape((2 * CAP, lat_rows), F32),
-        ),
-        in_specs=[VMEM] * 5,
-        out_specs=(VMEM,) * 4,
-        compiler_params=params(20),
-        cost_estimate=pl.CostEstimate(
-            flops=8 * count * lat_rows * 64, bytes_accessed=32 * count * lat_rows, transcendentals=0
-        ),
-    )(act, hit, codes, base, enc)
+        functools.partial(scores_kernel, rows_dev),
+        name="scores",
+        out_shape=(shape((lat_rows // BLK, count), F32), shape((8, LANES), F32)),
+        in_specs=[VMEM],
+        out_specs=(VMEM, VMEM),
+        compiler_params=params(8),
+    )(act)
 
 
 def exchanged(value, step, mask):
@@ -260,21 +288,22 @@
     )
 
 
-def combine_kernel(rows_dev, mine_ref, mate_ref, sums_ref, sent_ref):
+def combine_kernel(rows_dev, mine_ref, mate_ref, after_ref, sums_ref, sent_ref):
+    del after_ref
     sums = mine_ref[...] + exchanged(mate_ref[...], rows_dev, 1)
     sums_ref[...] = sums
     sent_ref[...] = sums.astype(BF16)
 
 
-def combine(rows_dev, mine, mate):
+def combine(rows_dev, mine, mate, after):
     return pl.pallas_call(
         functools.partial(combine_kernel, rows_dev),
         name="combine",
         out_shape=(shape(mine.shape, F32), shape(mine.shape, BF16)),
-        in_specs=[VMEM] * 2,
+        in_specs=[VMEM, VMEM, ANY],
         out_specs=(VMEM, VMEM),
         compiler_params=params(12),
-    )(mine, mate)
+    )(mine, mate, after)
 
 
 def errors_kernel(rows_dev, dec_ref, input_ref, parts, recon_ref, errors_ref):
@@ -290,18 +319,15 @@
     turneds, refs = refs[:splits], refs[splits:]
     cent_ref, codes_ref, base_ref, gate_ref = refs[:4]
     refs = refs[4:]
-    second_ref, compact_ref = refs[:2]
+    second_ref = refs[0]
     if rows_dev:
         chips = cent_ref.shape[0] // (2 * rows_dev)
-        dec_ref, input_ref = refs[2:4]
-        parts, outs = restored(ORDER, refs[4 : 4 + chips]), refs[4 + chips :]
+        dec_ref, input_ref = refs[1:3]
+        parts, outs = restored(ORDER, refs[3 : 3 + chips]), refs[3 + chips :]
         recon_ref, packets, errors_ref = outs[0], outs[1:-1], outs[-1]
         errors_kernel(rows_dev, dec_ref, input_ref, parts, recon_ref, errors_ref)
     else:
-        errors_ref, packets = refs[2], refs[3:]
-    count, width = cent_ref.shape
-    lat_rows = codes_ref.shape[1]
-    cols = width // groups
+        errors_ref, packets = refs[1], refs[2:]
     grad = times(errors_ref[...], turneds)
     pre_grad = (grad * gate_ref[...]).astype(BF16).astype(F32)
     codes = codes_ref[...].astype(F32)
@@ -309,23 +335,14 @@
     high = along.astype(BF16).astype(F32)
     both = jnp.sum(pre_grad, axis=0, keepdims=True)
     later = jnp.sum(pre_grad * second_ref[...], axis=0, keepdims=True)
-    table = compact_ref[...]
-    terms = jnp.concatenate([table, both - later, later, high, along - high], axis=0).astype(BF16)
-    group = lax.axis_index("dp")
-    for k, packet in enumerate(packets):
-        at = pl.ds(pl.multiple_of((group ^ k) * cols, LANES), cols)
-        packet[:count, :] = errors_ref[:, at]
-        packet[count : 2 * count, :] = cent_ref[:, at]
-        for part in range(lat_rows // cols):
-            rows = pl.ds(2 * count + part * TERMS, TERMS)
-            packet[rows, :] = terms[:, part * cols : (part + 1) * cols]
+    terms = jnp.concatenate([both - later, later, high, along - high], axis=0)
+    fill(groups, packets, errors_ref, terms)
 
 
 def backward(groups, rows_dev, turneds, cent, rest):
     count, width = cent.shape
     lat_rows = rest[0].shape[1]
-    cols = width // groups
-    packet = shape((2 * count + TERMS * lat_rows // cols, cols), BF16)
+    packet = packet_shape(groups, cent, lat_rows)
     outs = (packet,) * groups
     scratch = []
     if rows_dev:
@@ -362,27 +379,24 @@
 
 def gradient_kernel(count, given, unit_ref, inverse_ref, *refs):
     out_ref, left_ref, right_ref, held_ref, sems = refs[-5:]
-    packets, before_refs = refs[:given], refs[given:-5]
+    sides, packets, before_refs = refs[:given], refs[given : 2 * given], refs[2 * given : -5]
     lat_rows, cols = out_ref.shape
     depth = 2 * count * len(packets)
     extra = left_ref.shape[0] - depth
     along = []
     number = (lax.broadcasted_iota(jnp.int32, (count, lat_rows), 0) + 1).astype(F32)
-    for g, packet in enumerate(packets):
+    for g, (known, packet) in enumerate(zip(sides, packets)):
         base = g * 2 * count
-        right_ref[base : base + 2 * count, :cols] = packet[: 2 * count, :]
-        parts = [
-            packet[2 * count + p * TERMS : 2 * count + (p + 1) * TERMS, :].astype(F32)
-            for p in range(lat_rows // cols)
-        ]
-        terms = jnp.concatenate(parts, axis=1)
-        code0, code1, row0, row1, grad0, grad1 = [terms[t : t + 1] for t in range(TERMS - 2)]
+        right_ref[base : base + count, :cols] = packet[:count, :]
+        right_ref[base + count : base + 2 * count, :cols] = known[:count, :]
+        code0, code1, row0, row1 = unfilled(known, count)
+        grad0, grad1, *shares = unfilled(packet, count)
         at0, at1 = number == row0, number == row1
         code = jnp.where(at0, code0, jnp.where(at1, code1, 0.0))
         grad = jnp.where(at0, grad0, jnp.where(at1, grad1, 0.0))
         left_ref[base : base + count, :] = code.astype(BF16)
         left_ref[base + count : base + 2 * count, :] = grad.astype(BF16)
-        along.append(terms[TERMS - 2 :])
+        along += shares
     if extra > 2 * len(packets):
         along.append(jnp.zeros((extra - 2 * len(packets), lat_rows), F32))
     left_ref[depth:, :] = jnp.concatenate(along, axis=0).astype(BF16)
@@ -415,7 +429,14 @@
         copy.wait()
 
 
-def gradient(name, count, unit, inverse, packets, before):
+def unfilled(packet, count):
+    values = packet[count:, :].astype(F32)
+    parts = [values[at : at + TERMS] for at in range(0, values.shape[0], TERMS)]
+    terms = jnp.concatenate(parts, axis=1)
+    return [terms[t : t + 1] for t in range(TERMS)]
+
+
+def gradient(name, count, unit, inverse, sides, packets, before):
     lat_rows = unit.shape[0]
     cols = packets[0].shape[1]
     depth = 2 * count * len(packets)
@@ -424,7 +445,7 @@
         functools.partial(gradient_kernel, count, len(packets)),
         name=name,
         out_shape=shape((lat_rows, cols), F32),
-        in_specs=[VMEM] * (2 + len(packets) + len(before)),
+        in_specs=[VMEM] * (2 + 2 * len(packets) + len(before)),
         out_specs=HBM if before else VMEM,
         scratch_shapes=[
             pltpu.VMEM((rows, lat_rows), BF16),
@@ -436,7 +457,7 @@
         cost_estimate=pl.CostEstimate(
             flops=2 * depth * lat_rows * cols, bytes_accessed=8 * lat_rows * cols, transcendentals=0
         ),
-    )(unit, inverse, *packets, *before)
+    )(unit, inverse, *sides, *packets, *before)
 
 
 def local(inputs, blocks, weights, enc_bias, dec_bias):
@@ -461,9 +482,11 @@
     contrib, cent, rows, codes, base, act, hit = forward(
         rows_dev, top, dec, enc, units, turneds, pieces
     )
-    sums, sent = combine(rows_dev, contrib, swap(contrib, "latent", 1))
-    block_scores, gate, second, compact = side(rows_dev, act, hit, codes, base, enc)
-    known = (codes, base, gate, second, compact)
+    block_scores, token = scores(rows_dev, act)
+    sums, sent = combine(rows_dev, contrib, swap(contrib, "latent", 1), token)
+    gate, second, *sides = side(groups, hit, codes, base, enc, cent)
+    sides = swaps(sides, "dp", 1)
+    known = (codes, base, gate, second)
     if chips <= DIRECT:
         parts = [sums] + swaps([sent] * chips, "latent", 2)[1:]
         recon, *packets = backward(
@@ -481,9 +504,13 @@
         packets = backward(groups, 0, turneds, cent, (*known, errors))
     packets = swaps(packets, "dp", 1)
     late = LATE if groups == len(ORDER) else groups - 1
-    early = [p for k, p in enumerate(packets) if k != late]
-    partial = gradient("early", count, unit, inverse, early, [])
-    grad_weights = gradient("gradient", count, unit, inverse, [packets[late]], [partial])
+    early = [k for k in range(groups) if k != late]
+    partial = gradient(
+        "early", count, unit, inverse, [sides[k] for k in early], [packets[k] for k in early], []
+    )
+    grad_weights = gradient(
+        "gradient", count, unit, inverse, [sides[late]], [packets[late]], [partial]
+    )
     return (rounded(recon), grad_weights, block_scores)
 
 

time: 32.1 us -> 31.7 us (0.988)
  waiting for transfers between devices: 9.07 us -> 3.8 us
  starting transfers between devices: 12.7 us -> 17.4 us
    ppermute x12 -> x15, waiting for transfers between devices: 9.07 us -> 3.8 us  [swap(): return lax.ppermute(x, axis, [(i, i ^ mask) for i in range(size)])]
    ppermute x12 -> x15, starting transfers between devices: 12.7 us -> 17.4 us  [swap(): return lax.ppermute(x, axis, [(i, i ^ mask) for i in range(size)])]
    pallas_call x1 -> x2, Pallas kernels: 0.97 us -> 1.15 us  [the longest x1 0.97 us: scores(): pl.pallas_call(functools.partial(scores_kernel, rows_dev), name='scores',...]
  transfers between devices with their start and end apart: 12 -> 15, of which waited for: 10 -> 6; matrix products, arithmetic and copies ran while one was open for 3% -> 3% of each run, Pallas kernels for 15% -> 18%
where the time goes in v8:
time: 31.7 us; the launch traced here: 31.5 us
  starting transfers between devices  17.4 us (55%)
  Pallas kernels  8.74 us (28%)
  waiting for transfers between devices  3.8 us (12%)
  other arithmetic  0.85 us (3%)
  between operations  0.72 us (2%)
    ppermute x15, starting transfers between devices, swap(): return lax.ppermute(x, axis, [(i, i ^ mask) for i in range(size)])  17.4 us
    ppermute x15, waiting for transfers between devices, swap(): return lax.ppermute(x, axis, [(i, i ^ mask) for i in range(size)])  3.8 us
    pallas_call x1, Pallas kernels, normalize(): pl.pallas_call(normalize_kernel, name='normalize', out_shape=(shape((lat_...  2.51 us
    pallas_call x2, Pallas kernels, gradient(): pl.pallas_call(functools.partial(gradient_kernel, count, len(packets)), n...  2.39 us
    pallas_call x1, Pallas kernels, forward(): pl.pallas_call(functools.partial(forward_kernel, rows_dev, top, len(units...  1.26 us
    pallas_call x1, Pallas kernels, scores(): pl.pallas_call(functools.partial(scores_kernel, rows_dev), name='scores',...  0.97 us
    select_n x1, other arithmetic, local(): jnp.where(lane < width, jnp.pad(inputs, ((0, 0), (0, LANES))), lists.asty...  0.84 us
    pallas_call x1, Pallas kernels, backward(): pl.pallas_call(functools.partial(backward_kernel, groups, rows_dev, len(t...  0.71 us
  transfers between devices with their start and end apart: 15, of which 6 were waited for; matrix products, arithmetic and copies ran while one was open for 3% of the time, Pallas kernels for 18%

profile of v8, /device:TPU:0, one launch (start us, length us, event | category | flops | bytes accessed | tf_op | source)
XLA Modules:
  0.0 31.5 jit_solution(17660691947557828555)
XLA Ops:
  0.6 0.5 %collective-permute-start.1 = (s32[2,4]{1,0:T(2,128)}, s32[2,4]{1,0:T(2,128)S(1)}, u32[]{:S(2)}, u32[]{:S(2)}) collective-permute-start(s32[2,4]{1,0:T(2,128)} %param.6), channel_id=1, source_target_pairs={{0,1},{1,0},{2,3},{3,2},{4,5},{5,4},{6,7},{7,6},{8,9},{9,8},{10,11... | collective-permute-start | bytes 104 | tf_op jit(solution)/shard_map/ppermute | solution.py:28
  1.1 0.1 collective-permute-start
  1.2 0.8 %broadcast_select_fusion.own_ref = bf16[2,2176]{1,0:T(2,128)(2,1)S(1)} fusion(pred[2176]{0:T(1024)(128)(4,1)S(1)} %get-tuple-element.54, s32[2,4]{1,0:T(2,128)} %param.6, pred[2176]{0:T(1024)(128)(4,1)S(1)} %get-tuple-element.53, bf16[2,2048]{1,0:T(2,128)(2,1)} %param.5), kind=kLoop, calls=%fused_computation.1 | loop fusion | flops 21760 | bytes 21280 | tf_op jit(solution)/shard_map/jit(_where)/select_n | solution.py:477
  2.1 0.1 collective-permute-done.1.mate_names_ref
  2.2 0.4 %collective-permute-done.mate_ref = bf16[2,2048]{1,0:T(2,128)(2,1)S(1)} collective-permute-done((bf16[2,2048]{1,0:T(2,128)(2,1)}, bf16[2,2048]{1,0:T(2,128)(2,1)S(1)}, u32[]{:S(2)}, u32[]{:S(2)}) %collective-permute-start) | collective-permute-done | bytes 8224 | tf_op jit(solution)/shard_map/ppermute | solution.py:28
  2.5 0.1 pack.1.after_ref.refs_2_
  2.6 0.0 copy-start.2
  2.6 3.7 %collective-permute-start.4 = (bf16[4,2176]{1,0:T(4,128)(2,1)S(1)}, bf16[4,2176]{1,0:T(4,128)(2,1)S(1)}, u32[]{:S(2)}, u32[]{:S(2)}) collective-permute-start(bf16[4,2176]{1,0:T(4,128)(2,1)S(1)} %pack.1.after_ref.refs_2_), channel_id=1, source_target_pairs={{0,6},{1,7},{2,4},{3,5},{4,2},{5,3},{6,0},{7,1},{8,14},{9,15},{10,... | collective-permute-start | bytes 52232 | tf_op jit(solution)/shard_map/ppermute | solution.py:28
  6.3 0.5 %collective-permute-start.3 = (bf16[4,2176]{1,0:T(4,128)(2,1)S(1)}, bf16[4,2176]{1,0:T(4,128)(2,1)S(1)}, u32[]{:S(2)}, u32[]{:S(2)}) collective-permute-start(bf16[4,2176]{1,0:T(4,128)(2,1)S(1)} %pack.1.after_ref.refs_2_), channel_id=1, source_target_pairs={{0,4},{1,5},{2,6},{3,7},{4,0},{5,1},{6,2},{7,3},{8,12},{9,13},{10,... | collective-permute-start | bytes 52232 | tf_op jit(solution)/shard_map/ppermute | solution.py:28
  6.8 0.1 collective-permute-start.2
  7.0 2.5 %normalize.1 = (bf16[1024,2048]{1,0:T(8,128)(2,1)S(1)}, bf16[2048,1024]{1,0:T(8,128)(2,1)S(1)}, f32[1024,128]{1,0:T(8,128)S(1)}) custom-call(bf16[4,2176]{1,0:T(4,128)(2,1)S(1)} %pack.1.after_ref.refs_2_, bf16[1024,2048]{1,0:T(8,128)(2,1)S(1)} %copy-done), custom_call_target="tpu_custom_call" | custom-call | flops 8388608 | bytes 12582912 | tf_op jit(solution)/shard_map/normalize/pallas_call | solution.py:108
  9.5 0.0 collective-permute-done.4.refs_5_
  9.5 0.6 %collective-permute-done.3.refs_4_ = bf16[4,2176]{1,0:T(4,128)(2,1)S(1)} collective-permute-done((bf16[4,2176]{1,0:T(4,128)(2,1)S(1)}, bf16[4,2176]{1,0:T(4,128)(2,1)S(1)}, u32[]{:S(2)}, u32[]{:S(2)}) %collective-permute-start.3) | collective-permute-done | bytes 17440 | tf_op jit(solution)/shard_map/ppermute | solution.py:28
  10.1 0.5 %collective-permute-done.2.refs_3_ = bf16[4,2176]{1,0:T(4,128)(2,1)S(1)} collective-permute-done((bf16[4,2176]{1,0:T(4,128)(2,1)S(1)}, bf16[4,2176]{1,0:T(4,128)(2,1)S(1)}, u32[]{:S(2)}, u32[]{:S(2)}) %collective-permute-start.2) | collective-permute-done | bytes 17440 | tf_op jit(solution)/shard_map/ppermute | solution.py:28
  10.6 1.3 %forward.1 = (f32[16,2048]{1,0:T(8,128)S(1)}, bf16[16,2048]{1,0:T(8,128)(2,1)S(1)}, bf16[16,2048]{1,0:T(8,128)(2,1)S(1)}, bf16[16,1024]{1,0:T(8,128)(2,1)S(1)}, ...) custom-call(f32[1,2048]{1,0:T(1,128)S(1)} %bitcast.2, f32[1,1024]{1,0:T(1,128)S(1)} %bitcast.4, ...), custom_call_target="tpu_custom_call" | custom-call | flops 134217728 | bytes 8388608 | tf_op jit(solution)/shard_map/forward/pallas_call | solution.py:171
  11.8 1.0 %scores.1 = (f32[16,16]{1,0:T(8,128)}, f32[8,128]{1,0:T(8,128)S(1)}) custom-call(f32[16,1024]{1,0:T(8,128)S(1)} %get-tuple-element.38.act_ref), custom_call_target="tpu_custom_call" | custom-call | tf_op jit(solution)/shard_map/scores/pallas_call | solution.py:274
  12.8 0.4 %collective-permute-done.5.mate_ref = f32[16,2048]{1,0:T(8,128)S(1)} collective-permute-done((f32[16,2048]{1,0:T(8,128)S(1)}, f32[16,2048]{1,0:T(8,128)S(1)}, u32[]{:S(2)}, u32[]{:S(2)}) %collective-permute-start.5) | collective-permute-done | bytes 131104 | tf_op jit(solution)/shard_map/ppermute | solution.py:28
  13.2 1.9 %collective-permute-start.8 = (bf16[16,2048]{1,0:T(8,128)(2,1)S(1)}, bf16[16,2048]{1,0:T(8,128)(2,1)S(1)}, u32[]{:S(2)}, u32[]{:S(2)}) collective-permute-start(bf16[16,2048]{1,0:T(8,128)(2,1)S(1)} %get-tuple-element.41), channel_id=1, source_target_pairs={{0,6},{1,7},{2,4},{3,5},{4,2},{5,3},{6,0},{7,1},{8,14},{9,15},{10,... | collective-permute-start | bytes 196616 | tf_op jit(solution)/shard_map/ppermute | solution.py:28
  15.1 0.5 %collective-permute-start.7 = (bf16[16,2048]{1,0:T(8,128)(2,1)S(1)}, bf16[16,2048]{1,0:T(8,128)(2,1)S(1)}, u32[]{:S(2)}, u32[]{:S(2)}) collective-permute-start(bf16[16,2048]{1,0:T(8,128)(2,1)S(1)} %get-tuple-element.41), channel_id=1, source_target_pairs={{0,4},{1,5},{2,6},{3,7},{4,0},{5,1},{6,2},{7,3},{8,12},{9,13},{10,... | collective-permute-start | bytes 196616 | tf_op jit(solution)/shard_map/ppermute | solution.py:28
  15.6 1.2 %collective-permute-start.6 = (bf16[16,2048]{1,0:T(8,128)(2,1)S(1)}, bf16[16,2048]{1,0:T(8,128)(2,1)S(1)}, u32[]{:S(2)}, u32[]{:S(2)}) collective-permute-start(bf16[16,2048]{1,0:T(8,128)(2,1)S(1)} %get-tuple-element.41), channel_id=1, source_target_pairs={{0,2},{1,3},{2,0},{3,1},{4,6},{5,7},{6,4},{7,5},{8,10},{9,11},{10,... | collective-permute-start | bytes 196616 | tf_op jit(solution)/shard_map/ppermute | solution.py:28
  16.8 0.2 side.1
  17.0 2.7 %collective-permute-start.11 = (bf16[24,512]{1,0:T(8,128)(2,1)S(1)}, bf16[24,512]{1,0:T(8,128)(2,1)S(1)}, u32[]{:S(2)}, u32[]{:S(2)}) collective-permute-start(bf16[24,512]{1,0:T(8,128)(2,1)S(1)} %get-tuple-element.47), channel_id=1, source_target_pairs={{0,16},{8,24},{16,0},{24,8},{1,17},{9,25},{17,1},{25,9},{2,18},{10... | collective-permute-start | bytes 73736 | tf_op jit(solution)/shard_map/ppermute | solution.py:28
  19.6 1.3 %collective-permute-start.12 = (bf16[24,512]{1,0:T(8,128)(2,1)S(1)}, bf16[24,512]{1,0:T(8,128)(2,1)S(1)}, u32[]{:S(2)}, u32[]{:S(2)}) collective-permute-start(bf16[24,512]{1,0:T(8,128)(2,1)S(1)} %get-tuple-element.48), channel_id=1, source_target_pairs={{0,24},{8,16},{16,8},{24,0},{1,25},{9,17},{17,9},{25,1},{2,26},{10... | collective-permute-start | bytes 73736 | tf_op jit(solution)/shard_map/ppermute | solution.py:28
  21.0 0.7 %backward.1 = (f32[2,2048]{1,0:T(2,128)S(1)}, bf16[24,512]{1,0:T(8,128)(2,1)S(1)}, bf16[24,512]{1,0:T(8,128)(2,1)S(1)}, bf16[24,512]{1,0:T(8,128)(2,1)S(1)}, bf16[24,512]{1,0:T(8,128)(2,1)S(1)}) custom-call(bf16[2048,1024]{1,0:T(8,128)(2,1)S(1)} %get-tuple-element.28.refs_1_.refs_0_, bf16[16,2048]{1,0:T(8,128)(2,1)S(1)} %get-tuple-element.30.cent_ref.refs_1_, ...), custom_call_target="tpu_custom_call" | custom-call | flops 67108864 | bytes 4194304 | tf_op jit(solution)/shard_map/backward/pallas_call | solution.py:351
  21.7 1.8 %collective-permute-start.13 = (bf16[24,512]{1,0:T(8,128)(2,1)S(1)}, bf16[24,512]{1,0:T(8,128)(2,1)S(1)}, u32[]{:S(2)}, u32[]{:S(2)}) collective-permute-start(bf16[24,512]{1,0:T(8,128)(2,1)S(1)} %get-tuple-element.50), channel_id=1, source_target_pairs={{0,16},{8,24},{16,0},{24,8},{1,17},{9,25},{17,1},{25,9},{2,18},{10... | collective-permute-start | bytes 73736 | tf_op jit(solution)/shard_map/ppermute | solution.py:28
  23.4 1.1 %collective-permute-start.14 = (bf16[24,512]{1,0:T(8,128)(2,1)S(1)}, bf16[24,512]{1,0:T(8,128)(2,1)S(1)}, u32[]{:S(2)}, u32[]{:S(2)}) collective-permute-start(bf16[24,512]{1,0:T(8,128)(2,1)S(1)} %get-tuple-element.51), channel_id=1, source_target_pairs={{0,24},{8,16},{16,8},{24,0},{1,25},{9,17},{17,9},{25,1},{2,26},{10... | collective-permute-start | bytes 73736 | tf_op jit(solution)/shard_map/ppermute | solution.py:28
  24.6 0.7 %collective-permute-start.9 = (bf16[24,512]{1,0:T(8,128)(2,1)S(1)}, bf16[24,512]{1,0:T(8,128)(2,1)S(1)}, u32[]{:S(2)}, u32[]{:S(2)}) collective-permute-start(bf16[24,512]{1,0:T(8,128)(2,1)S(1)} %get-tuple-element.44), channel_id=1, source_target_pairs={{0,8},{8,0},{16,24},{24,16},{1,9},{9,1},{17,25},{25,17},{2,10},{10... | collective-permute-start | bytes 73736 | tf_op jit(solution)/shard_map/ppermute | solution.py:28
  25.3 1.4 %collective-permute-start.10 = (bf16[24,512]{1,0:T(8,128)(2,1)S(1)}, bf16[24,512]{1,0:T(8,128)(2,1)S(1)}, u32[]{:S(2)}, u32[]{:S(2)}) collective-permute-start(bf16[24,512]{1,0:T(8,128)(2,1)S(1)} %get-tuple-element.45), channel_id=1, source_target_pairs={{0,8},{8,0},{16,24},{24,16},{1,9},{9,1},{17,25},{25,17},{2,10},{10... | collective-permute-start | bytes 73736 | tf_op jit(solution)/shard_map/ppermute | solution.py:28
  26.6 0.6 %rounded.1 = bf16[2,2048]{1,0:T(2,128)(2,1)} custom-call(f32[2,2048]{1,0:T(2,128)S(1)} %get-tuple-element.42.value_ref), custom_call_target="tpu_custom_call" | custom-call | tf_op jit(solution)/shard_map/rounded/pallas_call | solution.py:370
  27.2 1.9 %collective-permute-done.14.refs_5_ = bf16[24,512]{1,0:T(8,128)(2,1)S(1)} collective-permute-done((bf16[24,512]{1,0:T(8,128)(2,1)S(1)}, bf16[24,512]{1,0:T(8,128)(2,1)S(1)}, u32[]{:S(2)}, u32[]{:S(2)}) %collective-permute-start.14) | collective-permute-done | bytes 24608 | tf_op jit(solution)/shard_map/ppermute | solution.py:28
  29.1 0.7 %early.1.refs_2_ = f32[1024,512]{1,0:T(8,128)S(1)} custom-call(bf16[1024,2048]{1,0:T(8,128)(2,1)S(1)} %get-tuple-element.29.refs_0_.unit_ref, f32[1024,128]{1,0:T(8,128)S(1)} %get-tuple-element.43.inverse_ref, bf16[24,512]{1,0:T(8,128)(2,1)S(1)} %get-tuple-element.46.refs_0_, bf16[24,512]{1,0:T(8,128)(2,1)S(1)} %collective-permute-done.11.refs_1_, ...), custom_call_target="tpu_custom_call" | custom-call | flops 100663296 | bytes 4194304 | tf_op jit(solution)/shard_map/early/pallas_call | solution.py:444
  29.9 1.7 %gradient.1 = f32[1024,512]{1,0:T(8,128)} custom-call(bf16[1024,2048]{1,0:T(8,128)(2,1)S(1)} %get-tuple-element.29.refs_0_.unit_ref, f32[1024,128]{1,0:T(8,128)S(1)} %get-tuple-element.43.inverse_ref, bf16[24,512]{1,0:T(8,128)(2,1)S(1)} %collective-permute-done.9.refs_0_, bf16[24,512]{1,0:T(8,128)(2,1)S(1)} %collective-permute-done.10.refs_1_, ...), custom_call_target="tpu_custom_call" | custom-call | flops 33554432 | bytes 4194304 | tf_op jit(solution)/shard_map/gradient/pallas_call | solution.py:444
  (16 shorter events, 0.1 us)
Async XLA Ops:
  0.6 1.5 %collective-permute-start.1 = (s32[2,4]{1,0:T(2,128)}, s32[2,4]{1,0:T(2,128)S(1)}, u32[]{:S(2)}, u32[]{:S(2)}) collective-permute-start(s32[2,4]{1,0:T(2,128)} %param.6), channel_id=1, source_target_pairs={{0,1},{1,0},{2,3},{3,2},{4,5},{5,4},{6,7},{7,6},{8,9},{9,8},{10,11... | collective-permute-start | bytes 104 | tf_op jit(solution)/shard_map/ppermute | solution.py:28
  1.1 1.4 %collective-permute-start = (bf16[2,2048]{1,0:T(2,128)(2,1)}, bf16[2,2048]{1,0:T(2,128)(2,1)S(1)}, u32[]{:S(2)}, u32[]{:S(2)}) collective-permute-start(bf16[2,2048]{1,0:T(2,128)(2,1)} %param.5), channel_id=1, source_target_pairs={{0,1},{1,0},{2,3},{3,2},{4,5},{5,4},{6,7},{7,6},{8,9},{9,8},{10,11... | collective-permute-start | bytes 24584 | tf_op jit(solution)/shard_map/ppermute | solution.py:28
  2.1 4.9 %copy-start = (bf16[1024,2048]{1,0:T(8,128)(2,1)S(1)}, bf16[1024,2048]{1,0:T(8,128)(2,1)}, u32[]{:S(2)}) copy-start(bf16[1024,2048]{1,0:T(8,128)(2,1)} %weights_ref.1) | copy-start | bytes 12582916
  2.6 8.0 %copy-start.1 = (f32[2048]{0:T(1024)S(1)}, f32[2048]{0:T(1024)}, u32[]{:S(2)}) copy-start(f32[2048]{0:T(1024)} %param.9) | copy-start | bytes 24580
  2.6 7.9 %copy-start.2 = (f32[1024]{0:T(1024)S(1)}, f32[1024]{0:T(1024)}, u32[]{:S(2)}) copy-start(f32[1024]{0:T(1024)} %param.8) | copy-start | bytes 12292
  2.6 6.8 %collective-permute-start.4 = (bf16[4,2176]{1,0:T(4,128)(2,1)S(1)}, bf16[4,2176]{1,0:T(4,128)(2,1)S(1)}, u32[]{:S(2)}, u32[]{:S(2)}) collective-permute-start(bf16[4,2176]{1,0:T(4,128)(2,1)S(1)} %pack.1.after_ref.refs_2_), channel_id=1, source_target_pairs={{0,6},{1,7},{2,4},{3,5},{4,2},{5,3},{6,0},{7,1},{8,14},{9,15},{10,... | collective-permute-start | bytes 52232 | tf_op jit(solution)/shard_map/ppermute | solution.py:28
  6.3 3.8 %collective-permute-start.3 = (bf16[4,2176]{1,0:T(4,128)(2,1)S(1)}, bf16[4,2176]{1,0:T(4,128)(2,1)S(1)}, u32[]{:S(2)}, u32[]{:S(2)}) collective-permute-start(bf16[4,2176]{1,0:T(4,128)(2,1)S(1)} %pack.1.after_ref.refs_2_), channel_id=1, source_target_pairs={{0,4},{1,5},{2,6},{3,7},{4,0},{5,1},{6,2},{7,3},{8,12},{9,13},{10,... | collective-permute-start | bytes 52232 | tf_op jit(solution)/shard_map/ppermute | solution.py:28
  6.8 3.8 %collective-permute-start.2 = (bf16[4,2176]{1,0:T(4,128)(2,1)S(1)}, bf16[4,2176]{1,0:T(4,128)(2,1)S(1)}, u32[]{:S(2)}, u32[]{:S(2)}) collective-permute-start(bf16[4,2176]{1,0:T(4,128)(2,1)S(1)} %pack.1.after_ref.refs_2_), channel_id=1, source_target_pairs={{0,2},{1,3},{2,0},{3,1},{4,6},{5,7},{6,4},{7,5},{8,10},{9,11},{10,... | collective-permute-start | bytes 52232 | tf_op jit(solution)/shard_map/ppermute | solution.py:28
  11.8 1.4 %collective-permute-start.5 = (f32[16,2048]{1,0:T(8,128)S(1)}, f32[16,2048]{1,0:T(8,128)S(1)}, u32[]{:S(2)}, u32[]{:S(2)}) collective-permute-start(f32[16,2048]{1,0:T(8,128)S(1)} %get-tuple-element.37.mine_ref), channel_id=1, source_target_pairs={{0,1},{1,0},{2,3},{3,2},{4,5},{5,4},{6,7},{7,6},{8,9},{9,8},{10,11... | collective-permute-start | bytes 393224 | tf_op jit(solution)/shard_map/ppermute | solution.py:28
  13.2 7.7 %collective-permute-start.8 = (bf16[16,2048]{1,0:T(8,128)(2,1)S(1)}, bf16[16,2048]{1,0:T(8,128)(2,1)S(1)}, u32[]{:S(2)}, u32[]{:S(2)}) collective-permute-start(bf16[16,2048]{1,0:T(8,128)(2,1)S(1)} %get-tuple-element.41), channel_id=1, source_target_pairs={{0,6},{1,7},{2,4},{3,5},{4,2},{5,3},{6,0},{7,1},{8,14},{9,15},{10,... | collective-permute-start | bytes 196616 | tf_op jit(solution)/shard_map/ppermute | solution.py:28
  15.1 5.9 %collective-permute-start.7 = (bf16[16,2048]{1,0:T(8,128)(2,1)S(1)}, bf16[16,2048]{1,0:T(8,128)(2,1)S(1)}, u32[]{:S(2)}, u32[]{:S(2)}) collective-permute-start(bf16[16,2048]{1,0:T(8,128)(2,1)S(1)} %get-tuple-element.41), channel_id=1, source_target_pairs={{0,4},{1,5},{2,6},{3,7},{4,0},{5,1},{6,2},{7,3},{8,12},{9,13},{10,... | collective-permute-start | bytes 196616 | tf_op jit(solution)/shard_map/ppermute | solution.py:28
  15.6 5.4 %collective-permute-start.6 = (bf16[16,2048]{1,0:T(8,128)(2,1)S(1)}, bf16[16,2048]{1,0:T(8,128)(2,1)S(1)}, u32[]{:S(2)}, u32[]{:S(2)}) collective-permute-start(bf16[16,2048]{1,0:T(8,128)(2,1)S(1)} %get-tuple-element.41), channel_id=1, source_target_pairs={{0,2},{1,3},{2,0},{3,1},{4,6},{5,7},{6,4},{7,5},{8,10},{9,11},{10,... | collective-permute-start | bytes 196616 | tf_op jit(solution)/shard_map/ppermute | solution.py:28
  17.0 8.3 %collective-permute-start.11 = (bf16[24,512]{1,0:T(8,128)(2,1)S(1)}, bf16[24,512]{1,0:T(8,128)(2,1)S(1)}, u32[]{:S(2)}, u32[]{:S(2)}) collective-permute-start(bf16[24,512]{1,0:T(8,128)(2,1)S(1)} %get-tuple-element.47), channel_id=1, source_target_pairs={{0,16},{8,24},{16,0},{24,8},{1,17},{9,25},{17,1},{25,9},{2,18},{10... | collective-permute-start | bytes 73736 | tf_op jit(solution)/shard_map/ppermute | solution.py:28
  19.6 7.6 %collective-permute-start.12 = (bf16[24,512]{1,0:T(8,128)(2,1)S(1)}, bf16[24,512]{1,0:T(8,128)(2,1)S(1)}, u32[]{:S(2)}, u32[]{:S(2)}) collective-permute-start(bf16[24,512]{1,0:T(8,128)(2,1)S(1)} %get-tuple-element.48), channel_id=1, source_target_pairs={{0,24},{8,16},{16,8},{24,0},{1,25},{9,17},{17,9},{25,1},{2,26},{10... | collective-permute-start | bytes 73736 | tf_op jit(solution)/shard_map/ppermute | solution.py:28
  21.7 5.6 %collective-permute-start.13 = (bf16[24,512]{1,0:T(8,128)(2,1)S(1)}, bf16[24,512]{1,0:T(8,128)(2,1)S(1)}, u32[]{:S(2)}, u32[]{:S(2)}) collective-permute-start(bf16[24,512]{1,0:T(8,128)(2,1)S(1)} %get-tuple-element.50), channel_id=1, source_target_pairs={{0,16},{8,24},{16,0},{24,8},{1,17},{9,25},{17,1},{25,9},{2,18},{10... | collective-permute-start | bytes 73736 | tf_op jit(solution)/shard_map/ppermute | solution.py:28
  23.4 5.7 %collective-permute-start.14 = (bf16[24,512]{1,0:T(8,128)(2,1)S(1)}, bf16[24,512]{1,0:T(8,128)(2,1)S(1)}, u32[]{:S(2)}, u32[]{:S(2)}) collective-permute-start(bf16[24,512]{1,0:T(8,128)(2,1)S(1)} %get-tuple-element.51), channel_id=1, source_target_pairs={{0,24},{8,16},{16,8},{24,0},{1,25},{9,17},{17,9},{25,1},{2,26},{10... | collective-permute-start | bytes 73736 | tf_op jit(solution)/shard_map/ppermute | solution.py:28
  24.6 5.2 %collective-permute-start.9 = (bf16[24,512]{1,0:T(8,128)(2,1)S(1)}, bf16[24,512]{1,0:T(8,128)(2,1)S(1)}, u32[]{:S(2)}, u32[]{:S(2)}) collective-permute-start(bf16[24,512]{1,0:T(8,128)(2,1)S(1)} %get-tuple-element.44), channel_id=1, source_target_pairs={{0,8},{8,0},{16,24},{24,16},{1,9},{9,1},{17,25},{25,17},{2,10},{10... | collective-permute-start | bytes 73736 | tf_op jit(solution)/shard_map/ppermute | solution.py:28
  25.3 4.6 %collective-permute-start.10 = (bf16[24,512]{1,0:T(8,128)(2,1)S(1)}, bf16[24,512]{1,0:T(8,128)(2,1)S(1)}, u32[]{:S(2)}, u32[]{:S(2)}) collective-permute-start(bf16[24,512]{1,0:T(8,128)(2,1)S(1)} %get-tuple-element.45), channel_id=1, source_target_pairs={{0,8},{8,0},{16,24},{24,16},{1,9},{9,1},{17,25},{25,17},{2,10},{10... | collective-permute-start | bytes 73736 | tf_op jit(solution)/shard_map/ppermute | solution.py:28
